TPU v7x, 32 devices: a whole 2x2x4 slice. The times are simulated.
32 devices in a mesh: dp: 4 (over x, core), tensor: 8 (over z, y).
Axes of the slice: x: 2, y: 2, z: 4, core: 2. Of those that a mesh axis runs over, the one named last changes fastest.
Arguments:
- tokens: bfloat16 [12288, 1024], P(('dp', 'tensor')), may hold values from -6 to 6
- seq_ids: int32 [12288], P('dp'), may hold values from 0 to 11, as said below
- blk_ids: int32 [12288], P('dp'), may hold values from 0 to 11, as said below
- norm1_gain: bfloat16 [1024], P('dp'), may hold values from 0.099609375 to 1.8984375
- w_query: bfloat16 [1024, 1024], P('dp', 'tensor'), may hold values from -0.375 to 0.375
- w_key: bfloat16 [1024, 1024], P('dp', 'tensor'), may hold values from -0.1875 to 0.1875
- w_value: bfloat16 [1024, 1024], P('dp', 'tensor'), may hold values from -0.1875 to 0.1875
- w_out: bfloat16 [1024, 1024], P('tensor', 'dp'), may hold values from -0.75 to 0.75
- norm2_gain: bfloat16 [1024], P('dp'), may hold values from 0.099609375 to 1.8984375
- w_gate: bfloat16 [1024, 4096], P('dp', 'tensor'), may hold values from -0.1875 to 0.1875
- w_up: bfloat16 [1024, 4096], P('dp', 'tensor'), may hold values from -0.1875 to 0.1875
- w_down: bfloat16 [4096, 1024], P('tensor', 'dp'), may hold values from -0.09375 to 0.09375
- cotangent: bfloat16 [12288, 1024], P(('dp', 'tensor')), may hold values from -6 to 6
Outputs:
- output: bfloat16 [12288, 1024], P(('dp', 'tensor'))
- input_grad: bfloat16 [12288, 1024], P(('dp', 'tensor'))
- grad_query: float32 [1024, 1024], P('dp', 'tensor')
- grad_key: float32 [1024, 1024], P('dp', 'tensor')
- grad_value: float32 [1024, 1024], P('dp', 'tensor')
- grad_out: float32 [1024, 1024], P('tensor', 'dp')
- grad_gate: float32 [1024, 4096], P('dp', 'tensor')
- grad_up: float32 [1024, 4096], P('dp', 'tensor')
- grad_down: float32 [4096, 1024], P('tensor', 'dp')
- grad_norm1: float32 [1024], P(('dp', 'tensor'))
- grad_norm2: float32 [1024], P(('dp', 'tensor'))
Inputs may be any that keep to these rules, and one draw needn't show every extreme that they name: `seq_ids`: sequence ids never fall along the tokens; each sequence is a whole number of aligned runs of 1024 tokens and lies within one aligned run of 3072 tokens. `blk_ids`: the block index of a token is its position within its sequence divided by 256, rounded down.
All inputs are finite; a program needn't handle non-finite values.
Results may differ from a plain program's by a relative error of at most 0.02.
Values may be sent and summed in bfloat16 or wider, within the bound.
No kernel may reach another device: no remote copies, remote signals or barrier semaphores. Data moves between devices by JAX's collectives and lax.ppermute only.
A program may use at most 128 MiB of HBM per device.

v0:
```python
import jax
import jax.numpy as jnp
from jax import lax
from jax.sharding import PartitionSpec as P

DH = 64


EPS = 1e-06
NEG = -1e30


def row_scale(values):
    return lax.rsqrt(jnp.mean(values * values, axis=-1, keepdims=True) + EPS)


def norm_back(grad_normed, values, scale, gain):
    weighted = grad_normed * gain
    inner = jnp.mean(weighted * values, axis=-1, keepdims=True)
    grad_values = scale * weighted - values * (scale * scale * scale) * inner
    grad_gain = jnp.sum(grad_normed * values * scale, axis=0)
    return (grad_values, grad_gain)


def allowed_mask(seq_ids, blk_ids, start, count):
    query_seq = lax.dynamic_slice_in_dim(seq_ids, start, count, 0)
    query_blk = lax.dynamic_slice_in_dim(blk_ids, start, count, 0)
    return (query_seq[:, None] == seq_ids[None, :]) & (blk_ids[None, :] <= query_blk[:, None])


def attention_forward(queries, keys, values, seq_ids, blk_ids, factor):
    rows, heads, width = queries.shape
    block = min(512, rows)

    def one_block(start):
        query_block = lax.dynamic_slice_in_dim(queries, start, block, 0)
        allowed = allowed_mask(seq_ids, blk_ids, start, block)
        scores = (
            jnp.einsum("qhd,khd->hqk", query_block, keys, preferred_element_type=jnp.float32)
            * factor
        )
        scores = jnp.where(allowed[None], scores, NEG)
        highest = jnp.max(scores, axis=-1, keepdims=True)
        weights = jnp.exp(scores - highest)
        totals = jnp.sum(weights, axis=-1, keepdims=True)
        probs = (weights / totals).astype(jnp.bfloat16)
        mixed = jnp.einsum("hqk,khd->qhd", probs, values, preferred_element_type=jnp.float32)
        return (mixed.astype(jnp.bfloat16), (highest + jnp.log(totals))[..., 0])

    starts = jnp.arange(rows // block, dtype=jnp.int32) * block
    mixed, logsum = lax.map(one_block, starts)
    return (mixed.reshape(rows, heads * width), logsum)


def attention_backward(queries, keys, values, grad_mixed, logsum, seq_ids, blk_ids, factor):
    rows, heads, width = queries.shape
    block = min(512, rows)
    grad_heads = grad_mixed.reshape(rows, heads, width)

    def one_block(carry, inputs):
        start, block_logsum = inputs
        grad_keys, grad_values = carry
        query_block = lax.dynamic_slice_in_dim(queries, start, block, 0)
        grad_block = lax.dynamic_slice_in_dim(grad_heads, start, block, 0)
        allowed = allowed_mask(seq_ids, blk_ids, start, block)
        scores = (
            jnp.einsum("qhd,khd->hqk", query_block, keys, preferred_element_type=jnp.float32)
            * factor
        )
        scores = jnp.where(allowed[None], scores, NEG)
        probs = jnp.exp(scores - block_logsum[..., None])
        grad_probs = jnp.einsum(
            "qhd,khd->hqk", grad_block, values, preferred_element_type=jnp.float32
        )
        inner = jnp.sum(probs * grad_probs, axis=-1, keepdims=True)
        grad_scores = (probs * (grad_probs - inner)).astype(jnp.bfloat16)
        grad_query = (
            jnp.einsum("hqk,khd->qhd", grad_scores, keys, preferred_element_type=jnp.float32)
            * factor
        )
        grad_keys = (
            grad_keys
            + jnp.einsum(
                "hqk,qhd->khd", grad_scores, query_block, preferred_element_type=jnp.float32
            )
            * factor
        )
        grad_values = grad_values + jnp.einsum(
            "hqk,qhd->khd",
            probs.astype(jnp.bfloat16),
            grad_block,
            preferred_element_type=jnp.float32,
        )
        return ((grad_keys, grad_values), grad_query.astype(jnp.bfloat16))

    starts = jnp.arange(rows // block, dtype=jnp.int32) * block
    zeros = jnp.zeros((rows, heads, width), jnp.float32)
    (grad_keys, grad_values), grad_queries = lax.scan(one_block, (zeros, zeros), (starts, logsum))
    return (
        grad_queries.reshape(rows, heads * width),
        grad_keys.astype(jnp.bfloat16).reshape(rows, heads * width),
        grad_values.astype(jnp.bfloat16).reshape(rows, heads * width),
    )


def on_device(
    tokens,
    seq_ids,
    blk_ids,
    norm1_gain,
    w_query,
    w_key,
    w_value,
    w_out,
    norm2_gain,
    w_gate,
    w_up,
    w_down,
    cotangent,
):
    factor = DH ** (-0.5)
    gathered = (
        lax.all_gather(norm1_gain, "dp", axis=0, tiled=True),
        lax.all_gather(norm2_gain, "dp", axis=0, tiled=True),
        lax.all_gather(w_query, "dp", axis=0, tiled=True),
        lax.all_gather(w_key, "dp", axis=0, tiled=True),
        lax.all_gather(w_value, "dp", axis=0, tiled=True),
        lax.all_gather(w_out, "dp", axis=1, tiled=True),
        lax.all_gather(w_gate, "dp", axis=0, tiled=True),
        lax.all_gather(w_up, "dp", axis=0, tiled=True),
        lax.all_gather(w_down, "dp", axis=1, tiled=True),
    )
    (
        gain_first,
        gain_second,
        query_full,
        key_full,
        value_full,
        out_full,
        gate_full,
        up_full,
        down_full,
    ) = gathered
    resid = tokens.astype(jnp.float32)
    first_gain = gain_first.astype(jnp.float32)
    first_scale = row_scale(resid)
    normed_first = (resid * first_scale * first_gain).astype(jnp.bfloat16)
    group_first = lax.all_gather(normed_first, "tensor", axis=0, tiled=True)
    rows = group_first.shape[0]
    heads = query_full.shape[1] // DH
    queries = (
        jnp.dot(group_first, query_full, preferred_element_type=jnp.float32)
        .astype(jnp.bfloat16)
        .reshape(rows, heads, DH)
    )
    keys = (
        jnp.dot(group_first, key_full, preferred_element_type=jnp.float32)
        .astype(jnp.bfloat16)
        .reshape(rows, heads, DH)
    )
    values = (
        jnp.dot(group_first, value_full, preferred_element_type=jnp.float32)
        .astype(jnp.bfloat16)
        .reshape(rows, heads, DH)
    )
    attended, logsum = attention_forward(queries, keys, values, seq_ids, blk_ids, factor)
    piece = attended
    attn_total = lax.psum_scatter(
        jnp.dot(piece, out_full, preferred_element_type=jnp.float32),
        "tensor",
        scatter_dimension=0,
        tiled=True,
    )
    mixed = resid + attn_total
    second_gain = gain_second.astype(jnp.float32)
    second_scale = row_scale(mixed)
    normed_second = (mixed * second_scale * second_gain).astype(jnp.bfloat16)
    group_second = lax.all_gather(normed_second, "tensor", axis=0, tiled=True)
    gate = jnp.dot(group_second, gate_full, preferred_element_type=jnp.float32)
    upward = jnp.dot(group_second, up_full, preferred_element_type=jnp.float32)
    sigmoid_gate = jax.nn.sigmoid(gate)
    silu_gate = gate * sigmoid_gate
    hidden = (silu_gate * upward).astype(jnp.bfloat16)
    piece = hidden
    ffn_total = lax.psum_scatter(
        jnp.dot(piece, down_full, preferred_element_type=jnp.float32).astype(jnp.bfloat16),
        "tensor",
        scatter_dimension=0,
        tiled=True,
    ).astype(jnp.float32)
    output = (mixed + ffn_total).astype(jnp.bfloat16)
    back_params = (
        lax.all_gather(norm1_gain, "dp", axis=0, tiled=True),
        lax.all_gather(norm2_gain, "dp", axis=0, tiled=True),
        lax.all_gather(w_query, "dp", axis=0, tiled=True),
        lax.all_gather(w_key, "dp", axis=0, tiled=True),
        lax.all_gather(w_value, "dp", axis=0, tiled=True),
        lax.all_gather(w_out, "dp", axis=1, tiled=True),
        lax.all_gather(w_gate, "dp", axis=0, tiled=True),
        lax.all_gather(w_up, "dp", axis=0, tiled=True),
        lax.all_gather(w_down, "dp", axis=1, tiled=True),
    )
    (
        back_gain_first,
        back_gain_second,
        back_query,
        back_key,
        back_value,
        back_out,
        back_gate,
        back_up,
        back_down,
    ) = back_params
    first_gain_back = back_gain_first.astype(jnp.float32)
    second_gain_back = back_gain_second.astype(jnp.float32)
    grad_rows = lax.all_gather(cotangent, "tensor", axis=0, tiled=True)
    grad_hidden = jnp.einsum("tm,fm->tf", grad_rows, back_down, preferred_element_type=jnp.float32)
    grad_down_w = jnp.einsum("tf,tm->fm", hidden, grad_rows, preferred_element_type=jnp.float32)
    slope = sigmoid_gate * (1.0 + gate * (1.0 - sigmoid_gate))
    grad_gate = (grad_hidden * upward * slope).astype(jnp.bfloat16)
    grad_upward = (grad_hidden * silu_gate).astype(jnp.bfloat16)
    grad_gate_w = jnp.einsum(
        "tm,tf->mf", group_second, grad_gate, preferred_element_type=jnp.float32
    )
    grad_up_w = jnp.einsum(
        "tm,tf->mf", group_second, grad_upward, preferred_element_type=jnp.float32
    )
    first_part = jnp.einsum("tf,mf->tm", grad_gate, back_gate, preferred_element_type=jnp.float32)
    grad_normed_second = lax.psum_scatter(
        (
            first_part
            + jnp.einsum("tf,mf->tm", grad_upward, back_up, preferred_element_type=jnp.float32)
        ).astype(jnp.bfloat16),
        "tensor",
        scatter_dimension=0,
        tiled=True,
    ).astype(jnp.float32)
    grad_mixed_norm, grad_gain_second = norm_back(
        grad_normed_second, mixed, second_scale, second_gain_back
    )
    grad_mixed = cotangent.astype(jnp.float32) + grad_mixed_norm
    attn_grad_group = lax.all_gather(grad_mixed.astype(jnp.bfloat16), "tensor", axis=0, tiled=True)
    grad_attended = jnp.einsum(
        "tm,hm->th", attn_grad_group, back_out, preferred_element_type=jnp.float32
    ).astype(jnp.bfloat16)
    grad_out_w = jnp.einsum(
        "th,tm->hm", attended, attn_grad_group, preferred_element_type=jnp.float32
    )
    grad_queries, grad_keys, grad_values = attention_backward(
        queries, keys, values, grad_attended, logsum, seq_ids, blk_ids, factor
    )
    grad_query_w = jnp.einsum(
        "tm,th->mh", group_first, grad_queries, preferred_element_type=jnp.float32
    )
    grad_key_w = jnp.einsum("tm,th->mh", group_first, grad_keys, preferred_element_type=jnp.float32)
    grad_value_w = jnp.einsum(
        "tm,th->mh", group_first, grad_values, preferred_element_type=jnp.float32
    )
    summed = (
        lax.psum_scatter(
            grad_query_w.astype(jnp.bfloat16), "dp", scatter_dimension=0, tiled=True
        ).astype(jnp.float32),
        lax.psum_scatter(
            grad_key_w.astype(jnp.bfloat16), "dp", scatter_dimension=0, tiled=True
        ).astype(jnp.float32),
        lax.psum_scatter(
            grad_value_w.astype(jnp.bfloat16), "dp", scatter_dimension=0, tiled=True
        ).astype(jnp.float32),
        lax.psum_scatter(
            grad_out_w.astype(jnp.bfloat16), "dp", scatter_dimension=1, tiled=True
        ).astype(jnp.float32),
        lax.psum_scatter(
            grad_gate_w.astype(jnp.bfloat16), "dp", scatter_dimension=0, tiled=True
        ).astype(jnp.float32),
        lax.psum_scatter(
            grad_up_w.astype(jnp.bfloat16), "dp", scatter_dimension=0, tiled=True
        ).astype(jnp.float32),
        lax.psum_scatter(
            grad_down_w.astype(jnp.bfloat16), "dp", scatter_dimension=1, tiled=True
        ).astype(jnp.float32),
    )
    grad_query_w, grad_key_w, grad_value_w, grad_out_w, grad_gate_w, grad_up_w, grad_down_w = summed
    total = jnp.einsum("th,mh->tm", grad_queries, back_query, preferred_element_type=jnp.float32)
    total = total + jnp.einsum("th,mh->tm", grad_keys, back_key, preferred_element_type=jnp.float32)
    grad_normed_first = lax.psum_scatter(
        (
            total
            + jnp.einsum("th,mh->tm", grad_values, back_value, preferred_element_type=jnp.float32)
        ).astype(jnp.bfloat16),
        "tensor",
        scatter_dimension=0,
        tiled=True,
    ).astype(jnp.float32)
    grad_tokens_norm, grad_gain_first = norm_back(
        grad_normed_first, resid, first_scale, first_gain_back
    )
    input_grad = (grad_mixed + grad_tokens_norm).astype(jnp.bfloat16)
    grad_norm_first, grad_norm_second = (
        lax.psum_scatter(grad_gain_first, ("dp", "tensor"), scatter_dimension=0, tiled=True),
        lax.psum_scatter(grad_gain_second, ("dp", "tensor"), scatter_dimension=0, tiled=True),
    )
    return (
        output,
        input_grad,
        grad_query_w,
        grad_key_w,
        grad_value_w,
        grad_out_w,
        grad_gate_w,
        grad_up_w,
        grad_down_w,
        grad_norm_first,
        grad_norm_second,
    )


def solution(mesh):
    return jax.shard_map(
        on_device,
        mesh=mesh,
        in_specs=(
            P(("dp", "tensor"), None),
            P("dp"),
            P("dp"),
            P("dp"),
            P("dp", "tensor"),
            P("dp", "tensor"),
            P("dp", "tensor"),
            P("tensor", "dp"),
            P("dp"),
            P("dp", "tensor"),
            P("dp", "tensor"),
            P("tensor", "dp"),
            P(("dp", "tensor"), None),
        ),
        out_specs=(
            P(("dp", "tensor"), None),
            P(("dp", "tensor"), None),
            P("dp", "tensor"),
            P("dp", "tensor"),
            P("dp", "tensor"),
            P("tensor", "dp"),
            P("dp", "tensor"),
            P("dp", "tensor"),
            P("tensor", "dp"),
            P(("dp", "tensor")),
            P(("dp", "tensor")),
        ),
        check_vma=False,
    )
```

profile of v0, /device:TPU:0, one launch (start us, length us, event | category | flops | bytes accessed | tf_op | source)
XLA Modules:
  0.0 1455.7 jit_solution(128816638901233754)
XLA Ops:
  10.7 6.0 all-gather
  19.0 6.5 all_gather.50
  25.5 6.1 all_gather.51
  31.6 6.1 all_gather.52
  37.7 6.1 all_gather.53
  43.7 76.2 %all-gather.10.cloned.1.call-done = bf16[3072,1024]{1,0:T(8,128)(2,1)} async-done(((bf16[384,1024]{1,0:T(8,128)(2,1)}), bf16[3072,1024]{1,0:T(8,128)(2,1)}) %all-gather.10.cloned.1.call-update) | async-done | bytes 6291472 | tf_op jit(solution)/shard_map/all_gather | solution.py:148
  119.9 5.1 convolution_convert_fusion.2
  129.7 88.6 %while.27 = (s32[]{:T(128)}, bf16[6,512,2,64]{1,3,2,0:T(8,128)(2,1)S(1)}, f32[6,2,512]{2,1,0:T(2,128)S(1)}, s32[6]{0:T(128)S(1)}, s32[3072]{0:T(1024)S(1)}, /*in...) while((s32[]{:T(128)}, ...), condition=%wide.region_4.5_spmd, body=%wide.region_1.4_spmd.sunk | while | flops 847838208 | bytes 45945020 | solution.py:51
  219.1 6.4 fusion.58
  231.2 200.0 %reduce-scatter.12.cloned.1.call-done = f32[384,1024]{1,0:T(8,128)} async-done(((f32[3072,1024]{1,0:T(8,128)}), f32[384,1024]{1,0:T(8,128)}) %reduce-scatter.12.cloned.1.call-update) | async-done | bytes 1572880 | tf_op jit(solution)/shard_map/reduce_scatter | solution.py:168
  436.8 95.5 %all-gather.12.cloned.1.call-done = bf16[3072,1024]{1,0:T(8,128)(2,1)} async-done(((bf16[384,1024]{1,0:T(8,128)(2,1)}), bf16[3072,1024]{1,0:T(8,128)(2,1)}) %all-gather.12.cloned.1.call-update) | async-done | bytes 6291472 | tf_op jit(solution)/shard_map/all_gather | solution.py:178
  532.3 9.1 fusion.60
  541.5 7.1 all-gather.14.cloned.1.call-done
  548.5 9.1 fusion.59
  557.6 9.2 all-gather.18.cloned.1.call-done
  566.8 101.0 %all-gather.20.cloned.1.call-done = bf16[3072,1024]{1,0:T(8,128)(2,1)} async-done(((bf16[384,1024]{1,0:T(8,128)(2,1)}), bf16[3072,1024]{1,0:T(8,128)(2,1)}) %all-gather.20.cloned.1.call-update) | async-done | bytes 6291472 | tf_op jit(solution)/shard_map/all_gather | solution.py:216
  667.8 14.8 %multiply_convert_fusion.1 = (bf16[3072,512]{1,0:T(8,128)(2,1)}, bf16[3072,512]{1,0:T(8,128)(2,1)}, bf16[3072,512]{1,0:T(8,128)(2,1)}) fusion(f32[3072,512]{1,0:T(8,128)} %fusion.59, f32[3072,512]{1,0:T(8,128)} %fusion.60, bf16[3072,1024]{1,0:T(8,128)(2,1)} %all-gather.20.cloned.1.call-done, bf16[512,1024]{1,0:T(8,128)(2,1)} %all-gather.18.cloned.1.call-done), kind=kOutput, calls=%fused_computation.47 | convolution fusion | flops 3244818432 | bytes 29360128 | tf_op jit(solution)/shard_map/tm,fm->tf/dot_general | solution.py:217
  682.7 5.7 fusion.61
  688.4 7.7 add_convert_fusion.1
  696.1 115.9 %reduce-scatter.16.cloned.1.call-done = bf16[384,1024]{1,0:T(8,128)(2,1)} async-done(((bf16[3072,1024]{1,0:T(8,128)(2,1)}), bf16[384,1024]{1,0:T(8,128)(2,1)}) %reduce-scatter.16.cloned.1.call-update) | async-done | bytes 786448 | tf_op jit(solution)/shard_map/reduce_scatter | solution.py:229
  817.6 8.1 convolution_convert_fusion.5
  826.0 8.2 convolution_convert_fusion.6
  834.3 8.2 convolution_convert_fusion.7
  842.6 73.4 %all-gather.22.cloned.1.call-done = bf16[3072,1024]{1,0:T(8,128)(2,1)} async-done(((bf16[384,1024]{1,0:T(8,128)(2,1)}), bf16[3072,1024]{1,0:T(8,128)(2,1)}) %all-gather.22.cloned.1.call-update) | async-done | bytes 6291472 | tf_op jit(solution)/shard_map/all_gather | solution.py:242
  920.8 5.9 convolution_convert_fusion.1
  927.7 201.2 %while.28 = (s32[]{:T(128)}, f32[3072,2,64]{0,2,1:T(8,128)S(1)}, f32[3072,2,64]{0,2,1:T(8,128)}, bf16[6,512,2,64]{1,3,2,0:T(8,128)(2,1)}, s32[6]{0:T(128)S(1)}, ...) while((s32[]{:T(128)}, f32[3072,2,64]{0,2,1:T(8,128)S(1)}, ...), condition=%wide.region_12.13_spmd.clone, body=%wide.region_10.12_spmd.clone.sunk | while | flops 2067266560 | bytes 122618160 | solution.py:98
  939.9 8.9 multiply_reduce_fusion.3
  948.8 7.5 multiply_convert_fusion.6
  973.3 8.9 multiply_reduce_fusion.3
  982.3 7.5 multiply_convert_fusion.6
  1006.8 8.9 multiply_reduce_fusion.3
  1015.7 7.5 multiply_convert_fusion.6
  1040.3 8.9 multiply_reduce_fusion.3
  1049.2 7.5 multiply_convert_fusion.6
  1073.8 8.9 multiply_reduce_fusion.3
  1082.7 7.5 multiply_convert_fusion.6
  1107.2 8.9 multiply_reduce_fusion.3
  1116.1 7.5 multiply_convert_fusion.6
  1131.8 5.5 convolution_convert_fusion.11
  1137.3 7.6 fusion.63
  1147.7 6.4 fusion.62
  1154.2 5.3 convolution_convert_fusion.9
  1159.6 12.2 add_convert_fusion
  1173.0 7.6 convolution_convert_fusion
  1190.8 10.3 reduce-scatter.24.cloned.1.call-done
  1202.6 120.1 %reduce-scatter.18.cloned.1.call-done = bf16[384,1024]{1,0:T(8,128)(2,1)} async-done(((bf16[3072,1024]{1,0:T(8,128)(2,1)}), bf16[384,1024]{1,0:T(8,128)(2,1)}) %reduce-scatter.18.cloned.1.call-update) | async-done | bytes 786448 | tf_op jit(solution)/shard_map/reduce_scatter | solution.py:285
  1324.4 42.2 %all-reduce.2 = (f32[1024]{0:T(1024)S(1)}, f32[1024]{0:T(1024)S(1)}) all-reduce(f32[1024]{0:T(1024)S(1)} %get-tuple-element.169, f32[1024]{0:T(1024)S(1)} %copy-done.31), channel_id=13, replica_groups=mesh['dp'=4,'tensor'=8] {'dp','tensor'}, use_global_device_ids=true, to_apply=%region_23.24.clone | all-reduce | flops 2048 | bytes 16384
  1367.8 76.8 %reduce-scatter.14.cloned.1.call-done = bf16[384,1024]{1,0:T(8,128)(2,1)} async-done(((bf16[3072,1024]{1,0:T(8,128)(2,1)}), bf16[384,1024]{1,0:T(8,128)(2,1)}) %reduce-scatter.14.cloned.1.call-update) | async-done | bytes 786448 | tf_op jit(solution)/shard_map/reduce_scatter | solution.py:185
  (286 shorter events, 224.7 us)
Async XLA Ops:
  8.0 111.9 %all-gather.10.cloned.1.call-start = ((), (), s32[]{:S(2)}) async-start(), calls=%async_computation.11 | async-start | bytes 7077888 | tf_op jit(solution)/shard_map/all_gather | solution.py:148
  10.7 14.8 %copy-start.25 = (f32[384]{0:T(512)}, f32[384]{0:T(512)S(1)}, u32[]{:S(2)}) copy-start(f32[384]{0:T(512)S(1)} %get-tuple-element.227) | copy-start | bytes 4612
  16.7 8.8 copy-start.21
  19.0 412.2 %reduce-scatter.12.cloned.1.call-start = ((), (), s32[]{:S(2)}) async-start(), calls=%async_computation.12 | async-start | bytes 14155776 | tf_op jit(solution)/shard_map/reduce_scatter | solution.py:168
  25.5 101.8 %copy-start.10 = (bf16[1024,128]{1,0:T(8,128)(2,1)}, bf16[1024,128]{1,0:T(8,128)(2,1)S(1)}, u32[]{:S(2)}) copy-start(bf16[1024,128]{1,0:T(8,128)(2,1)S(1)} %all_gather.50) | copy-start | bytes 786436
  31.6 93.5 %copy-start.12 = (bf16[1024,128]{1,0:T(8,128)(2,1)}, bf16[1024,128]{1,0:T(8,128)(2,1)S(1)}, u32[]{:S(2)}) copy-start(bf16[1024,128]{1,0:T(8,128)(2,1)S(1)} %all_gather.51) | copy-start | bytes 786436
  37.7 82.3 %copy-start.8 = (bf16[1024,128]{1,0:T(8,128)(2,1)}, bf16[1024,128]{1,0:T(8,128)(2,1)S(1)}, u32[]{:S(2)}) copy-start(bf16[1024,128]{1,0:T(8,128)(2,1)S(1)} %all_gather.52) | copy-start | bytes 786436
  225.4 211.4 %all-gather.16.cloned.1.call-start = ((), (), s32[]{:S(2)}) async-start(), calls=%async_computation.15 | async-start | bytes 1310720 | tf_op jit(solution)/shard_map/all_gather | solution.py:130
  226.0 306.3 %all-gather.12.cloned.1.call-start = ((), (), s32[]{:S(2)}) async-start(), calls=%async_computation.13 | async-start | bytes 7077888 | tf_op jit(solution)/shard_map/all_gather | solution.py:178
  231.2 583.1 %copy-start.19 = (f32[4,1,256]{2,1,0:T(1,128)}, f32[4,1,256]{2,1,0:T(1,128)S(1)}, u32[]{:S(2)}) copy-start(f32[4,1,256]{2,1,0:T(1,128)S(1)} %convert_element_type.176) | copy-start | bytes 12292
  433.1 381.2 %copy-start.1 = (f32[384,1024]{1,0:T(8,128)}, f32[384,1024]{1,0:T(8,128)S(1)}, u32[]{:S(2)}) copy-start(f32[384,1024]{1,0:T(8,128)S(1)} %get-tuple-element.216) | copy-start | bytes 4718596
  433.1 381.2 %copy-start.23 = (f32[384]{0:T(512)}, f32[384]{0:T(512)S(1)}, u32[]{:S(2)}) copy-start(f32[384]{0:T(512)S(1)} %get-tuple-element.229) | copy-start | bytes 4612
  433.1 381.2 %copy-start.27 = (f32[384]{0:T(512)}, f32[384]{0:T(512)S(1)}, u32[]{:S(2)}) copy-start(f32[384]{0:T(512)S(1)} %get-tuple-element.228) | copy-start | bytes 4612
  434.4 114.1 %all-gather.14.cloned.1.call-start = ((), (), s32[]{:S(2)}) async-start(), calls=%async_computation.14 | async-start | bytes 1310720 | tf_op jit(solution)/shard_map/all_gather | solution.py:129
  435.0 131.9 %all-gather.18.cloned.1.call-start = ((), (), s32[]{:S(2)}) async-start(), calls=%async_computation.16 | async-start | bytes 1310720 | tf_op jit(solution)/shard_map/all_gather | solution.py:131
  435.7 232.1 %all-gather.20.cloned.1.call-start = ((), (), s32[]{:S(2)}) async-start(), calls=%async_computation.18 | async-start | bytes 7077888 | tf_op jit(solution)/shard_map/all_gather | solution.py:216
  436.5 375.5 %reduce-scatter.16.cloned.1.call-start = ((), (), s32[]{:S(2)}) async-start(), calls=%async_computation.19 | async-start | bytes 7077888 | tf_op jit(solution)/shard_map/reduce_scatter | solution.py:229
  667.8 14.8 %copy-start.35 = (bf16[1024,512]{1,0:T(8,128)(2,1)S(1)}, bf16[1024,512]{1,0:T(8,128)(2,1)}, u32[]{:S(2)}) copy-start(bf16[1024,512]{1,0:T(8,128)(2,1)} %all-gather.14.cloned.1.call-done) | copy-start | bytes 3145732
  696.1 219.9 %all-gather.22.cloned.1.call-start = ((), (), s32[]{:S(2)}) async-start(), calls=%async_computation.20 | async-start | bytes 7077888 | tf_op jit(solution)/shard_map/all_gather | solution.py:242
  817.6 363.2 %reduce-scatter.32.cloned.1.call-start = ((), (), s32[]{:S(2)}) async-start(), calls=%async_computation.28 | async-start | bytes 1310720 | tf_op jit(solution)/shard_map/reduce_scatter | solution.py:278
  825.8 356.9 %reduce-scatter.30.cloned.1.call-start = ((), (), s32[]{:S(2)}) async-start(), calls=%async_computation.27 | async-start | bytes 1310720 | tf_op jit(solution)/shard_map/reduce_scatter | solution.py:275
  834.3 350.2 %reduce-scatter.28.cloned.1.call-start = ((), (), s32[]{:S(2)}) async-start(), calls=%async_computation.26 | async-start | bytes 1310720 | tf_op jit(solution)/shard_map/reduce_scatter | solution.py:272
  842.5 343.8 %reduce-scatter.26.cloned.1.call-start = ((), (), s32[]{:S(2)}) async-start(), calls=%async_computation.25 | async-start | bytes 327680 | tf_op jit(solution)/shard_map/reduce_scatter | solution.py:269
  920.8 267.1 %reduce-scatter.20.cloned.1.call-start = ((), (), s32[]{:S(2)}) async-start(), calls=%async_computation.22 | async-start | bytes 327680 | tf_op jit(solution)/shard_map/reduce_scatter | solution.py:260
  939.8 8.9 copy-start.17
  973.3 8.9 copy-start.17
  1006.8 8.9 copy-start.17
  1040.3 8.9 copy-start.17
  1073.8 8.9 copy-start.17
  1107.2 8.9 copy-start.17
  1131.8 13.2 slice-start
  1137.3 52.0 %reduce-scatter.22.cloned.1.call-start = ((), (), s32[]{:S(2)}) async-start(), calls=%async_computation.23 | async-start | bytes 327680 | tf_op jit(solution)/shard_map/reduce_scatter | solution.py:263
  1137.3 7.7 slice-start.1
  1137.3 7.7 copy-start.7
  1147.6 53.5 %reduce-scatter.24.cloned.1.call-start = ((), (), s32[]{:S(2)}) async-start(), calls=%async_computation.24 | async-start | bytes 327680 | tf_op jit(solution)/shard_map/reduce_scatter | solution.py:266
  1159.5 163.2 %reduce-scatter.18.cloned.1.call-start = ((), (), s32[]{:S(2)}) async-start(), calls=%async_computation.21 | async-start | bytes 7077888 | tf_op jit(solution)/shard_map/reduce_scatter | solution.py:285
  1171.8 272.8 %reduce-scatter.14.cloned.1.call-start = ((), (), s32[]{:S(2)}) async-start(), calls=%async_computation.17 | async-start | bytes 7077888 | tf_op jit(solution)/shard_map/reduce_scatter | solution.py:185
  1180.6 142.1 %copy-start.3 = (bf16[384,1024]{1,0:T(8,128)(2,1)S(1)}, bf16[384,1024]{1,0:T(8,128)(2,1)}, u32[]{:S(2)}) copy-start(bf16[384,1024]{1,0:T(8,128)(2,1)} %param.17) | copy-start | bytes 2359300
  1180.6 142.1 %copy-start.22 = (f32[4,1,256]{2,1,0:T(1,128)S(1)}, f32[4,1,256]{2,1,0:T(1,128)}, u32[]{:S(2)}) copy-start(f32[4,1,256]{2,1,0:T(1,128)} %copy-done.21) | copy-start | bytes 12292
  1180.6 142.1 %copy-start.26 = (f32[384]{0:T(512)S(1)}, f32[384]{0:T(512)}, u32[]{:S(2)}) copy-start(f32[384]{0:T(512)} %copy-done.25) | copy-start | bytes 4612
  1180.6 143.8 %copy-start.31 = (f32[1024]{0:T(1024)S(1)}, f32[1024]{0:T(1024)}, u32[]{:S(2)}) copy-start(f32[1024]{0:T(1024)} %get-tuple-element.167) | copy-start | bytes 12292
  1180.6 264.0 %copy-start.2 = (f32[384,1024]{1,0:T(8,128)S(1)}, f32[384,1024]{1,0:T(8,128)}, u32[]{:S(2)}) copy-start(f32[384,1024]{1,0:T(8,128)} %copy-done.1) | copy-start | bytes 4718596
  1180.6 264.0 %copy-start.6 = (bf16[384,1024]{1,0:T(8,128)(2,1)S(1)}, bf16[384,1024]{1,0:T(8,128)(2,1)}, u32[]{:S(2)}) copy-start(bf16[384,1024]{1,0:T(8,128)(2,1)} %param.29) | copy-start | bytes 2359300
  1180.6 264.0 %copy-start.20 = (f32[4,1,256]{2,1,0:T(1,128)S(1)}, f32[4,1,256]{2,1,0:T(1,128)}, u32[]{:S(2)}) copy-start(f32[4,1,256]{2,1,0:T(1,128)} %copy-done.19) | copy-start | bytes 12292
  1180.7 264.0 %copy-start.24 = (f32[384]{0:T(512)S(1)}, f32[384]{0:T(512)}, u32[]{:S(2)}) copy-start(f32[384]{0:T(512)} %copy-done.23) | copy-start | bytes 4612
  1180.7 264.0 %copy-start.28 = (f32[384]{0:T(512)S(1)}, f32[384]{0:T(512)}, u32[]{:S(2)}) copy-start(f32[384]{0:T(512)} %copy-done.27) | copy-start | bytes 4612
  1180.7 264.0 %copy-start.30 = (f32[384]{0:T(512)S(1)}, f32[384]{0:T(512)}, u32[]{:S(2)}) copy-start(f32[384]{0:T(512)} %copy-done.29) | copy-start | bytes 4612
  1180.7 264.0 %copy-start.32 = (f32[384]{0:T(512)S(1)}, f32[384]{0:T(512)}, u32[]{:S(2)}) copy-start(f32[384]{0:T(512)} %get-tuple-element.226) | copy-start | bytes 4612
  (19 other events, 70.8 us)
Sparse Core Ops, SparseCore 0:
  19.1 100.8 all-gather.9
  225.6 205.5 reduce-scatter.11
  817.7 98.2 all-gather.21
Sparse Core Ops, SparseCore 1:
  227.5 14.8 all-gather.15
  434.5 97.8 all-gather.11
  533.8 14.7 all-gather.13
  550.1 16.7 all-gather.17
  569.1 98.7 all-gather.19
  696.2 115.8 reduce-scatter.15
  825.9 24.1 reduce-scatter.31
  852.5 24.8 reduce-scatter.29
  879.8 24.9 reduce-scatter.27
  920.8 18.2 reduce-scatter.25
  1137.3 18.1 reduce-scatter.19
  1158.7 20.0 reduce-scatter.21
  1181.1 20.0 reduce-scatter.23
  1205.1 117.5 reduce-scatter.17
  1326.7 117.8 reduce-scatter.13
where the time goes:
time: 1460 us
  waiting for transfers between devices  888 us (61%)
  matrix products  316 us (22%)
  other arithmetic  115 us (8%)
  blocking collectives  77.9 us (5%)
  loops' own time  24.7 us (2%)
  between operations  16.6 us (1%)
  local copies, waits for them, and re-layouts  16.3 us (1%)
    reduce_scatter x1, waiting for transfers between devices, on_device(): lax.psum_scatter(jnp.dot(piece, out_full, preferred_element_type=jnp.floa...  200 us
    reduce_scatter x1, waiting for transfers between devices, on_device(): lax.psum_scatter((total + jnp.einsum('th,mh->tm', grad_values, back_value...  120 us
    reduce_scatter x1, waiting for transfers between devices, on_device(): lax.psum_scatter((first_part + jnp.einsum('tf,mf->tm', grad_upward, back_...  116 us
    all_gather x1, waiting for transfers between devices, on_device(): grad_rows = lax.all_gather(cotangent, 'tensor', axis=0, tiled=True)  101 us
    all_gather x1, waiting for transfers between devices, on_device(): group_second = lax.all_gather(normed_second, 'tensor', axis=0, tiled=True)  95.5 us
    reduce_scatter x1, waiting for transfers between devices, on_device(): lax.psum_scatter(jnp.dot(piece, down_full, preferred_element_type=jnp.flo...  76.8 us
    all_gather x1, waiting for transfers between devices, on_device(): group_first = lax.all_gather(normed_first, 'tensor', axis=0, tiled=True)  76.2 us
    all_gather x1, waiting for transfers between devices, on_device(): lax.all_gather(grad_mixed.astype(jnp.bfloat16), 'tensor', axis=0, tiled=T...  73.4 us
  transfers between devices with their start and end apart: 18, of which 11 were waited for; matrix products, arithmetic and copies ran while one was open for 21% of the time, Pallas kernels for 0%

commit v1 on v0

v1 whole, which is shorter than its diff:
```python
import functools

import jax
import jax.numpy as jnp
from jax import lax
from jax.experimental import pallas as pl
from jax.experimental.pallas import tpu as pltpu
from jax.sharding import PartitionSpec as P

DH = 64
BLK = 256
EPS = 1e-06
HT = 256
NT = (((1,), (1,)), ((), ()))
NN = (((1,), (0,)), ((), ()))
TN = (((0,), (0,)), ((), ()))


def dot(a, b, dims):
    return lax.dot_general(a, b, dims, preferred_element_type=jnp.float32)


def split_heads(block):
    low = lax.broadcasted_iota(jnp.int32, block.shape, 1) < DH
    zero = jnp.zeros_like(block)
    return jnp.concatenate([jnp.where(low, block, zero), jnp.where(low, zero, block)], axis=0)


def scaled_q(qkv_ref, rows):
    return split_heads((qkv_ref[rows, 0:128].astype(jnp.float32) * DH ** -0.5).astype(jnp.bfloat16))


def attn_fwd_kernel(first_ref, qkv_ref, out_ref, log_ref, vt_ref, top_ref, sum_ref, acc_ref):
    i = pl.program_id(0)
    @pl.when(i == 0)
    def _():
        vt_ref[...] = jnp.transpose(qkv_ref[:, 256:384])
    rows = pl.ds(pl.multiple_of(i * BLK, BLK), BLK)
    both = scaled_q(qkv_ref, rows)
    top_ref[...] = jnp.full_like(top_ref, -1e30)
    sum_ref[...] = jnp.zeros_like(sum_ref)
    acc_ref[...] = jnp.zeros_like(acc_ref)

    def step(j, _):
        at = pl.ds(pl.multiple_of(j * BLK, BLK), BLK)
        scores = dot(qkv_ref[at, 128:256], both, NT)
        old = top_ref[...]
        new = jnp.maximum(old, jnp.max(scores, axis=0, keepdims=True))
        top_ref[...] = new
        weights = jnp.exp(scores - new)
        shrink = jnp.exp(old - new)
        sum_ref[...] = sum_ref[...] * shrink + jnp.sum(weights, axis=0, keepdims=True)
        probs = weights.astype(jnp.bfloat16)
        acc_ref[:, 0:BLK] = acc_ref[:, 0:BLK] * shrink[:, 0:BLK] + dot(vt_ref[0:DH, at], probs[:, 0:BLK], NN)
        acc_ref[:, BLK:] = acc_ref[:, BLK:] * shrink[:, BLK:] + dot(vt_ref[DH:, at], probs[:, BLK:], NN)
        return 0

    lax.fori_loop(first_ref[i], i + 1, step, 0)
    mixed = acc_ref[...] / sum_ref[...]
    out_ref[...] = jnp.transpose(jnp.concatenate([mixed[:, 0:BLK], mixed[:, BLK:]], axis=0)).astype(jnp.bfloat16)
    log_ref[0] = top_ref[...] + jnp.log(sum_ref[...])


def attn_fwd(qkv, first):
    rows = qkv.shape[0]
    n = rows // BLK
    return pl.pallas_call(
        attn_fwd_kernel, name="attn_fwd",
        out_shape=(jax.ShapeDtypeStruct((rows,128),jnp.bfloat16), jax.ShapeDtypeStruct((n,1,2*BLK),jnp.float32)),
        grid_spec=pltpu.PrefetchScalarGridSpec(
            num_scalar_prefetch=1, grid=(n,),
            in_specs=[pl.BlockSpec((rows,384), lambda i,s:(0,0))],
            out_specs=[pl.BlockSpec((BLK,128), lambda i,s:(i,0)), pl.BlockSpec((1,1,2*BLK), lambda i,s:(i,0,0))],
            scratch_shapes=[pltpu.VMEM((128,rows),jnp.bfloat16), pltpu.VMEM((1,2*BLK),jnp.float32), pltpu.VMEM((1,2*BLK),jnp.float32), pltpu.VMEM((DH,2*BLK),jnp.float32)]),
        compiler_params=pltpu.CompilerParams(vmem_limit_bytes=32<<20),
        cost_estimate=pl.CostEstimate(flops=10*10**9, bytes_accessed=5*10**6, transcendentals=10**7),
    )(first, qkv)


def attn_bwd_kernel(first_ref, qkv_ref, do_ref, o_ref, log_ref, out_ref, kt_ref, dk_ref, dv_ref, dq_ref):
    i = pl.program_id(0)
    @pl.when(i == 0)
    def _():
        kt_ref[...] = jnp.transpose(qkv_ref[:, 128:256])
        dk_ref[...] = jnp.zeros_like(dk_ref)
        dv_ref[...] = jnp.zeros_like(dv_ref)
    rows = pl.ds(pl.multiple_of(i * BLK, BLK), BLK)
    both = scaled_q(qkv_ref, rows)
    grads = split_heads(do_ref[...])
    outs = o_ref[...].astype(jnp.float32)
    product = grads.astype(jnp.float32) * jnp.concatenate([outs, outs], axis=0)
    delta = lax.dot_general(jnp.ones((8, 128), jnp.float32), product, NT, precision=lax.Precision.HIGHEST, preferred_element_type=jnp.float32)[0:1]
    logs = log_ref[0]
    dq_ref[...] = jnp.zeros_like(dq_ref)

    def step(j, _):
        at = pl.ds(pl.multiple_of(j * BLK, BLK), BLK)
        probs = jnp.exp(dot(qkv_ref[at, 128:256], both, NT) - logs)
        dp = dot(qkv_ref[at, 256:384], grads, NT)
        ds = (probs * (dp - delta)).astype(jnp.bfloat16)
        dv_ref[at, :] += dot(probs.astype(jnp.bfloat16), grads, NN)
        dk_ref[at, :] += dot(ds, both, NN)
        dq_ref[:, 0:BLK] += dot(kt_ref[0:DH, at], ds[:, 0:BLK], NN)
        dq_ref[:, BLK:] += dot(kt_ref[DH:, at], ds[:, BLK:], NN)
        return 0

    lax.fori_loop(first_ref[i], i + 1, step, 0)
    dq = jnp.concatenate([dq_ref[:, 0:BLK], dq_ref[:, BLK:]], axis=0)
    out_ref[rows, 0:128] = (jnp.transpose(dq) * DH ** -0.5).astype(jnp.bfloat16)

    @pl.when(i == pl.num_programs(0) - 1)
    def _():
        out_ref[:, 128:256] = dk_ref[...].astype(jnp.bfloat16)
        out_ref[:, 256:384] = dv_ref[...].astype(jnp.bfloat16)


def attn_bwd(qkv, do, o, log, first):
    rows = qkv.shape[0]
    n = rows // BLK
    blk = pl.BlockSpec((BLK,128), lambda i,s:(i,0))
    return pl.pallas_call(
        attn_bwd_kernel, name="attn_bwd",
        out_shape=jax.ShapeDtypeStruct((rows,384),jnp.bfloat16),
        grid_spec=pltpu.PrefetchScalarGridSpec(
            num_scalar_prefetch=1, grid=(n,),
            in_specs=[pl.BlockSpec((rows,384), lambda i,s:(0,0)), blk, blk, pl.BlockSpec((1,1,2*BLK), lambda i,s:(i,0,0))],
            out_specs=pl.BlockSpec((rows,384), lambda i,s:(0,0)),
            scratch_shapes=[pltpu.VMEM((128,rows),jnp.bfloat16), pltpu.VMEM((rows,128),jnp.float32), pltpu.VMEM((rows,128),jnp.float32), pltpu.VMEM((DH,2*BLK),jnp.float32)]),
        compiler_params=pltpu.CompilerParams(vmem_limit_bytes=40<<20),
        cost_estimate=pl.CostEstimate(flops=26*10**9, bytes_accessed=9*10**6, transcendentals=10**7),
    )(first, qkv, do, o, log)


def ffn_kernel(n_ref, c_ref, w_ref, f_ref, d_ref, z_ref, g_ref, u_ref):
    n2, c = n_ref[0], c_ref[0]
    wg, wu, wd = w_ref[0], w_ref[1], w_ref[2]
    gate, up, dz = dot(n2, wg, NT), dot(n2, wu, NT), dot(c, wd, NT)
    sig = jax.nn.sigmoid(gate)
    silu = gate * sig
    z = (silu * up).astype(jnp.bfloat16)
    dg = (dz * up * (sig * (1.0 + gate * (1.0 - sig)))).astype(jnp.bfloat16)
    du = (dz * silu).astype(jnp.bfloat16)
    z_ref[0] = z
    g_ref[0] = dg
    u_ref[0] = du
    f_ref[0] = dot(z, wd, NN).astype(jnp.bfloat16)
    d_ref[0] = (dot(dg, wg, NN) + dot(du, wu, NN)).astype(jnp.bfloat16)


def ffn(n2, c, w):
    nb, rows, width = n2.shape; hid = w.shape[1]
    full = pl.BlockSpec((1,rows,width), lambda s:(s,0,0))
    col = pl.BlockSpec((1,rows,hid), lambda s:(s,0,0))
    bf = jnp.bfloat16
    return pl.pallas_call(
        ffn_kernel, name="ffn",
        grid=(nb,),
        out_shape=[jax.ShapeDtypeStruct((nb,rows,width),bf)]*2+[jax.ShapeDtypeStruct((nb,rows,hid),bf)]*3,
        in_specs=[full]*2+[pl.BlockSpec((3,hid,width), lambda s:(0,0,0), pipeline_mode=pl.Buffered(1))],
        out_specs=[full]*2+[col]*3,
        compiler_params=pltpu.CompilerParams(vmem_limit_bytes=56<<20),
        cost_estimate=pl.CostEstimate(flops=2*nb*rows*width*hid*6, bytes_accessed=20*10**6, transcendentals=nb*rows*hid),
    )(n2,c,w)


def ffn_grad_kernel(nb, *refs):
    ns, cs, zs, gs, us = (refs[k*nb:(k+1)*nb] for k in range(5))
    out = refs[5*nb]
    for which, (left, right) in enumerate(((gs, ns), (us, ns), (zs, cs))):
        total = dot(left[0][...], right[0][...], TN)
        for b in range(1, nb):
            total += dot(left[b][...], right[b][...], TN)
        out[which] = total.astype(jnp.bfloat16)


def ffn_grad(ns, cs, zs, gs, us):
    nb = len(ns); rows, width = ns[0].shape; hid = zs[0].shape[1]
    full = pl.BlockSpec((rows,width), lambda s:(0,0))
    col = pl.BlockSpec((rows,HT), lambda s:(0,s))
    return pl.pallas_call(
        functools.partial(ffn_grad_kernel, nb), name="ffn_grad",
        grid=(hid//HT,),
        out_shape=jax.ShapeDtypeStruct((3,hid,width),jnp.bfloat16),
        in_specs=[full]*(2*nb)+[col]*(3*nb),
        out_specs=pl.BlockSpec((3,HT,width), lambda s:(0,s,0)),
        compiler_params=pltpu.CompilerParams(vmem_limit_bytes=56<<20),
        cost_estimate=pl.CostEstimate(flops=2*nb*rows*width*hid*3, bytes_accessed=20*10**6, transcendentals=0),
    )(*ns,*cs,*zs,*gs,*us)


def row_scale(values):
    return lax.rsqrt(jnp.mean(values * values, axis=-1, keepdims=True) + EPS)


def norm_back(grad_normed, values, scale, gain):
    weighted = grad_normed * gain
    inner = jnp.mean(weighted * values, axis=-1, keepdims=True)
    return scale * weighted - values * (scale * scale * scale) * inner


def make(n_dp, n_t):
    ring = list(range(0, n_t, 2)) + list(range(n_t - 1, 0, -2))
    bf = jnp.bfloat16

    def hop(value, k):
        return lax.ppermute(value, "tensor", [(ring[i], ring[(i + k) % n_t]) for i in range(n_t)])

    def flip(value, k):
        return lax.ppermute(value, "dp", [(i, i ^ k) for i in range(n_dp)])

    bits = [1 << b for b in range(n_dp.bit_length() - 1)]
    n_ff = min(n_dp, 4)
    ff_bits = [b for b in bits if b < n_ff]

    def put(buf, piece, start, axis):
        return lax.dynamic_update_slice_in_dim(buf, piece, start, axis)

    def take(buf, start, size, axis):
        return lax.dynamic_slice_in_dim(buf, start, size, axis)

    def gather_dp(piece, axis, me):
        size = piece.shape[axis]
        shape = list(piece.shape)
        shape[axis] = size * n_dp
        buf = put(jnp.zeros(shape, piece.dtype), piece, me * size, axis)
        for k in range(1, n_dp):
            buf = put(buf, flip(piece, k), (me ^ k) * size, axis)
        return buf

    def scatter_sum_dp(whole, axis, me):
        size = whole.shape[axis] // n_dp
        shape = whole.shape
        core = whole.reshape(shape[:axis] + (n_dp, size) + shape[axis + 1 :])
        left = n_dp
        for bit in bits:
            now = core.reshape(core.shape[:axis] + (left // 2, 2) + core.shape[axis + 1 :])
            side = (me // bit) % 2
            keep = lax.dynamic_index_in_dim(now, side, axis + 1, keepdims=False)
            send = lax.dynamic_index_in_dim(now, 1 - side, axis + 1, keepdims=False)
            core = keep + flip(send.astype(bf), bit).astype(jnp.float32)
            left //= 2
        return core.reshape(shape[:axis] + (size,) + shape[axis + 1 :])

    def scatter_sum_all(total, d, at):
        width = total.shape[0] // (n_dp * n_t)
        parts = total.reshape(n_dp, n_t, width)
        own = lax.dynamic_index_in_dim(parts, d, 0, keepdims=False)
        for k in range(1, n_dp):
            own = own + flip(lax.dynamic_index_in_dim(parts, d ^ k, 0, keepdims=False), k)
        mine = lax.dynamic_index_in_dim(own, at[0], 0, keepdims=False)
        for j in range(1, n_t):
            mine = mine + hop(lax.dynamic_index_in_dim(own, at[j], 0, keepdims=False), j)
        return mine

    def on_device(
        tokens, seq_ids, blk_ids, norm1_gain, w_query, w_key, w_value, w_out, norm2_gain,
        w_gate, w_up, w_down, cotangent,
    ):
        d = lax.axis_index("dp")
        t = lax.axis_index("tensor")
        half_t = n_t // 2
        pos = jnp.where(t % 2 == 0, t // 2, n_t - 1 - t // 2)

        def owner(p):
            p = lax.rem(p + 2 * n_t, n_t)
            return jnp.where(p < half_t, 2 * p, 2 * (n_t - 1 - p) + 1)

        ahead = [owner(pos + j) for j in range(n_t)]
        behind = [owner(pos - j) for j in range(n_t)]
        own_rows, width = tokens.shape
        rows = own_rows * n_t
        half = own_rows // 2
        part = width // n_dp

        gains = gather_dp(jnp.stack([norm1_gain, norm2_gain]), 1, d).astype(jnp.float32)
        gain1, gain2 = gains[0:1], gains[1:2]
        w_qkv = gather_dp(jnp.concatenate([w_query, w_key, w_value], axis=1), 0, d)
        resid = tokens.astype(jnp.float32)
        scale1 = row_scale(resid)
        normed1 = (resid * scale1 * gain1).astype(bf)

        all1 = put(jnp.zeros((rows, width), bf), normed1, t * own_rows, 0)
        up_going, down_going = normed1[:half], normed1[half:]
        for k in range(1, n_t):
            up_going = hop(up_going, 1)
            down_going = hop(down_going, -1)
            all1 = put(all1, up_going, behind[k] * own_rows, 0)
            all1 = put(all1, down_going, ahead[k] * own_rows + half, 0)
        qkv = jnp.dot(all1, w_qkv, preferred_element_type=jnp.float32).astype(bf)

        def gather_slots(value):
            acc, ids = value[None], [0]
            for bit in ff_bits[:0:-1]:
                acc = jnp.concatenate([acc, flip(acc, bit)])
                ids = ids + [k ^ bit for k in ids]
            return acc, ids

        hid_t = w_down.shape[0]
        hid = hid_t // n_ff
        shards = jnp.stack([w_gate.T, w_up.T, w_down]).reshape(3, n_ff, hid, part)
        own_w = jnp.zeros((3, hid, width), bf)
        for k in range(n_dp):
            piece = lax.dynamic_index_in_dim(shards, (d ^ k) % n_ff, 1, keepdims=False)
            own_w = put(own_w, flip(piece, k) if k else piece, (d ^ k) * part, 2)
        out_rows = gather_dp(w_out, 1, d)
        out_half = w_out.shape[0] // 2
        core = d % 2
        own_o = take(out_rows, core * out_half, out_half, 0)
        own_w, own_o, all1 = lax.optimization_barrier((own_w, own_o, all1))

        def ring_slots(block, axis):
            cut = block.shape[axis] // 2
            one = lax.slice_in_dim(block, 0, cut, axis=axis)
            two = lax.slice_in_dim(block, cut, 2 * cut, axis=axis)
            out = [(one, two)]
            for _ in range(1, n_t):
                one, two = hop(one, 1), hop(two, -1)
                out.append((one, two))
            return out

        o_slots = ring_slots(own_o, 0)
        o_mine = jnp.concatenate(
            [piece for j in range(n_t) for piece in (o_slots[(n_t - j) % n_t][0], o_slots[j][1])]
        ).reshape(n_t, out_half, width)
        o_peer = flip(o_mine, 1)
        out_full = jnp.where(
            core == 0,
            jnp.concatenate([o_mine, o_peer], axis=1),
            jnp.concatenate([o_peer, o_mine], axis=1),
        ).reshape(n_t * 2 * out_half, width)
        w_slots = ring_slots(own_w, 1)
        weights = jnp.concatenate([piece for pair in w_slots for piece in pair], axis=1)

        units = seq_ids.reshape(-1, 4 * BLK)[:, 0]
        n_units = rows // (4 * BLK)
        same = units[:, None] == units[None, :]
        first_unit = jnp.min(jnp.where(same, jnp.arange(n_units)[None, :], n_units), axis=1)
        first = jnp.repeat(first_unit * 4, 4).astype(jnp.int32)
        attended, logs = attn_fwd(qkv, first)

        mixed_cols = [take(attended, t * own_rows, own_rows, 0)]
        for j in range(1, n_t):
            mixed_cols.append(hop(take(attended, behind[j] * own_rows, own_rows, 0), -j))
        heads_own = jnp.concatenate(mixed_cols, axis=1)
        mixed = resid + jnp.dot(heads_own, out_full, preferred_element_type=jnp.float32)
        scale2 = row_scale(mixed)
        normed2 = (mixed * scale2 * gain2).astype(bf)

        c_slots, ids = gather_slots(cotangent)
        n_slots, _ = gather_slots(normed2)
        c_near = jnp.concatenate([c_slots[:1], flip(c_slots[:1], 1)])
        n_near = jnp.concatenate([n_slots[:1], flip(n_slots[:1], 1)])
        c_far = jnp.concatenate([c_slots[1:], flip(c_slots[1:], 1)])
        n_far = jnp.concatenate([n_slots[1:], flip(n_slots[1:], 1)])
        f_near, d_near, z_near, g_near, u_near = ffn(n_near, c_near, weights)
        f_far, d_far, z_far, g_far, u_far = ffn(n_far, c_far, weights)

        def back_slots(near, far):
            f32 = jnp.float32
            n_far_slots = far.shape[0] // 2
            far_sum = far[:n_far_slots].astype(f32) + flip(far[n_far_slots:], 1).astype(f32)
            near_sum = near[:1].astype(f32) + flip(near[1:], 1).astype(f32)
            acc = jnp.concatenate([near_sum, far_sum])
            for bit in ff_bits[1:]:
                cut = acc.shape[0] // 2
                acc = acc[:cut] + flip(acc[cut:].astype(bf), bit).astype(f32)
            return acc[0]

        grad_normed2 = back_slots(d_near, d_far)
        ffn_total = back_slots(f_near, f_far)
        output = (mixed + ffn_total).astype(bf)
        grad_w = ffn_grad(
            [n_near.reshape(-1, width), n_far.reshape(-1, width)],
            [c_near.reshape(-1, width), c_far.reshape(-1, width)],
            [z.reshape(-1, z.shape[-1]) for z in (z_near, z_far)],
            [g.reshape(-1, g.shape[-1]) for g in (g_near, g_far)],
            [u.reshape(-1, u.shape[-1]) for u in (u_near, u_far)],
        )

        cot = cotangent.astype(jnp.float32)
        grad_mixed = cot + norm_back(grad_normed2, mixed, scale2, gain2)
        grad_gain2 = jnp.sum(grad_normed2 * mixed * scale2, axis=0)
        grad_bf = grad_mixed.astype(bf)
        grad_heads = lax.dot_general(
            grad_bf, out_full, NT, preferred_element_type=jnp.float32
        ).astype(bf)
        wide = 2 * out_half
        grad_att = put(
            jnp.zeros((rows, wide), bf), grad_heads[:, :wide], t * own_rows, 0
        )
        for j in range(1, n_t):
            piece = hop(grad_heads[:, j * wide : (j + 1) * wide], j)
            grad_att = put(grad_att, piece, behind[j] * own_rows, 0)
        grad_qkv = attn_bwd(qkv, grad_att, attended, logs, first)

        back_rows = lax.dot_general(
            grad_qkv, w_qkv, NT, preferred_element_type=jnp.float32
        ).astype(bf)

        def rows_of(which, low):
            return take(back_rows, which * own_rows + (0 if low else half), half, 0)

        one, two = rows_of(behind[n_t - 1], True), rows_of(ahead[n_t - 1], False)
        for k in range(n_t - 2, -1, -1):
            one = hop(one, -1).astype(jnp.float32) + rows_of(behind[k], True).astype(jnp.float32)
            two = hop(two, 1).astype(jnp.float32) + rows_of(ahead[k], False).astype(jnp.float32)
            if k:
                one, two = one.astype(bf), two.astype(bf)
        grad_normed1 = jnp.concatenate([one, two])
        input_grad = (grad_mixed + norm_back(grad_normed1, resid, scale1, gain1)).astype(bf)
        grad_gain1 = jnp.sum(grad_normed1 * resid * scale1, axis=0)

        grad_wqkv = lax.dot_general(all1, grad_qkv, TN, preferred_element_type=jnp.float32)
        grad_wqkv = scatter_sum_dp(grad_wqkv, 0, d)
        grad_query, grad_key, grad_value = jnp.split(grad_wqkv, 3, axis=1)

        grad_wo = lax.dot_general(heads_own, grad_bf, TN, preferred_element_type=jnp.float32)
        grad_wo = scatter_sum_dp(grad_wo, 1, d).astype(bf).reshape(n_t, wide, part)
        grad_out = grad_wo[0].astype(jnp.float32)
        for j in range(1, n_t):
            grad_out = grad_out + hop(grad_wo[j], j).astype(jnp.float32)

        cut = hid // 2
        g_slots = grad_w.reshape(3, n_t, 2, cut, width)
        one, two = g_slots[:, n_t - 1, 0], g_slots[:, n_t - 1, 1]
        for k in range(n_t - 2, -1, -1):
            one = (hop(one, -1).astype(jnp.float32) + g_slots[:, k, 0].astype(jnp.float32)).astype(bf)
            two = (hop(two, 1).astype(jnp.float32) + g_slots[:, k, 1].astype(jnp.float32)).astype(bf)
        summed = jnp.concatenate([one, two], axis=1).reshape(3, hid, n_dp, part)
        full = jnp.zeros((3, n_ff, hid, part), jnp.float32)
        for k in range(n_ff):
            total = 0.0
            for far in range(k, n_dp, n_ff):
                piece = lax.dynamic_index_in_dim(summed, d ^ far, 2, keepdims=False)[:, None]
                total = total + (flip(piece, far) if far else piece).astype(jnp.float32)
            full = put(full, total, (d ^ k) % n_ff, 1)
        full = full.reshape(3, hid_t, part)
        grad_gate, grad_up, grad_down = full[0].T, full[1].T, full[2]

        grad_norm1 = scatter_sum_all(grad_gain1, d, [t] + ahead[1:])
        grad_norm2 = scatter_sum_all(grad_gain2, d, [t] + ahead[1:])
        return (
            output, input_grad, grad_query, grad_key, grad_value, grad_out,
            grad_gate, grad_up, grad_down, grad_norm1, grad_norm2,
        )

    return on_device


def solution(mesh):
    rows = P(("dp", "tensor"), None)
    return jax.shard_map(
        make(mesh.shape["dp"], mesh.shape["tensor"]),
        mesh=mesh,
        in_specs=(
            rows, P("dp"), P("dp"), P("dp"), P("dp", "tensor"), P("dp", "tensor"),
            P("dp", "tensor"), P("tensor", "dp"), P("dp"), P("dp", "tensor"),
            P("dp", "tensor"), P("tensor", "dp"), rows,
        ),
        out_specs=(
            rows, rows, P("dp", "tensor"), P("dp", "tensor"), P("dp", "tensor"),
            P("tensor", "dp"), P("dp", "tensor"), P("dp", "tensor"), P("tensor", "dp"),
            P(("dp", "tensor")), P(("dp", "tensor")),
        ),
        check_vma=False,
    )
```

time: 1460 us -> 635 us (0.43)
  waiting for transfers between devices: 888 us -> 201 us
  matrix products: 316 us -> 20.1 us
  starting transfers between devices: 1.19 us -> 146 us
  Pallas kernels: 0 us -> 128 us
  blocking collectives: 77.9 us -> 0 us
  other arithmetic: 115 us -> 51.8 us
  local copies, waits for them, and re-layouts: 16.3 us -> 74.8 us
  loops' own time: 24.7 us -> 0 us
    reduce_scatter x11 -> x0, waiting for transfers between devices: 523 us -> none  [the longest x1 200 us: on_device(): lax.psum_scatter(jnp.dot(piece, out_full, preferred_element_type=jnp.floa...]
    all_gather x7 -> x0, waiting for transfers between devices: 362 us -> none  [the longest x1 101 us: on_device(): grad_rows = lax.all_gather(cotangent, 'tensor', axis=0, tiled=True)]
    dot_general x63 -> x6, matrix products: 316 us -> 20.1 us  [the longest x1 6.22 us: on_device(): qkv = jnp.dot(all1, w_qkv, preferred_element_type=jnp.float32).astype(bf)]
    ppermute x0 -> x143, waiting for transfers between devices: none -> 201 us  [the longest x105 158 us: hop(): lax.ppermute(value, 'tensor', [(ring[i], ring[(i + k) % n_t]) for i in ra...]
    ppermute x0 -> x143, starting transfers between devices: none -> 146 us  [the longest x105 131 us: hop(): lax.ppermute(value, 'tensor', [(ring[i], ring[(i + k) % n_t]) for i in ra...]
    pallas_call x0 -> x5, Pallas kernels: none -> 128 us  [the longest x1 42.2 us: attn_bwd(): pl.pallas_call(attn_bwd_kernel, name='attn_bwd', out_shape=jax.ShapeDtype...]
    unnamed x1 -> x0, blocking collectives: 42.2 us -> none
    all_gather x6 -> x0, blocking collectives: 35.7 us -> none  [the longest x1 6.5 us: on_device(): lax.all_gather(w_query, 'dp', axis=0, tiled=True)]
  transfers between devices with their start and end apart: 18 -> 143, of which waited for: 11 -> 62; matrix products, arithmetic and copies ran while one was open for 21% -> 21% of each run, Pallas kernels for 0% -> 18%
where the time goes in v1:
time: 635 us; the launch traced here: 624 us
  waiting for transfers between devices  201 us (32%)
  starting transfers between devices  146 us (23%)
  Pallas kernels  128 us (20%)
  local copies, waits for them, and re-layouts  74.8 us (12%)
  other arithmetic  51.8 us (8%)
  matrix products  20.1 us (3%)
    ppermute x105, waiting for transfers between devices, hop(): lax.ppermute(value, 'tensor', [(ring[i], ring[(i + k) % n_t]) for i in ra...  158 us
    ppermute x105, starting transfers between devices, hop(): lax.ppermute(value, 'tensor', [(ring[i], ring[(i + k) % n_t]) for i in ra...  131 us
    ppermute x38, waiting for transfers between devices, flip(): return lax.ppermute(value, 'dp', [(i, i ^ k) for i in range(n_dp)])  43 us
    pallas_call x1, Pallas kernels, attn_bwd(): pl.pallas_call(attn_bwd_kernel, name='attn_bwd', out_shape=jax.ShapeDtype...  42.2 us
    pallas_call x1, Pallas kernels, attn_fwd(): pl.pallas_call(attn_fwd_kernel, name='attn_fwd', out_shape=(jax.ShapeDtyp...  39.1 us
    pallas_call x2, Pallas kernels, ffn(): pl.pallas_call(ffn_kernel, name='ffn', grid=(nb,), out_shape=[jax.ShapeDt...  31 us
    unnamed x107, local copies, waits for them, and re-layouts  24.3 us
    dynamic_update_slice x37, local copies, waits for them, and re-layouts, put(): return lax.dynamic_update_slice_in_dim(buf, piece, start, axis)  18.1 us
  transfers between devices with their start and end apart: 143, of which 62 were waited for; matrix products, arithmetic and copies ran while one was open for 21% of the time, Pallas kernels for 18%

profile of v1, /device:TPU:0, one launch (start us, length us, event | category | flops | bytes accessed | tf_op | source)
XLA Modules:
  0.0 623.9 jit_solution(9098556344514844914)
XLA Ops:
  2.6 2.6 collective-permute-start.1
  14.8 3.5 broadcast_in_dim.60
  23.2 4.1 collective-permute-done.31
  27.4 3.7 collective-permute-done.32
  45.8 13.3 %collective-permute-done.28 = bf16[3,128,256]{2,1,0:T(8,128)(2,1)S(1)} collective-permute-done((bf16[3,128,256]{2,1,0:T(8,128)(2,1)}, bf16[3,128,256]{2,1,0:T(8,128)(2,1)S(1)}, u32[]{:S(2)}, u32[]{:S(2)}) %collective-permute-start.28) | collective-permute-done | bytes 196640 | tf_op jit(solution)/shard_map/ppermute | solution.py:209
  61.4 4.8 collective-permute-done.29
  79.4 3.1 collective-permute-done.10
  107.8 3.1 collective-permute-done.16
  112.6 6.2 convolution_convert_fusion.1.qkv_ref
  120.9 39.1 %attn_fwd.1 = (bf16[3072,128]{1,0:T(8,128)(2,1)S(1)}, f32[12,1,512]{2,1,0:T(1,128)S(1)}) custom-call(s32[12]{0:T(128)S(1)} %reshape.224.first_ref, bf16[3072,384]{1,0:T(8,128)(2,1)S(1)} %convolution_convert_fusion.1.qkv_ref), custom_call_target="tpu_custom_call" | custom-call | flops 10000000000 | bytes 5000000 | tf_op jit(solution)/shard_map/attn_fwd/pallas_call | solution.py:67
  162.2 2.9 collective-permute-done.41
  179.8 3.0 collective-permute-done.44
  188.9 6.7 %collective-permute-done.46 = bf16[32,1024]{1,0:T(8,128)(2,1)S(1)} collective-permute-done((bf16[32,1024]{1,0:T(8,128)(2,1)S(1)}, bf16[32,1024]{1,0:T(8,128)(2,1)S(1)}, u32[]{:S(2)}, u32[]{:S(2)}) %collective-permute-start.46) | collective-permute-done | bytes 65568 | tf_op jit(solution)/shard_map/ppermute | solution.py:206
  195.6 2.8 collective-permute-start.23
  203.1 4.2 collective-permute-done.24
  207.4 10.4 %collective-permute-done.25 = bf16[384,128]{1,0:T(8,128)(2,1)S(1)} collective-permute-done((bf16[384,128]{1,0:T(8,128)(2,1)S(1)}, bf16[384,128]{1,0:T(8,128)(2,1)S(1)}, u32[]{:S(2)}, u32[]{:S(2)}) %collective-permute-start.25) | collective-permute-done | bytes 98336 | tf_op jit(solution)/shard_map/ppermute | solution.py:206
  223.1 6.8 %collective-permute-done.54 = bf16[3,64,1024]{2,1,0:T(8,128)(2,1)S(1)} collective-permute-done((bf16[3,64,1024]{2,1,0:T(8,128)(2,1)S(1)}, bf16[3,64,1024]{2,1,0:T(8,128)(2,1)S(1)}, u32[]{:S(2)}, u32[]{:S(2)}) %collective-permute-start.54) | collective-permute-done | bytes 393248 | tf_op jit(solution)/shard_map/ppermute | solution.py:206
  234.5 5.8 collective-permute-done.56
  245.5 4.4 collective-permute-done.58
  254.4 4.2 collective-permute-done.60
  263.9 3.3 collective-permute-done.62
  269.9 15.5 %ffn.2 = (bf16[2,384,1024]{2,1,0:T(8,128)(2,1)}, bf16[2,384,1024]{2,1,0:T(8,128)(2,1)}, bf16[2,384,1024]{2,1,0:T(8,128)(2,1)}, bf16[2,384,1024]{2,1,0:T(8,128)(2,1)}, bf16[2,384,1024]{2,1,0:T(8,128)(2,1)}) custom-call(bf16[2,384,1024]{2,1,0:T(8,128)(2,1)} %pad_maximum_fusion.n_ref, bf16[2,384,1024]{2,1,0:T(8,128)(2,1)} %pad_maximum_fusion.1.c_ref, ...), custom_call_target="tpu_custom_call" | custom-call | flops 9663676416 | bytes 20000000 | tf_op jit(solution)/shard_map/ffn/pallas_call | solution.py:155
  286.6 15.5 %ffn.3 = (bf16[2,384,1024]{2,1,0:T(8,128)(2,1)}, bf16[2,384,1024]{2,1,0:T(8,128)(2,1)}, bf16[2,384,1024]{2,1,0:T(8,128)(2,1)}, bf16[2,384,1024]{2,1,0:T(8,128)(2,1)}, bf16[2,384,1024]{2,1,0:T(8,128)(2,1)}) custom-call(bf16[2,384,1024]{2,1,0:T(8,128)(2,1)} %copy-done.27, bf16[2,384,1024]{2,1,0:T(8,128)(2,1)} %copy-done.28, ...), custom_call_target="tpu_custom_call" | custom-call | flops 9663676416 | bytes 20000000 | tf_op jit(solution)/shard_map/ffn/pallas_call | solution.py:155
  303.4 15.8 %ffn_grad.1 = bf16[3,1024,1024]{2,1,0:T(8,128)(2,1)} custom-call(bf16[768,1024]{1,0:T(8,128)(2,1)} %bitcast.310, bf16[768,1024]{1,0:T(8,128)(2,1)} %bitcast.319, bf16[768,1024]{1,0:T(8,128)(2,1)} %bitcast.309, bf16[768,1024]{1,0:T(8,128)(2,1)} %bitcast.320, bf16[768,1024]{1,0:T(8,128)(2,1)} %bitcast.333, bf16[768,1024]{1,0:T(8,128)(2,1)} %bitcast.336, ...), custom_call_target="tpu_custom_call" | custom-call | flops 9663676416 | bytes 20000000 | tf_op jit(solution)/shard_map/ffn_grad/pallas_call | solution.py:180
  324.2 8.1 %collective-permute-done.106 = bf16[3,64,1024]{2,1,0:T(8,128)(2,1)S(1)} collective-permute-done((bf16[3,64,1024]{2,1,0:T(8,128)(2,1)S(1)}, bf16[3,64,1024]{2,1,0:T(8,128)(2,1)S(1)}, u32[]{:S(2)}, u32[]{:S(2)}) %collective-permute-start.106) | collective-permute-done | bytes 393248 | tf_op jit(solution)/shard_map/ppermute | solution.py:206
  336.5 8.0 %collective-permute-done.107 = bf16[3,64,1024]{2,1,0:T(8,128)(2,1)S(1)} collective-permute-done((bf16[3,64,1024]{2,1,0:T(8,128)(2,1)S(1)}, bf16[3,64,1024]{2,1,0:T(8,128)(2,1)S(1)}, u32[]{:S(2)}, u32[]{:S(2)}) %collective-permute-start.107) | collective-permute-done | bytes 393248 | tf_op jit(solution)/shard_map/ppermute | solution.py:206
  363.9 11.0 %collective-permute-done.70 = bf16[1,384,1024]{2,1,0:T(8,128)(2,1)S(1)} collective-permute-done((bf16[1,384,1024]{2,1,0:T(8,128)(2,1)S(1)}, bf16[1,384,1024]{2,1,0:T(8,128)(2,1)S(1)}, u32[]{:S(2)}, u32[]{:S(2)}) %collective-permute-start.70) | collective-permute-done | bytes 786464 | tf_op jit(solution)/shard_map/ppermute | solution.py:209
  374.9 3.4 subtract_add_fusion
  392.6 2.9 copy.142
  405.4 2.8 collective-permute-start.139
  411.7 2.6 collective-permute-done.138
  416.1 2.8 collective-permute-start.77
  419.7 3.2 collective-permute-start.79
  427.3 3.5 collective-permute-done.79
  432.6 42.2 %attn_bwd.1 = bf16[3072,384]{1,0:T(8,128)(2,1)S(1)} custom-call(s32[12]{0:T(128)S(1)} %reshape.224.first_ref, bf16[3072,384]{1,0:T(8,128)(2,1)S(1)} %copy-done.1, bf16[3072,128]{1,0:T(8,128)(2,1)S(1)} %constant_dynamic-update-slice_fusion.45.do_ref, bf16[3072,128]{1,0:T(8,128)(2,1)S(1)} %get-tuple-element.26.o_ref, f32[12,1,512]{2,1,0:T(1,128)S(1)} %get-tuple-element.33.log_ref), custom_call_target="tpu_custom_call" | custom-call | flops 25999998976 | bytes 9000000 | tf_op jit(solution)/shard_map/attn_bwd/pallas_call | solution.py:121
  474.8 5.6 fusion.83
  480.6 3.7 convolution_convert_fusion
  484.5 2.7 collective-permute-start.88
  490.7 6.3 %collective-permute-done.81 = bf16[192,1024]{1,0:T(8,128)(2,1)S(1)} collective-permute-done((bf16[192,1024]{1,0:T(8,128)(2,1)S(1)}, bf16[192,1024]{1,0:T(8,128)(2,1)S(1)}, u32[]{:S(2)}, u32[]{:S(2)}) %collective-permute-start.81) | collective-permute-done | bytes 393248 | tf_op jit(solution)/shard_map/ppermute | solution.py:206
  499.1 4.4 collective-permute-done.96
  509.5 4.4 collective-permute-done.82
  539.2 2.6 collective-permute-start.104
  552.6 3.4 collective-permute-start.92
  557.3 3.3 collective-permute-start.100
  561.8 7.6 %collective-permute-done.101 = bf16[128,256]{1,0:T(8,128)(2,1)S(1)} collective-permute-done((bf16[128,256]{1,0:T(8,128)(2,1)S(1)}, bf16[128,256]{1,0:T(8,128)(2,1)S(1)}, u32[]{:S(2)}, u32[]{:S(2)}) %collective-permute-start.101) | collective-permute-done | bytes 65568 | tf_op jit(solution)/shard_map/ppermute | solution.py:206
  577.2 8.9 %collective-permute-done.86 = bf16[192,1024]{1,0:T(8,128)(2,1)S(1)} collective-permute-done((bf16[192,1024]{1,0:T(8,128)(2,1)S(1)}, bf16[192,1024]{1,0:T(8,128)(2,1)S(1)}, u32[]{:S(2)}, u32[]{:S(2)}) %collective-permute-start.86) | collective-permute-done | bytes 393248 | tf_op jit(solution)/shard_map/ppermute | solution.py:206
  593.9 6.5 %collective-permute-done.87 = bf16[192,1024]{1,0:T(8,128)(2,1)} collective-permute-done((bf16[192,1024]{1,0:T(8,128)(2,1)}, bf16[192,1024]{1,0:T(8,128)(2,1)}, u32[]{:S(2)}, u32[]{:S(2)}) %collective-permute-start.87) | collective-permute-done | bytes 393248 | tf_op jit(solution)/shard_map/ppermute | solution.py:206
  615.8 2.7 collective-permute-start.128
  (501 shorter events, 283.8 us)
Async XLA Ops:
  7.8 25.9 %collective-permute-start.17 = (bf16[256,384]{1,0:T(8,128)(2,1)S(1)}, bf16[256,384]{1,0:T(8,128)(2,1)}, u32[]{:S(2)}, u32[]{:S(2)}) collective-permute-start(bf16[256,384]{1,0:T(8,128)(2,1)S(1)} %constant_dynamic-update-slice_fusion), channel_id=1, source_target_pairs={{0,8},{8,0},{16,24},{24,16},{1,9},{9,1},{17,25},{25,17},{2,10},{10... | collective-permute-start | bytes 589832 | tf_op jit(solution)/shard_map/ppermute | solution.py:209
  8.0 26.3 %collective-permute-start.18 = (bf16[256,384]{1,0:T(8,128)(2,1)S(1)}, bf16[256,384]{1,0:T(8,128)(2,1)}, u32[]{:S(2)}, u32[]{:S(2)}) collective-permute-start(bf16[256,384]{1,0:T(8,128)(2,1)S(1)} %constant_dynamic-update-slice_fusion), channel_id=1, source_target_pairs={{0,16},{8,24},{16,0},{24,8},{1,17},{9,25},{17,1},{25,9},{2,18},{10... | collective-permute-start | bytes 589832 | tf_op jit(solution)/shard_map/ppermute | solution.py:209
  33.8 25.3 %collective-permute-start.6 = (bf16[192,1024]{1,0:T(8,128)(2,1)S(1)}, bf16[192,1024]{1,0:T(8,128)(2,1)S(1)}, u32[]{:S(2)}, u32[]{:S(2)}) collective-permute-start(bf16[192,1024]{1,0:T(8,128)(2,1)S(1)} %collective-permute-done.4), channel_id=1, source_target_pairs={{0,1},{2,0},{4,2},{6,4},{7,6},{5,7},{3,5},{1,3},{8,9},{10,8},{12,1... | collective-permute-start | bytes 1179656 | tf_op jit(solution)/shard_map/ppermute | solution.py:206
  34.4 35.3 %collective-permute-start.67 = (bf16[1,384,1024]{2,1,0:T(8,128)(2,1)S(1)}, bf16[1,384,1024]{2,1,0:T(8,128)(2,1)S(1)}, u32[]{:S(2)}, u32[]{:S(2)}) collective-permute-start(bf16[1,384,1024]{2,1,0:T(8,128)(2,1)S(1)} %bitcast.301), channel_id=1, source_target_pairs={{0,16},{8,24},{16,0},{24,8},{1,17},{9,25},{17,1},{25,9},{2,18},{10... | collective-permute-start | bytes 2359304 | tf_op jit(solution)/shard_map/ppermute | solution.py:209
  38.1 35.9 %collective-permute-start.49 = (bf16[1,384,1024]{2,1,0:T(8,128)(2,1)S(1)}, bf16[1,384,1024]{2,1,0:T(8,128)(2,1)S(1)}, u32[]{:S(2)}, u32[]{:S(2)}) collective-permute-start(bf16[1,384,1024]{2,1,0:T(8,128)(2,1)S(1)} %bitcast.302), channel_id=1, source_target_pairs={{0,8},{8,0},{16,24},{24,16},{1,9},{9,1},{17,25},{25,17},{2,10},{10... | collective-permute-start | bytes 2359304 | tf_op jit(solution)/shard_map/ppermute | solution.py:209
  38.1 21.0 %collective-permute-start.28 = (bf16[3,128,256]{2,1,0:T(8,128)(2,1)}, bf16[3,128,256]{2,1,0:T(8,128)(2,1)S(1)}, u32[]{:S(2)}, u32[]{:S(2)}) collective-permute-start(bf16[3,128,256]{2,1,0:T(8,128)(2,1)} %get-tuple-element.99), channel_id=1, source_target_pairs={{0,16},{8,24},{16,0},{24,8},{1,17},{9,25},{17,1},{25,9},{2,18},{10... | collective-permute-start | bytes 589832 | tf_op jit(solution)/shard_map/ppermute | solution.py:209
  43.4 22.9 %collective-permute-start.7 = (bf16[192,1024]{1,0:T(8,128)(2,1)S(1)}, bf16[192,1024]{1,0:T(8,128)(2,1)S(1)}, u32[]{:S(2)}, u32[]{:S(2)}) collective-permute-start(bf16[192,1024]{1,0:T(8,128)(2,1)S(1)} %collective-permute-done.5), channel_id=1, source_target_pairs={{0,2},{2,4},{4,6},{6,7},{7,5},{5,3},{3,1},{1,0},{8,10},{10,12},{12... | collective-permute-start | bytes 1179656 | tf_op jit(solution)/shard_map/ppermute | solution.py:206
  69.7 24.5 %collective-permute-start.68 = (bf16[1,384,1024]{2,1,0:T(8,128)(2,1)S(1)}, bf16[1,384,1024]{2,1,0:T(8,128)(2,1)S(1)}, u32[]{:S(2)}, u32[]{:S(2)}) collective-permute-start(bf16[1,384,1024]{2,1,0:T(8,128)(2,1)S(1)} %collective-permute-done.67), channel_id=1, source_target_pairs={{0,8},{8,0},{16,24},{24,16},{1,9},{9,1},{17,25},{25,17},{2,10},{10... | collective-permute-start | bytes 2359304 | tf_op jit(solution)/shard_map/ppermute | solution.py:209
  118.8 41.2 %collective-permute-start.40 = (bf16[32,1024]{1,0:T(8,128)(2,1)S(1)}, bf16[32,1024]{1,0:T(8,128)(2,1)S(1)}, u32[]{:S(2)}, u32[]{:S(2)}) collective-permute-start(bf16[32,1024]{1,0:T(8,128)(2,1)S(1)} %get-tuple-element.121), channel_id=1, source_target_pairs={{0,1},{2,0},{4,2},{6,4},{7,6},{5,7},{3,5},{1,3},{8,9},{10,8},{12,1... | collective-permute-start | bytes 196616 | tf_op jit(solution)/shard_map/ppermute | solution.py:206
  120.1 41.2 %collective-permute-start.34 = (bf16[32,1024]{1,0:T(8,128)(2,1)S(1)}, bf16[32,1024]{1,0:T(8,128)(2,1)S(1)}, u32[]{:S(2)}, u32[]{:S(2)}) collective-permute-start(bf16[32,1024]{1,0:T(8,128)(2,1)S(1)} %collective-permute-done.33), channel_id=1, source_target_pairs={{0,2},{2,4},{4,6},{6,7},{7,5},{5,3},{3,1},{1,0},{8,10},{10,12},{12... | collective-permute-start | bytes 196616 | tf_op jit(solution)/shard_map/ppermute | solution.py:206
  172.8 25.7 %collective-permute-start.21 = (bf16[384,128]{1,0:T(8,128)(2,1)S(1)}, bf16[384,128]{1,0:T(8,128)(2,1)S(1)}, u32[]{:S(2)}, u32[]{:S(2)}) collective-permute-start(bf16[384,128]{1,0:T(8,128)(2,1)S(1)} %get-tuple-element.106), channel_id=1, source_target_pairs={{0,3},{2,1},{4,0},{6,2},{7,4},{5,6},{3,7},{1,5},{8,11},{10,9},{12,... | collective-permute-start | bytes 294920 | tf_op jit(solution)/shard_map/ppermute | solution.py:206
  175.1 23.5 %collective-permute-start.22 = (bf16[384,128]{1,0:T(8,128)(2,1)S(1)}, bf16[384,128]{1,0:T(8,128)(2,1)S(1)}, u32[]{:S(2)}, u32[]{:S(2)}) collective-permute-start(bf16[384,128]{1,0:T(8,128)(2,1)S(1)} %get-tuple-element.105), channel_id=1, source_target_pairs={{0,5},{2,3},{4,1},{6,0},{7,2},{5,4},{3,6},{1,7},{8,13},{10,11},{12... | collective-permute-start | bytes 294920 | tf_op jit(solution)/shard_map/ppermute | solution.py:206
  179.2 19.9 %collective-permute-start.50 = (bf16[3,64,1024]{2,1,0:T(8,128)(2,1)S(1)}, bf16[3,64,1024]{2,1,0:T(8,128)(2,1)S(1)}, u32[]{:S(2)}, u32[]{:S(2)}) collective-permute-start(bf16[3,64,1024]{2,1,0:T(8,128)(2,1)S(1)} %get-tuple-element.97), channel_id=1, source_target_pairs={{0,2},{2,4},{4,6},{6,7},{7,5},{5,3},{3,1},{1,0},{8,10},{10,12},{12... | collective-permute-start | bytes 1179656 | tf_op jit(solution)/shard_map/ppermute | solution.py:206
  198.4 33.5 %collective-permute-start.47 = (bf16[8,64,1024]{2,1,0:T(8,128)(2,1)S(1)}, bf16[8,64,1024]{2,1,0:T(8,128)(2,1)S(1)}, u32[]{:S(2)}, u32[]{:S(2)}) collective-permute-start(bf16[8,64,1024]{2,1,0:T(8,128)(2,1)S(1)} %bitcast.311), channel_id=1, source_target_pairs={{0,8},{8,0},{16,24},{24,16},{1,9},{9,1},{17,25},{25,17},{2,10},{10... | collective-permute-start | bytes 3145736 | tf_op jit(solution)/shard_map/ppermute | solution.py:209
  199.0 18.8 %collective-permute-start.52 = (bf16[3,64,1024]{2,1,0:T(8,128)(2,1)S(1)}, bf16[3,64,1024]{2,1,0:T(8,128)(2,1)S(1)}, u32[]{:S(2)}, u32[]{:S(2)}) collective-permute-start(bf16[3,64,1024]{2,1,0:T(8,128)(2,1)S(1)} %collective-permute-done.50), channel_id=1, source_target_pairs={{0,2},{2,4},{4,6},{6,7},{7,5},{5,3},{3,1},{1,0},{8,10},{10,12},{12... | collective-permute-start | bytes 1179656 | tf_op jit(solution)/shard_map/ppermute | solution.py:206
  201.1 18.0 %collective-permute-start.53 = (bf16[3,64,1024]{2,1,0:T(8,128)(2,1)S(1)}, bf16[3,64,1024]{2,1,0:T(8,128)(2,1)S(1)}, u32[]{:S(2)}, u32[]{:S(2)}) collective-permute-start(bf16[3,64,1024]{2,1,0:T(8,128)(2,1)S(1)} %collective-permute-done.51), channel_id=1, source_target_pairs={{0,1},{2,0},{4,2},{6,4},{7,6},{5,7},{3,5},{1,3},{8,9},{10,8},{12,1... | collective-permute-start | bytes 1179656 | tf_op jit(solution)/shard_map/ppermute | solution.py:206
  203.1 14.7 %collective-permute-start.25 = (bf16[384,128]{1,0:T(8,128)(2,1)S(1)}, bf16[384,128]{1,0:T(8,128)(2,1)S(1)}, u32[]{:S(2)}, u32[]{:S(2)}) collective-permute-start(bf16[384,128]{1,0:T(8,128)(2,1)S(1)} %get-tuple-element.102), channel_id=1, source_target_pairs={{0,4},{2,6},{4,7},{6,5},{7,3},{5,1},{3,0},{1,2},{8,12},{10,14},{12... | collective-permute-start | bytes 294920 | tf_op jit(solution)/shard_map/ppermute | solution.py:206
  234.5 19.9 %collective-permute-start.65 = (bf16[1,384,1024]{2,1,0:T(8,128)(2,1)S(1)}, bf16[1,384,1024]{2,1,0:T(8,128)(2,1)S(1)}, u32[]{:S(2)}, u32[]{:S(2)}) collective-permute-start(bf16[1,384,1024]{2,1,0:T(8,128)(2,1)S(1)} %fusion.15), channel_id=1, source_target_pairs={{0,16},{8,24},{16,0},{24,8},{1,17},{9,25},{17,1},{25,9},{2,18},{10... | collective-permute-start | bytes 2359304 | tf_op jit(solution)/shard_map/ppermute | solution.py:209
  243.2 17.8 %collective-permute-start.48 = (bf16[1,384,1024]{2,1,0:T(8,128)(2,1)S(1)}, bf16[1,384,1024]{2,1,0:T(8,128)(2,1)S(1)}, u32[]{:S(2)}, u32[]{:S(2)}) collective-permute-start(bf16[1,384,1024]{2,1,0:T(8,128)(2,1)S(1)} %fusion.15), channel_id=1, source_target_pairs={{0,8},{8,0},{16,24},{24,16},{1,9},{9,1},{17,25},{25,17},{2,10},{10... | collective-permute-start | bytes 2359304 | tf_op jit(solution)/shard_map/ppermute | solution.py:209
  254.4 31.0 %collective-permute-start.66 = (bf16[1,384,1024]{2,1,0:T(8,128)(2,1)S(1)}, bf16[1,384,1024]{2,1,0:T(8,128)(2,1)S(1)}, u32[]{:S(2)}, u32[]{:S(2)}) collective-permute-start(bf16[1,384,1024]{2,1,0:T(8,128)(2,1)S(1)} %collective-permute-done.65), channel_id=1, source_target_pairs={{0,8},{8,0},{16,24},{24,16},{1,9},{9,1},{17,25},{25,17},{2,10},{10... | collective-permute-start | bytes 2359304 | tf_op jit(solution)/shard_map/ppermute | solution.py:209
  303.3 32.0 %collective-permute-start.72 = (bf16[1,384,1024]{2,1,0:T(8,128)(2,1)S(1)}, bf16[1,384,1024]{2,1,0:T(8,128)(2,1)S(1)}, u32[]{:S(2)}, u32[]{:S(2)}) collective-permute-start(bf16[1,384,1024]{2,1,0:T(8,128)(2,1)S(1)} %slice.207), channel_id=1, source_target_pairs={{0,8},{8,0},{16,24},{24,16},{1,9},{9,1},{17,25},{25,17},{2,10},{10... | collective-permute-start | bytes 2359304 | tf_op jit(solution)/shard_map/ppermute | solution.py:209
  322.4 30.8 %collective-permute-start.69 = (bf16[1,384,1024]{2,1,0:T(8,128)(2,1)}, bf16[1,384,1024]{2,1,0:T(8,128)(2,1)}, u32[]{:S(2)}, u32[]{:S(2)}) collective-permute-start(bf16[1,384,1024]{2,1,0:T(8,128)(2,1)} %slice.203), channel_id=1, source_target_pairs={{0,8},{8,0},{16,24},{24,16},{1,9},{9,1},{17,25},{25,17},{2,10},{10... | collective-permute-start | bytes 2359304 | tf_op jit(solution)/shard_map/ppermute | solution.py:209
  335.3 26.3 %collective-permute-start.71 = (bf16[1,384,1024]{2,1,0:T(8,128)(2,1)}, bf16[1,384,1024]{2,1,0:T(8,128)(2,1)}, u32[]{:S(2)}, u32[]{:S(2)}) collective-permute-start(bf16[1,384,1024]{2,1,0:T(8,128)(2,1)} %slice.205), channel_id=1, source_target_pairs={{0,8},{8,0},{16,24},{24,16},{1,9},{9,1},{17,25},{25,17},{2,10},{10... | collective-permute-start | bytes 2359304 | tf_op jit(solution)/shard_map/ppermute | solution.py:209
  336.5 25.4 %collective-permute-start.73 = (bf16[1,384,1024]{2,1,0:T(8,128)(2,1)}, bf16[1,384,1024]{2,1,0:T(8,128)(2,1)}, u32[]{:S(2)}, u32[]{:S(2)}) collective-permute-start(bf16[1,384,1024]{2,1,0:T(8,128)(2,1)} %add_convert_fusion), channel_id=1, source_target_pairs={{0,16},{8,24},{16,0},{24,8},{1,17},{9,25},{17,1},{25,9},{2,18},{10... | collective-permute-start | bytes 2359304 | tf_op jit(solution)/shard_map/ppermute | solution.py:209
  357.0 17.9 %collective-permute-start.70 = (bf16[1,384,1024]{2,1,0:T(8,128)(2,1)S(1)}, bf16[1,384,1024]{2,1,0:T(8,128)(2,1)S(1)}, u32[]{:S(2)}, u32[]{:S(2)}) collective-permute-start(bf16[1,384,1024]{2,1,0:T(8,128)(2,1)S(1)} %add_convert_fusion.1), channel_id=1, source_target_pairs={{0,16},{8,24},{16,0},{24,8},{1,17},{9,25},{17,1},{25,9},{2,18},{10... | collective-permute-start | bytes 2359304 | tf_op jit(solution)/shard_map/ppermute | solution.py:209
  359.9 27.2 %collective-permute-start.109 = (bf16[3,64,1024]{2,1,0:T(8,128)(2,1)}, bf16[3,64,1024]{2,1,0:T(8,128)(2,1)}, u32[]{:S(2)}, u32[]{:S(2)}) collective-permute-start(bf16[3,64,1024]{2,1,0:T(8,128)(2,1)} %get-tuple-element.59), channel_id=1, source_target_pairs={{0,1},{2,0},{4,2},{6,4},{7,6},{5,7},{3,5},{1,3},{8,9},{10,8},{12,1... | collective-permute-start | bytes 1179656 | tf_op jit(solution)/shard_map/ppermute | solution.py:206
  361.6 25.8 %collective-permute-start.115 = (bf16[3,64,1024]{2,1,0:T(8,128)(2,1)}, bf16[3,64,1024]{2,1,0:T(8,128)(2,1)}, u32[]{:S(2)}, u32[]{:S(2)}) collective-permute-start(bf16[3,64,1024]{2,1,0:T(8,128)(2,1)} %get-tuple-element.60), channel_id=1, source_target_pairs={{0,2},{2,4},{4,6},{6,7},{7,5},{5,3},{3,1},{1,0},{8,10},{10,12},{12... | collective-permute-start | bytes 1179656 | tf_op jit(solution)/shard_map/ppermute | solution.py:206
  380.5 39.3 %collective-permute-start.74 = (bf16[384,128]{1,0:T(8,128)(2,1)}, bf16[384,128]{1,0:T(8,128)(2,1)}, u32[]{:S(2)}, u32[]{:S(2)}) collective-permute-start(bf16[384,128]{1,0:T(8,128)(2,1)} %get-tuple-element.94), channel_id=1, source_target_pairs={{0,2},{2,4},{4,6},{6,7},{7,5},{5,3},{3,1},{1,0},{8,10},{10,12},{12... | collective-permute-start | bytes 294920 | tf_op jit(solution)/shard_map/ppermute | solution.py:206
  382.2 41.6 %collective-permute-start.75 = (bf16[384,128]{1,0:T(8,128)(2,1)}, bf16[384,128]{1,0:T(8,128)(2,1)}, u32[]{:S(2)}, u32[]{:S(2)}) collective-permute-start(bf16[384,128]{1,0:T(8,128)(2,1)} %get-tuple-element.93), channel_id=1, source_target_pairs={{0,4},{2,6},{4,7},{6,5},{7,3},{5,1},{3,0},{1,2},{8,12},{10,14},{12... | collective-permute-start | bytes 294920 | tf_op jit(solution)/shard_map/ppermute | solution.py:206
  383.1 14.7 %collective-permute-start.135 = (f32[8,32]{1,0:T(8,128)S(1)}, f32[8,32]{1,0:T(8,128)S(1)}, u32[]{:S(2)}, u32[]{:S(2)}) collective-permute-start(f32[8,32]{1,0:T(8,128)S(1)} %get-tuple-element.124), channel_id=1, source_target_pairs={{0,24},{8,16},{16,8},{24,0},{1,25},{9,17},{17,9},{25,1},{2,26},{10... | collective-permute-start | bytes 3080 | tf_op jit(solution)/shard_map/ppermute | solution.py:209
  397.8 27.0 %collective-permute-start.76 = (bf16[384,128]{1,0:T(8,128)(2,1)}, bf16[384,128]{1,0:T(8,128)(2,1)S(1)}, u32[]{:S(2)}, u32[]{:S(2)}) collective-permute-start(bf16[384,128]{1,0:T(8,128)(2,1)} %get-tuple-element.92), channel_id=1, source_target_pairs={{0,6},{2,7},{4,5},{6,3},{7,1},{5,0},{3,2},{1,4},{8,14},{10,15},{12... | collective-permute-start | bytes 294920 | tf_op jit(solution)/shard_map/ppermute | solution.py:206
  424.8 94.0 %collective-permute-start.97 = (bf16[1024,2,256]{2,0,1:T(8,128)(2,1)}, bf16[1024,2,256]{2,0,1:T(8,128)(2,1)S(1)}, u32[]{:S(2)}, u32[]{:S(2)}) collective-permute-start(bf16[1024,2,256]{2,0,1:T(8,128)(2,1)} %bitcast.313), channel_id=1, source_target_pairs={{0,8},{8,0},{16,24},{24,16},{1,9},{9,1},{17,25},{25,17},{2,10},{10... | collective-permute-start | bytes 3145736 | tf_op jit(solution)/shard_map/ppermute | solution.py:209
  424.9 59.5 %collective-permute-start.110 = (bf16[3,64,1024]{2,1,0:T(8,128)(2,1)}, bf16[3,64,1024]{2,1,0:T(8,128)(2,1)S(1)}, u32[]{:S(2)}, u32[]{:S(2)}) collective-permute-start(bf16[3,64,1024]{2,1,0:T(8,128)(2,1)} %get-tuple-element.57), channel_id=1, source_target_pairs={{0,1},{2,0},{4,2},{6,4},{7,6},{5,7},{3,5},{1,3},{8,9},{10,8},{12,1... | collective-permute-start | bytes 1179656 | tf_op jit(solution)/shard_map/ppermute | solution.py:206
  425.6 61.6 %collective-permute-start.116 = (bf16[3,64,1024]{2,1,0:T(8,128)(2,1)}, bf16[3,64,1024]{2,1,0:T(8,128)(2,1)S(1)}, u32[]{:S(2)}, u32[]{:S(2)}) collective-permute-start(bf16[3,64,1024]{2,1,0:T(8,128)(2,1)} %get-tuple-element.58), channel_id=1, source_target_pairs={{0,2},{2,4},{4,6},{6,7},{7,5},{5,3},{3,1},{1,0},{8,10},{10,12},{12... | collective-permute-start | bytes 1179656 | tf_op jit(solution)/shard_map/ppermute | solution.py:206
  488.5 17.3 %collective-permute-start.111 = (bf16[3,64,1024]{2,1,0:T(8,128)(2,1)S(1)}, bf16[3,64,1024]{2,1,0:T(8,128)(2,1)S(1)}, u32[]{:S(2)}, u32[]{:S(2)}) collective-permute-start(bf16[3,64,1024]{2,1,0:T(8,128)(2,1)S(1)} %get-tuple-element.55), channel_id=1, source_target_pairs={{0,1},{2,0},{4,2},{6,4},{7,6},{5,7},{3,5},{1,3},{8,9},{10,8},{12,1... | collective-permute-start | bytes 1179656 | tf_op jit(solution)/shard_map/ppermute | solution.py:206
  488.6 17.2 %collective-permute-start.117 = (bf16[3,64,1024]{2,1,0:T(8,128)(2,1)S(1)}, bf16[3,64,1024]{2,1,0:T(8,128)(2,1)S(1)}, u32[]{:S(2)}, u32[]{:S(2)}) collective-permute-start(bf16[3,64,1024]{2,1,0:T(8,128)(2,1)S(1)} %get-tuple-element.56), channel_id=1, source_target_pairs={{0,2},{2,4},{4,6},{6,7},{7,5},{5,3},{3,1},{1,0},{8,10},{10,12},{12... | collective-permute-start | bytes 1179656 | tf_op jit(solution)/shard_map/ppermute | solution.py:206
  497.3 16.5 %collective-permute-start.82 = (bf16[192,1024]{1,0:T(8,128)(2,1)S(1)}, bf16[192,1024]{1,0:T(8,128)(2,1)S(1)}, u32[]{:S(2)}, u32[]{:S(2)}) collective-permute-start(bf16[192,1024]{1,0:T(8,128)(2,1)S(1)} %get-tuple-element.75), channel_id=1, source_target_pairs={{0,1},{2,0},{4,2},{6,4},{7,6},{5,7},{3,5},{1,3},{8,9},{10,8},{12,1... | collective-permute-start | bytes 1179656 | tf_op jit(solution)/shard_map/ppermute | solution.py:206
  507.4 16.6 %collective-permute-start.118 = (bf16[3,64,1024]{2,1,0:T(8,128)(2,1)S(1)}, bf16[3,64,1024]{2,1,0:T(8,128)(2,1)S(1)}, u32[]{:S(2)}, u32[]{:S(2)}) collective-permute-start(bf16[3,64,1024]{2,1,0:T(8,128)(2,1)S(1)} %get-tuple-element.54), channel_id=1, source_target_pairs={{0,2},{2,4},{4,6},{6,7},{7,5},{5,3},{3,1},{1,0},{8,10},{10,12},{12... | collective-permute-start | bytes 1179656 | tf_op jit(solution)/shard_map/ppermute | solution.py:206
  509.0 18.5 %collective-permute-start.112 = (bf16[3,64,1024]{2,1,0:T(8,128)(2,1)S(1)}, bf16[3,64,1024]{2,1,0:T(8,128)(2,1)}, u32[]{:S(2)}, u32[]{:S(2)}) collective-permute-start(bf16[3,64,1024]{2,1,0:T(8,128)(2,1)S(1)} %get-tuple-element.53), channel_id=1, source_target_pairs={{0,1},{2,0},{4,2},{6,4},{7,6},{5,7},{3,5},{1,3},{8,9},{10,8},{12,1... | collective-permute-start | bytes 1179656 | tf_op jit(solution)/shard_map/ppermute | solution.py:206
  516.8 15.8 %collective-permute-start.90 = (bf16[192,1024]{1,0:T(8,128)(2,1)}, bf16[192,1024]{1,0:T(8,128)(2,1)}, u32[]{:S(2)}, u32[]{:S(2)}) collective-permute-start(bf16[192,1024]{1,0:T(8,128)(2,1)} %get-tuple-element.74), channel_id=1, source_target_pairs={{0,2},{2,4},{4,6},{6,7},{7,5},{5,3},{3,1},{1,0},{8,10},{10,12},{12... | collective-permute-start | bytes 1179656 | tf_op jit(solution)/shard_map/ppermute | solution.py:206
  521.2 15.9 %collective-permute-start.98 = (bf16[1024,1,256]{2,0,1:T(8,128)(2,1)}, bf16[1024,1,256]{2,0,1:T(8,128)(2,1)}, u32[]{:S(2)}, u32[]{:S(2)}) collective-permute-start(bf16[1024,1,256]{2,0,1:T(8,128)(2,1)} %dynamic-slice_convert_fusion), channel_id=1, source_target_pairs={{0,16},{8,24},{16,0},{24,8},{1,17},{9,25},{17,1},{25,9},{2,18},{10... | collective-permute-start | bytes 1572872 | tf_op jit(solution)/shard_map/ppermute | solution.py:209
  525.9 15.9 %collective-permute-start.119 = (bf16[3,64,1024]{2,1,0:T(8,128)(2,1)}, bf16[3,64,1024]{2,1,0:T(8,128)(2,1)}, u32[]{:S(2)}, u32[]{:S(2)}) collective-permute-start(bf16[3,64,1024]{2,1,0:T(8,128)(2,1)} %fusion.16), channel_id=1, source_target_pairs={{0,2},{2,4},{4,6},{6,7},{7,5},{5,3},{3,1},{1,0},{8,10},{10,12},{12... | collective-permute-start | bytes 1179656 | tf_op jit(solution)/shard_map/ppermute | solution.py:206
  535.1 14.5 %collective-permute-start.91 = (bf16[192,1024]{1,0:T(8,128)(2,1)}, bf16[192,1024]{1,0:T(8,128)(2,1)}, u32[]{:S(2)}, u32[]{:S(2)}) collective-permute-start(bf16[192,1024]{1,0:T(8,128)(2,1)} %get-tuple-element.72), channel_id=1, source_target_pairs={{0,2},{2,4},{4,6},{6,7},{7,5},{5,3},{3,1},{1,0},{8,10},{10,12},{12... | collective-permute-start | bytes 1179656 | tf_op jit(solution)/shard_map/ppermute | solution.py:206
  539.2 17.6 %collective-permute-start.104 = (bf16[128,256]{1,0:T(8,128)(2,1)}, bf16[128,256]{1,0:T(8,128)(2,1)}, u32[]{:S(2)}, u32[]{:S(2)}) collective-permute-start(bf16[128,256]{1,0:T(8,128)(2,1)} %get-tuple-element.113), channel_id=1, source_target_pairs={{0,3},{2,1},{4,0},{6,2},{7,4},{5,6},{3,7},{1,5},{8,11},{10,9},{12,... | collective-permute-start | bytes 196616 | tf_op jit(solution)/shard_map/ppermute | solution.py:206
  541.8 15.5 %collective-permute-start.103 = (bf16[128,256]{1,0:T(8,128)(2,1)S(1)}, bf16[128,256]{1,0:T(8,128)(2,1)}, u32[]{:S(2)}, u32[]{:S(2)}) collective-permute-start(bf16[128,256]{1,0:T(8,128)(2,1)S(1)} %get-tuple-element.114), channel_id=1, source_target_pairs={{0,5},{2,3},{4,1},{6,0},{7,2},{5,4},{3,6},{1,7},{8,13},{10,11},{12... | collective-permute-start | bytes 196616 | tf_op jit(solution)/shard_map/ppermute | solution.py:206
  552.2 20.9 %collective-permute-start.85 = (bf16[192,1024]{1,0:T(8,128)(2,1)}, bf16[192,1024]{1,0:T(8,128)(2,1)}, u32[]{:S(2)}, u32[]{:S(2)}) collective-permute-start(bf16[192,1024]{1,0:T(8,128)(2,1)} %get-tuple-element.69), channel_id=1, source_target_pairs={{0,1},{2,0},{4,2},{6,4},{7,6},{5,7},{3,5},{1,3},{8,9},{10,8},{12,1... | collective-permute-start | bytes 1179656 | tf_op jit(solution)/shard_map/ppermute | solution.py:206
  552.6 20.4 %collective-permute-start.92 = (bf16[192,1024]{1,0:T(8,128)(2,1)}, bf16[192,1024]{1,0:T(8,128)(2,1)}, u32[]{:S(2)}, u32[]{:S(2)}) collective-permute-start(bf16[192,1024]{1,0:T(8,128)(2,1)} %get-tuple-element.70), channel_id=1, source_target_pairs={{0,2},{2,4},{4,6},{6,7},{7,5},{5,3},{3,1},{1,0},{8,10},{10,12},{12... | collective-permute-start | bytes 1179656 | tf_op jit(solution)/shard_map/ppermute | solution.py:206
  569.5 21.5 %collective-permute-start.122 = (bf16[3,1,128,256]{3,2,0,1:T(8,128)(2,1)S(1)}, bf16[3,1,128,256]{3,2,0,1:T(8,128)(2,1)S(1)}, u32[]{:S(2)}, u32[]{:S(2)}) collective-permute-start(bf16[3,1,128,256]{3,2,0,1:T(8,128)(2,1)S(1)} %bitcast.324), channel_id=1, source_target_pairs={{0,24},{8,16},{16,8},{24,0},{1,25},{9,17},{17,9},{25,1},{2,26},{10... | collective-permute-start | bytes 589832 | tf_op jit(solution)/shard_map/ppermute | solution.py:209
  (128 other events, 1144.9 us)

commit v2 on v1

v2 whole, which is shorter than its diff:
```python
import functools

import jax
import jax.numpy as jnp
from jax import lax
from jax.experimental import pallas as pl
from jax.experimental.pallas import tpu as pltpu
from jax.sharding import PartitionSpec as P

DH = 64
BLK = 256
EPS = 1e-06
HT = 256
BULK_AT = 5
WEIGHTS_AT = 3
RS_LATE = True
NT = (((1,), (1,)), ((), ()))
NN = (((1,), (0,)), ((), ()))
TN = (((0,), (0,)), ((), ()))


def dot(a, b, dims):
    return lax.dot_general(a, b, dims, preferred_element_type=jnp.float32)


def split_heads(block):
    low = lax.broadcasted_iota(jnp.int32, block.shape, 1) < DH
    zero = jnp.zeros_like(block)
    return jnp.concatenate([jnp.where(low, block, zero), jnp.where(low, zero, block)], axis=0)


def scaled_q(qkv_ref, rows):
    return split_heads((qkv_ref[rows, 0:128].astype(jnp.float32) * DH ** -0.5).astype(jnp.bfloat16))


def in_pairs(first, last, ahead, work):
    count = last - first + 1
    ahead(first, 0)

    def pair(p, _):
        j = first + 2 * p
        ahead(j + 1, 1)
        work(j, 0)
        ahead(jnp.minimum(j + 2, last), 0)
        work(j + 1, 1)
        return 0

    lax.fori_loop(0, count // 2, pair, 0)

    @pl.when(count % 2 == 1)
    def _():
        work(last, 0)


def attn_fwd_kernel(first_ref, qkv_ref, out_ref, log_ref, vt_ref, top_ref, sum_ref, acc_ref, qt_ref, *score_refs):
    i = pl.program_id(0)
    @pl.when(i == 0)
    def _():
        vt_ref[...] = jnp.transpose(qkv_ref[:, 256:384])
    rows = pl.ds(pl.multiple_of(i * BLK, BLK), BLK)
    qt_ref[...] = jnp.transpose(scaled_q(qkv_ref, rows))
    top_ref[...] = jnp.full_like(top_ref, -1e30)
    sum_ref[...] = jnp.zeros_like(sum_ref)
    acc_ref[...] = jnp.zeros_like(acc_ref)

    def ahead(j, slot):
        at = pl.ds(pl.multiple_of(j * BLK, BLK), BLK)
        score_refs[slot][...] = dot(qkv_ref[at, 128:256], qt_ref[...], NN)

    def work(j, slot):
        at = pl.ds(pl.multiple_of(j * BLK, BLK), BLK)
        scores = score_refs[slot][...]
        old = top_ref[...]
        new = jnp.maximum(old, jnp.max(scores, axis=0, keepdims=True))
        top_ref[...] = new
        weights = jnp.exp(scores - new)
        shrink = jnp.exp(old - new)
        sum_ref[...] = sum_ref[...] * shrink + jnp.sum(weights, axis=0, keepdims=True)
        probs = weights.astype(jnp.bfloat16)
        acc_ref[:, 0:BLK] = acc_ref[:, 0:BLK] * shrink[:, 0:BLK] + dot(vt_ref[0:DH, at], probs[:, 0:BLK], NN)
        acc_ref[:, BLK:] = acc_ref[:, BLK:] * shrink[:, BLK:] + dot(vt_ref[DH:, at], probs[:, BLK:], NN)

    in_pairs(first_ref[i], i, ahead, work)
    mixed = acc_ref[...] / sum_ref[...]
    out_ref[...] = jnp.transpose(jnp.concatenate([mixed[:, 0:BLK], mixed[:, BLK:]], axis=0)).astype(jnp.bfloat16)
    log_ref[0] = top_ref[...] + jnp.log(sum_ref[...])


def attn_fwd(qkv, first):
    rows = qkv.shape[0]
    n = rows // BLK
    f32 = jnp.float32
    return pl.pallas_call(
        attn_fwd_kernel, name="attn_fwd",
        out_shape=(jax.ShapeDtypeStruct((rows,128),jnp.bfloat16), jax.ShapeDtypeStruct((n,1,2*BLK),f32)),
        grid_spec=pltpu.PrefetchScalarGridSpec(
            num_scalar_prefetch=1, grid=(n,),
            in_specs=[pl.BlockSpec((rows,384), lambda i,s:(0,0))],
            out_specs=[pl.BlockSpec((BLK,128), lambda i,s:(i,0)), pl.BlockSpec((1,1,2*BLK), lambda i,s:(i,0,0))],
            scratch_shapes=[pltpu.VMEM((128,rows),jnp.bfloat16), pltpu.VMEM((1,2*BLK),f32), pltpu.VMEM((1,2*BLK),f32), pltpu.VMEM((DH,2*BLK),f32),pltpu.VMEM((128,2*BLK),jnp.bfloat16)]+[pltpu.VMEM((BLK,2*BLK),f32)]*2),
        compiler_params=pltpu.CompilerParams(vmem_limit_bytes=32<<20),
        cost_estimate=pl.CostEstimate(flops=10*10**9, bytes_accessed=5*10**6, transcendentals=10**7),
    )(first, qkv)


def attn_bwd_kernel(first_ref, qkv_ref, do_ref, o_ref, log_ref, out_ref, kt_ref, dk_ref, dv_ref, dq_ref, qt_ref, gt_ref, *score_refs):
    i = pl.program_id(0)
    @pl.when(i == 0)
    def _():
        kt_ref[...] = jnp.transpose(qkv_ref[:, 128:256])
        dk_ref[...] = jnp.zeros_like(dk_ref)
        dv_ref[...] = jnp.zeros_like(dv_ref)
    rows = pl.ds(pl.multiple_of(i * BLK, BLK), BLK)
    both = scaled_q(qkv_ref, rows)
    grads = split_heads(do_ref[...])
    logs = log_ref[0]
    qt_ref[...] = jnp.transpose(both)
    turned = jnp.transpose(grads)
    gt_ref[...] = turned
    outs = jnp.transpose(o_ref[...]).astype(jnp.float32)
    delta = jnp.sum(turned.astype(jnp.float32) * jnp.concatenate([outs, outs], axis=1), axis=0, keepdims=True)
    dq_ref[...] = jnp.zeros_like(dq_ref)

    def ahead(j, slot):
        at = pl.ds(pl.multiple_of(j * BLK, BLK), BLK)
        score_refs[slot][...] = dot(qkv_ref[at, 128:256], qt_ref[...], NN)
        score_refs[2 + slot][...] = dot(qkv_ref[at, 256:384], gt_ref[...], NN)

    def work(j, slot):
        at = pl.ds(pl.multiple_of(j * BLK, BLK), BLK)
        probs = jnp.exp(score_refs[slot][...] - logs)
        ds = (probs * (score_refs[2 + slot][...] - delta)).astype(jnp.bfloat16)
        dv_ref[at, :] += dot(probs.astype(jnp.bfloat16), grads, NN)
        dk_ref[at, :] += dot(ds, both, NN)
        dq_ref[:, 0:BLK] += dot(kt_ref[0:DH, at], ds[:, 0:BLK], NN)
        dq_ref[:, BLK:] += dot(kt_ref[DH:, at], ds[:, BLK:], NN)

    in_pairs(first_ref[i], i, ahead, work)
    dq = jnp.concatenate([dq_ref[:, 0:BLK], dq_ref[:, BLK:]], axis=0)
    out_ref[rows, 0:128] = (jnp.transpose(dq) * DH ** -0.5).astype(jnp.bfloat16)

    @pl.when(i == pl.num_programs(0) - 1)
    def _():
        out_ref[:, 128:256] = dk_ref[...].astype(jnp.bfloat16)
        out_ref[:, 256:384] = dv_ref[...].astype(jnp.bfloat16)


def attn_bwd(qkv, do, o, log, first):
    rows = qkv.shape[0]
    n = rows // BLK
    f32 = jnp.float32
    blk = pl.BlockSpec((BLK,128), lambda i,s:(i,0))
    return pl.pallas_call(
        attn_bwd_kernel, name="attn_bwd",
        out_shape=jax.ShapeDtypeStruct((rows,384),jnp.bfloat16),
        grid_spec=pltpu.PrefetchScalarGridSpec(
            num_scalar_prefetch=1, grid=(n,),
            in_specs=[pl.BlockSpec((rows,384), lambda i,s:(0,0)), blk, blk, pl.BlockSpec((1,1,2*BLK), lambda i,s:(i,0,0))],
            out_specs=pl.BlockSpec((rows,384), lambda i,s:(0,0)),
            scratch_shapes=[pltpu.VMEM((128,rows),jnp.bfloat16), pltpu.VMEM((rows,128),f32), pltpu.VMEM((rows,128),f32), pltpu.VMEM((DH,2*BLK),f32)]+[pltpu.VMEM((128,2*BLK),jnp.bfloat16)]*2+[pltpu.VMEM((BLK,2*BLK),f32)]*4),
        compiler_params=pltpu.CompilerParams(vmem_limit_bytes=40<<20),
        cost_estimate=pl.CostEstimate(flops=26*10**9, bytes_accessed=9*10**6, transcendentals=10**7),
    )(first, qkv, do, o, log)


def ffn_kernel(n_ref, c_ref, gate_ref, up_ref, down_ref, f_ref, d_ref, z_ref, g_ref, u_ref):
    n2, c = n_ref[0], c_ref[0]
    wg, wu, wd = (ref[...].reshape(-1, n2.shape[1]) for ref in (gate_ref, up_ref, down_ref))
    gate, up, dz = dot(n2, wg, NT), dot(n2, wu, NT), dot(c, wd, NT)
    sig = jax.nn.sigmoid(gate)
    silu = gate * sig
    z = (silu * up).astype(jnp.bfloat16)
    dg = (dz * up * (sig * (1.0 + gate * (1.0 - sig)))).astype(jnp.bfloat16)
    du = (dz * silu).astype(jnp.bfloat16)
    z_ref[0] = z
    g_ref[0] = dg
    u_ref[0] = du
    f_ref[0] = dot(z, wd, NN).astype(jnp.bfloat16)
    d_ref[0] = (dot(dg, wg, NN) + dot(du, wu, NN)).astype(jnp.bfloat16)


def ffn(n2, c, weights, hid):
    nb, rows, width = n2.shape
    n_t = weights.shape[0]
    total = n_t * hid
    bf = jnp.bfloat16
    full = pl.BlockSpec((1, rows, width), lambda s: (s, 0, 0))
    col = pl.BlockSpec((1, rows, total), lambda s: (s, 0, 0))
    kinds = [
        pl.BlockSpec(
            (n_t, hid, width),
            functools.partial(lambda which, s: (0, which, 0), which),
            pipeline_mode=pl.Buffered(1),
        )
        for which in range(3)
    ]
    return pl.pallas_call(
        ffn_kernel,
        name="ffn",
        grid=(nb,),
        out_shape=[jax.ShapeDtypeStruct((nb, rows, width), bf)] * 2
        + [jax.ShapeDtypeStruct((nb, rows, total), bf)] * 3,
        in_specs=[full] * 2 + kinds,
        out_specs=[full] * 2 + [col] * 3,
        compiler_params=pltpu.CompilerParams(vmem_limit_bytes=56 << 20),
        cost_estimate=pl.CostEstimate(
            flops=2 * nb * rows * width * total * 6,
            bytes_accessed=20 * 10**6,
            transcendentals=nb * rows * total,
        ),
    )(n2, c, weights, weights, weights)


def ffn_grad_kernel(nb, *refs):
    ns, cs, zs, gs, us = (refs[k * nb : (k + 1) * nb] for k in range(5))
    out = refs[5 * nb]
    pieces, rows, width = out.shape
    hid = rows // 3
    for which, (left, right) in enumerate(((gs, ns), (us, ns), (zs, cs))):
        total = dot(left[0][...], right[0][...], TN)
        for b in range(1, nb):
            total += dot(left[b][...], right[b][...], TN)
        out[:, which * hid : (which + 1) * hid] = total.astype(jnp.bfloat16).reshape(pieces, hid, width)


def ffn_grad(ns, cs, zs, gs, us, n_t):
    nb = len(ns)
    width = ns[0].shape[1]
    total = zs[0].shape[1]
    hid = total // n_t
    rows = sum(n.shape[0] for n in ns)
    full = [pl.BlockSpec(n.shape, lambda s: (0, 0)) for n in ns]
    col = [pl.BlockSpec((n.shape[0], HT), lambda s: (0, s)) for n in ns]
    return pl.pallas_call(
        functools.partial(ffn_grad_kernel, nb),
        name="ffn_grad",
        grid=(total // HT,),
        out_shape=jax.ShapeDtypeStruct((n_t, 3 * hid, width), jnp.bfloat16),
        in_specs=full * 2 + col * 3,
        out_specs=pl.BlockSpec((HT // hid, 3 * hid, width), lambda s: (s, 0, 0)),
        compiler_params=pltpu.CompilerParams(vmem_limit_bytes=56 << 20),
        cost_estimate=pl.CostEstimate(
            flops=2 * rows * width * total * 3, bytes_accessed=20 * 10**6, transcendentals=0
        ),
    )(*ns, *cs, *zs, *gs, *us)


def late_kernel(near, order_ref, gq_ref, all_ref, w_ref, gains_ref, heads_ref, gm_ref, keep_ref, send_ref):
    wide = gq_ref.shape[1]
    grads = dot(gq_ref[...], all_ref[...], TN)
    first = jnp.sum(grads * w_ref[...].astype(jnp.float32), axis=0, keepdims=True) / gains_ref[0:1]
    row = lax.broadcasted_iota(jnp.int32, (16, first.shape[1]), 0)
    gains = jnp.where(row == 0, first, jnp.where(row == 1, gains_ref[1:2], 0.0))
    outs = dot(heads_ref[...], gm_ref[...], TN)
    step = pl.program_id(0)

    def write(ref, kind):
        ref[0:wide] = grads.astype(kind)
        ref[wide : wide + 16] = gains.astype(kind)
        ref[wide + 16 :] = outs.astype(kind)

    @pl.when(step < near)
    def _():
        write(keep_ref, jnp.float32)

    @pl.when(step >= near)
    def _():
        write(send_ref, jnp.bfloat16)


def late_grads(order, grad_qkv, all1, w_qkv, gains, heads_own, grad_bf):
    n = order.shape[0]
    near = n // 2
    width = all1.shape[1]
    part = width // n
    whole = lambda x: pl.BlockSpec(x.shape, lambda i, o: (0, 0))
    block = lambda x: pl.BlockSpec((x.shape[0], part), lambda i, o: (0, o[i]))
    total = grad_qkv.shape[1] + 16 + heads_own.shape[1]
    return pl.pallas_call(
        functools.partial(late_kernel, near),
        name="late_grads",
        out_shape=(
            jax.ShapeDtypeStruct((total, near * part), jnp.float32),
            jax.ShapeDtypeStruct((total, near * part), jnp.bfloat16),
        ),
        grid_spec=pltpu.PrefetchScalarGridSpec(
            num_scalar_prefetch=1,
            grid=(n,),
            in_specs=[whole(grad_qkv), block(all1), block(w_qkv), block(gains), whole(heads_own), block(grad_bf)],
            out_specs=[
                pl.BlockSpec((total, part), lambda i, o: (0, jnp.minimum(i, near - 1))),
                pl.BlockSpec((total, part), lambda i, o: (0, jnp.maximum(i - near, 0))),
            ],
        ),
        compiler_params=pltpu.CompilerParams(vmem_limit_bytes=40 << 20),
        cost_estimate=pl.CostEstimate(flops=4 * 10**9, bytes_accessed=14 * 10**6, transcendentals=0),
    )(order, grad_qkv, all1, w_qkv, gains, heads_own, grad_bf)


def blank(shape, dtype):
    return pl.pallas_call(
        lambda out_ref: None,
        name="blank",
        out_shape=jax.ShapeDtypeStruct(shape, dtype),
        out_specs=pl.BlockSpec(memory_space=pl.ANY),
    )()


def row_scale(values):
    return lax.rsqrt(jnp.mean(values * values, axis=-1, keepdims=True) + EPS)


def norm_back(grad_normed, values, scale, gain):
    weighted = grad_normed * gain
    inner = jnp.mean(weighted * values, axis=-1, keepdims=True)
    return scale * weighted - values * (scale * scale * scale) * inner


def after(value, *others):
    return lax.optimization_barrier((value,) + others)[0]


def make(n_dp, n_t):
    ring = list(range(0, n_t, 2)) + list(range(n_t - 1, 0, -2))
    bf = jnp.bfloat16
    f32 = jnp.float32

    def hop(value, k):
        return lax.ppermute(value, "tensor", [(ring[i], ring[(i + k) % n_t]) for i in range(n_t)])

    def flip(value, k):
        return lax.ppermute(value, "dp", [(i, i ^ k) for i in range(n_dp)])

    def flip_t(value, k):
        return lax.ppermute(value, "tensor", [(i, i ^ k) for i in range(n_t)])

    bits = [1 << b for b in range(n_dp.bit_length() - 1)]
    t_bits = [1 << b for b in range(n_t.bit_length() - 2, -1, -1)]
    n_ff = min(n_dp, 4)
    ff_bits = [b for b in bits if b < n_ff]
    put = lax.dynamic_update_slice_in_dim
    take = lax.dynamic_slice_in_dim

    def pick(value, index, axis):
        return lax.dynamic_index_in_dim(value, index, axis, keepdims=False)

    dp_order = [0]
    for bit in bits[::-1]:
        dp_order = dp_order + [k ^ bit for k in dp_order]

    def arrange(value, me):
        size = value.shape[-1] // n_dp
        axis = value.ndim - 1
        return jnp.concatenate([take(value, (me ^ k) * size, size, axis) for k in dp_order], axis=axis)

    def scatter_sum_dp(arranged, send_type):
        for bit in bits:
            cut = arranged.shape[-1] // 2
            arranged = arranged[..., :cut] + flip(arranged[..., cut:].astype(send_type), bit).astype(f32)
        return arranged

    def scatter_sum_t(value, t, send_type):
        for bit in t_bits:
            halves = value.reshape((2, -1) + value.shape[1:])
            side = (t // bit) % 2
            value = pick(halves, side, 0) + flip_t(pick(halves, 1 - side, 0).astype(send_type), bit).astype(f32)
        return value[0]

    def on_device(
        tokens, seq_ids, blk_ids, norm1_gain, w_query, w_key, w_value, w_out, norm2_gain,
        w_gate, w_up, w_down, cotangent,
    ):
        d = lax.axis_index("dp")
        t = lax.axis_index("tensor")
        half_t = n_t // 2
        pos = jnp.where(t % 2 == 0, t // 2, n_t - 1 - t // 2)

        def owner(p):
            p = lax.rem(p + 2 * n_t, n_t)
            return jnp.where(p < half_t, 2 * p, 2 * (n_t - 1 - p) + 1)

        ahead = [owner(pos + j) for j in range(n_t)]
        behind = [owner(pos - j) for j in range(n_t)]
        own_rows, width = tokens.shape
        rows = own_rows * n_t
        half = own_rows // 2
        part = width // n_dp
        wide = w_query.shape[1]

        one, two = [tokens[:half]], [tokens[half:]]
        for k in range(1, n_t):
            one.append(hop(one[-1], 1))
            two.append(hop(two[-1], -1))

        def gather_dp(piece):
            whole = put(jnp.zeros((piece.shape[0], width), bf), piece, d * part, 1)
            for k in range(1, n_dp):
                whole = put(whole, flip(piece, k), (d ^ k) * part, 1)
            return whole

        common = gather_dp(
            jnp.concatenate(
                [
                    jnp.concatenate([w_query, w_key, w_value], axis=1).T,
                    norm1_gain[None],
                    norm2_gain[None],
                    jnp.zeros((14, part), bf),
                ]
            )
        )
        w_qkv = common[: 3 * wide]
        gains = common[3 * wide :].astype(f32)
        gain1, gain2 = gains[0:1], gains[1:2]

        hid_t = w_down.shape[0]
        hid = hid_t // n_ff
        out_half = wide // 2
        core = d % 2
        shards = jnp.concatenate(
            [
                w_gate.T.reshape(n_ff, hid, part),
                w_up.T.reshape(n_ff, hid, part),
                w_down.reshape(n_ff, hid, part),
                jnp.tile(w_out.reshape(2, out_half, part), (n_ff // 2, 1, 1)),
            ],
            axis=1,
        )
        shards = after(shards, one[1])
        pieces = [pick(shards, (d ^ k) % n_ff, 0) for k in range(n_dp)]
        pieces = [flip(piece, k) if k else piece for k, piece in enumerate(pieces)]
        pieces = lax.optimization_barrier((*pieces, one[WEIGHTS_AT], two[WEIGHTS_AT]))[:n_dp]
        own_w = jnp.zeros((3 * hid + out_half, width), bf)
        for k in range(n_dp):
            own_w = put(own_w, pieces[k], (d ^ k) * part, 1)
        own_o = own_w[3 * hid :]
        own_w = after(own_w[: 3 * hid], one[BULK_AT], two[BULK_AT])

        cot_far = cotangent[None]
        for bit in ff_bits[:0:-1]:
            cot_far = jnp.concatenate([cot_far, flip(after(cot_far, one[2]), bit)])

        resid = tokens.astype(f32)
        scale1 = row_scale(resid)

        def normed(piece):
            value = piece.astype(f32)
            return (value * row_scale(value) * gain1).astype(bf)

        def project(piece):
            return lax.dot_general(piece, w_qkv, NT, preferred_element_type=f32).astype(bf)

        mine = normed(tokens)
        all1 = put(blank((rows, width), bf), mine, t * own_rows, 0)
        qkv = put(blank((rows, 3 * wide), bf), project(mine), t * own_rows, 0)
        for k in range(1, n_t):
            both = normed(jnp.concatenate([one[k], two[k]]))
            made = project(both)
            all1 = put(all1, both[:half], behind[k] * own_rows, 0)
            all1 = put(all1, both[half:], ahead[k] * own_rows + half, 0)
            qkv = put(qkv, made[:half], behind[k] * own_rows, 0)
            qkv = put(qkv, made[half:], ahead[k] * own_rows + half, 0)

        o_mine = lax.all_gather(own_o, "tensor", axis=0)
        weights = lax.all_gather(own_w, "tensor", axis=0)
        o_mine = after(o_mine, qkv)
        o_peer = flip(o_mine, 1)
        out_full = jnp.where(
            core == 0,
            jnp.concatenate([o_mine, o_peer], axis=1),
            jnp.concatenate([o_peer, o_mine], axis=1),
        ).reshape(n_t * wide, width)
        cot_far = after(cot_far, qkv)
        c_near = jnp.concatenate([cotangent[None], flip(cot_far[:1], 1)])
        c_far = jnp.concatenate([cot_far[1:], flip(cot_far[1:], 1)])

        units = seq_ids.reshape(-1, 4 * BLK)[:, 0]
        n_units = rows // (4 * BLK)
        same = units[:, None] == units[None, :]
        first_unit = jnp.min(jnp.where(same, jnp.arange(n_units)[None, :], n_units), axis=1)
        first = jnp.repeat(first_unit * 4, 4).astype(jnp.int32)
        attended, logs = attn_fwd(qkv, first)

        heads_own = put(
            blank((own_rows, n_t * wide), bf), take(attended, t * own_rows, own_rows, 0), t * wide, 1
        )
        for j in range(1, n_t):
            piece = hop(take(attended, behind[j] * own_rows, own_rows, 0), -j)
            heads_own = put(heads_own, piece, ahead[j] * wide, 1)
        mixed = resid + jnp.dot(heads_own, out_full, preferred_element_type=f32)
        scale2 = row_scale(mixed)
        normed2 = (mixed * scale2 * gain2).astype(bf)

        n_far = normed2[None]
        for bit in ff_bits[:0:-1]:
            n_far = jnp.concatenate([n_far, flip(n_far, bit)])
        n_near = jnp.concatenate([normed2[None], flip(normed2[None], 1)])
        f_near, d_near, z_near, g_near, u_near = ffn(n_near, c_near, weights, hid)
        n_far = after(n_far[1:], d_near)
        n_far = jnp.concatenate([n_far, flip(n_far, 1)])
        f_far, d_far, z_far, g_far, u_far = ffn(n_far, c_far, weights, hid)

        def fold_core(near, far):
            cut = far.shape[0] // 2
            far_sum = far[:cut].astype(f32) + flip(far[cut:], 1).astype(f32)
            near_sum = near[:1].astype(f32) + flip(near[1:], 1).astype(f32)
            return jnp.concatenate([near_sum, far_sum])

        def fold_far(acc, *late):
            for bit in ff_bits[1:]:
                cut = acc.shape[0] // 2
                got = flip(acc[cut:].astype(bf), bit)
                acc = acc[:cut] + (after(got, *late) if bit == ff_bits[-1] else got).astype(f32)
            return acc[0]

        grad_w = ffn_grad(
            [n_near.reshape(-1, width), n_far.reshape(-1, width)],
            [c_near.reshape(-1, width), c_far.reshape(-1, width)],
            [z.reshape(-1, z.shape[-1]) for z in (z_near, z_far)],
            [g.reshape(-1, g.shape[-1]) for g in (g_near, g_far)],
            [u.reshape(-1, u.shape[-1]) for u in (u_near, u_far)],
            n_t,
        )
        grad_normed2 = fold_far(fold_core(d_near, d_far), grad_w)

        cot = cotangent.astype(f32)
        grad_mixed = cot + norm_back(grad_normed2, mixed, scale2, gain2)
        grad_bf = grad_mixed.astype(bf)
        grad_heads = lax.dot_general(grad_bf, out_full, NT, preferred_element_type=f32).astype(bf)
        grad_att = put(
            blank((rows, wide), bf), take(grad_heads, t * wide, wide, 1), t * own_rows, 0
        )
        for j in range(1, n_t):
            piece = hop(take(grad_heads, ahead[j] * wide, wide, 1), j)
            grad_att = put(grad_att, piece, behind[j] * own_rows, 0)
        f_folded = after(fold_core(f_near, f_far), grad_heads)
        grad_qkv = attn_bwd(qkv, grad_att, attended, logs, first)
        output = (mixed + fold_far(f_folded, grad_qkv)).astype(bf)
        summed = lax.psum_scatter(
            (after(grad_w, grad_att) if RS_LATE else grad_w).reshape(-1, width),
            "tensor", scatter_dimension=0, tiled=True,
        )

        def back_rows(k):
            pair = jnp.concatenate(
                [
                    take(grad_qkv, behind[k] * own_rows, half, 0),
                    take(grad_qkv, ahead[k] * own_rows + half, half, 0),
                ]
            )
            made = jnp.dot(pair, w_qkv, preferred_element_type=f32)
            return lax.optimization_barrier(made.astype(bf))

        made = back_rows(n_t - 1)
        up, down = [made[:half]], [made[half:]]
        for k in range(n_t - 2, -1, -1):
            got_up, got_down = hop(up[-1], -1), hop(down[-1], 1)
            made = back_rows(k).astype(f32)
            up.append(got_up.astype(f32) + made[:half])
            down.append(got_down.astype(f32) + made[half:])
            if k:
                up[-1], down[-1] = up[-1].astype(bf), down[-1].astype(bf)
        grad_normed1 = jnp.concatenate([up[-1], down[-1]])
        input_grad = (grad_mixed + norm_back(grad_normed1, resid, scale1, gain1)).astype(bf)

        grad_gain2 = jnp.sum(grad_normed2 * mixed * scale2, axis=0, keepdims=True)
        gain_rows = jnp.concatenate([gain1, grad_gain2, jnp.zeros((6, width), f32)])
        if part % 128 == 0:
            order = jnp.stack([d ^ k for k in dp_order]).astype(jnp.int32)
            keep, send = late_grads(order, grad_qkv, all1, w_qkv, gain_rows, heads_own, grad_bf)
        else:
            grad_wqkv = lax.dot_general(grad_qkv, all1, TN, preferred_element_type=f32)
            grad_gain1 = jnp.sum(grad_wqkv * w_qkv.astype(f32), axis=0, keepdims=True) / gain1
            grad_wo = lax.dot_general(heads_own, grad_bf, TN, preferred_element_type=f32)
            gain_rows = jnp.concatenate([grad_gain1, grad_gain2, jnp.zeros((14, width), f32)])
            both = arrange(jnp.concatenate([grad_wqkv, gain_rows, grad_wo]), d)
            keep, send = both[:, : width // 2], both[:, width // 2 :].astype(bf)
        stage = 1
        for bit in bits:
            send = after(send, up[min(stage, n_t - 2)])
            got = after(flip(send, bit), up[min(stage + 1, n_t - 2)])
            stage += 1 if bit == 1 else 2
            keep = keep + got.astype(f32)
            cut = keep.shape[1] // 2
            if cut >= part:
                keep, send = keep[:, :cut], keep[:, cut:].astype(bf)
        grad_query, grad_key, grad_value = (keep[k * wide : (k + 1) * wide].T for k in range(3))
        gain_sums = jnp.broadcast_to(keep[3 * wide : 3 * wide + 16], (n_t, 16, part))
        parts = jnp.concatenate([keep[3 * wide + 16 :].reshape(n_t, wide, part), gain_sums], axis=1)
        mine = scatter_sum_t(parts, t, bf)
        grad_out = mine[:wide]
        share = part // n_t
        grad_norm1 = take(mine[wide], t * share, share, 0)
        grad_norm2 = take(mine[wide + 1], t * share, share, 0)

        summed = after(summed, up[2]).reshape(3, hid, n_dp, part)
        full = blank((3, n_ff, hid, part), f32)
        for k in range(n_ff):
            total = 0.0
            for far in range(k, n_dp, n_ff):
                piece = pick(summed, d ^ far, 2)[:, None]
                piece = after(flip(piece, far), up[5]) if far else piece
                total = total + piece.astype(f32)
            full = put(full, total, (d ^ k) % n_ff, 1)
        full = full.reshape(3, hid_t, part)

        return (
            output, input_grad, grad_query, grad_key, grad_value, grad_out,
            full[0].T, full[1].T, full[2], grad_norm1, grad_norm2,
        )

    return on_device


def solution(mesh):
    rows = P(("dp", "tensor"), None)
    return jax.shard_map(
        make(mesh.shape["dp"], mesh.shape["tensor"]),
        mesh=mesh,
        in_specs=(
            rows, P("dp"), P("dp"), P("dp"), P("dp", "tensor"), P("dp", "tensor"),
            P("dp", "tensor"), P("tensor", "dp"), P("dp"), P("dp", "tensor"),
            P("dp", "tensor"), P("tensor", "dp"), rows,
        ),
        out_specs=(
            rows, rows, P("dp", "tensor"), P("dp", "tensor"), P("dp", "tensor"),
            P("tensor", "dp"), P("dp", "tensor"), P("dp", "tensor"), P("tensor", "dp"),
            P(("dp", "tensor")), P(("dp", "tensor")),
        ),
        check_vma=False,
    )
```

time: 635 us -> 542 us (0.85)
  starting transfers between devices: 146 us -> 86.7 us
  between operations: 2.69 us -> 16.6 us
  local copies, waits for them, and re-layouts: 74.8 us -> 61.1 us
  Pallas kernels: 128 us -> 118 us
  waiting for transfers between devices: 201 us -> 191 us
  matrix products: 20.1 us -> 12.7 us
    ppermute x105 -> x42, starting transfers between devices: 131 us -> 67.9 us  [hop(): lax.ppermute(value, 'tensor', [(ring[i], ring[(i + k) % n_t]) for i in ra...]
    ppermute x38 -> x24, waiting for transfers between devices: 43 us -> 23 us  [flip(): return lax.ppermute(value, 'dp', [(i, i ^ k) for i in range(n_dp)])]
    ppermute x105 -> x42, waiting for transfers between devices: 158 us -> 138 us  [hop(): lax.ppermute(value, 'tensor', [(ring[i], ring[(i + k) % n_t]) for i in ra...]
    ppermute x0 -> x3, waiting for transfers between devices: none -> 16.5 us  [flip_t(): return lax.ppermute(value, 'tensor', [(i, i ^ k) for i in range(n_t)])]
    convert_element_type x18 -> x20, other arithmetic: 29.3 us -> 14.7 us  [the longest x2 5.16 us: normed(): return (value * row_scale(value) * gain1).astype(bf)]
    all_gather x0 -> x2, waiting for transfers between devices: none -> 13.5 us  [the longest x1 13.5 us: on_device(): weights = lax.all_gather(own_w, 'tensor', axis=0)]
    pallas_call x1, Pallas kernels: 39.1 us -> 26 us  [attn_fwd(): pl.pallas_call(attn_fwd_kernel, name='attn_fwd', out_shape=(jax.ShapeDtyp...]
    concatenate x3 -> x8, other arithmetic: 3.05 us -> 12.7 us  [the longest x1 2.68 us: on_device(): cot_far = jnp.concatenate([cot_far, flip(after(cot_far, one[2]), bit)])]
  transfers between devices with their start and end apart: 143 -> 72, of which waited for: 62 -> 36; matrix products, arithmetic and copies ran while one was open for 21% -> 18% of each run, Pallas kernels for 18% -> 19%
where the time goes in v2:
time: 542 us; the launch traced here: 535 us
  waiting for transfers between devices  191 us (35%)
  Pallas kernels  118 us (22%)
  starting transfers between devices  86.7 us (16%)
  local copies, waits for them, and re-layouts  61.1 us (11%)
  other arithmetic  48.9 us (9%)
  between operations  16.6 us (3%)
  matrix products  12.7 us (2%)
    ppermute x42, waiting for transfers between devices, hop(): lax.ppermute(value, 'tensor', [(ring[i], ring[(i + k) % n_t]) for i in ra...  138 us
    ppermute x42, starting transfers between devices, hop(): lax.ppermute(value, 'tensor', [(ring[i], ring[(i + k) % n_t]) for i in ra...  67.9 us
    pallas_call x1, Pallas kernels, attn_bwd(): pl.pallas_call(attn_bwd_kernel, name='attn_bwd', out_shape=jax.ShapeDtype...  36.7 us
    pallas_call x2, Pallas kernels, ffn(): pl.pallas_call(ffn_kernel, name='ffn', grid=(nb,), out_shape=[jax.ShapeDt...  31.4 us
    pallas_call x1, Pallas kernels, attn_fwd(): pl.pallas_call(attn_fwd_kernel, name='attn_fwd', out_shape=(jax.ShapeDtyp...  26 us
    ppermute x24, waiting for transfers between devices, flip(): return lax.ppermute(value, 'dp', [(i, i ^ k) for i in range(n_dp)])  23 us
    ppermute x3, waiting for transfers between devices, flip_t(): return lax.ppermute(value, 'tensor', [(i, i ^ k) for i in range(n_t)])  16.5 us
    pallas_call x1, Pallas kernels, ffn_grad(): pl.pallas_call(functools.partial(ffn_grad_kernel, nb), name='ffn_grad', g...  15.9 us
  transfers between devices with their start and end apart: 72, of which 36 were waited for; matrix products, arithmetic and copies ran while one was open for 18% of the time, Pallas kernels for 19%

profile of v2, /device:TPU:0, one launch (start us, length us, event | category | flops | bytes accessed | tf_op | source)
XLA Modules:
  0.0 535.0 jit_solution(17420419572164095871)
XLA Ops:
  12.9 2.5 collective-permute-start.1
  22.5 4.6 collective-permute-done.4
  33.7 4.0 collective-permute-done.6
  42.7 5.6 %collective-permute-done.25 = bf16[448,256]{1,0:T(8,128)(2,1)S(1)} collective-permute-done((bf16[448,256]{1,0:T(8,128)(2,1)S(1)}, bf16[448,256]{1,0:T(8,128)(2,1)S(1)}, u32[]{:S(2)}, u32[]{:S(2)}) %collective-permute-start.25) | collective-permute-done | bytes 229408 | tf_op jit(solution)/shard_map/ppermute | solution.py:332
  48.4 4.0 collective-permute-done.26
  69.0 6.5 %collective-permute-done.10 = bf16[192,1024]{1,0:T(8,128)(2,1)S(1)} collective-permute-done((bf16[192,1024]{1,0:T(8,128)(2,1)}, bf16[192,1024]{1,0:T(8,128)(2,1)S(1)}, u32[]{:S(2)}, u32[]{:S(2)}) %collective-permute-start.10) | collective-permute-done | bytes 393248 | tf_op jit(solution)/shard_map/ppermute | solution.py:329
  79.3 10.0 %collective-permute-done.12 = bf16[192,1024]{1,0:T(8,128)(2,1)} collective-permute-done((bf16[192,1024]{1,0:T(8,128)(2,1)S(1)}, bf16[192,1024]{1,0:T(8,128)(2,1)}, u32[]{:S(2)}, u32[]{:S(2)}) %collective-permute-start.12) | collective-permute-done | bytes 393248 | tf_op jit(solution)/shard_map/ppermute | solution.py:329
  89.4 2.9 collective-permute-start.14
  92.9 2.7 pad_maximum_fusion.1
  97.1 5.9 %collective-permute-done.14 = bf16[192,1024]{1,0:T(8,128)(2,1)} collective-permute-done((bf16[192,1024]{1,0:T(8,128)(2,1)}, bf16[192,1024]{1,0:T(8,128)(2,1)}, u32[]{:S(2)}, u32[]{:S(2)}) %collective-permute-start.14) | collective-permute-done | bytes 393248 | tf_op jit(solution)/shard_map/ppermute | solution.py:329
  104.4 3.5 collective-permute-start.16
  110.5 10.1 %collective-permute-done.16 = bf16[192,1024]{1,0:T(8,128)(2,1)S(1)} collective-permute-done((bf16[192,1024]{1,0:T(8,128)(2,1)}, bf16[192,1024]{1,0:T(8,128)(2,1)S(1)}, u32[]{:S(2)}, u32[]{:S(2)}) %collective-permute-start.16) | collective-permute-done | bytes 393248 | tf_op jit(solution)/shard_map/ppermute | solution.py:329
  120.6 3.4 collective-permute-done.15
  124.3 3.8 fusion.20
  132.4 26.0 %attn_fwd.1 = (bf16[3072,128]{1,0:T(8,128)(2,1)S(1)}, f32[12,1,512]{2,1,0:T(1,128)S(1)}) custom-call(s32[12]{0:T(128)S(1)} %reshape.225.first_ref, bf16[3072,384]{1,0:T(8,128)(2,1)S(1)} %slice_dynamic-update-slice_fusion.14.qkv_ref), custom_call_target="tpu_custom_call" | custom-call | flops 10000000000 | bytes 5000000 | tf_op jit(solution)/shard_map/attn_fwd/pallas_call | solution.py:93
  159.4 6.3 %collective-permute-start.17 = (bf16[384,128]{1,0:T(8,128)(2,1)}, bf16[384,128]{1,0:T(8,128)(2,1)}, u32[]{:S(2)}, u32[]{:S(2)}) collective-permute-start(bf16[384,128]{1,0:T(8,128)(2,1)} %get-tuple-element.193), channel_id=1, source_target_pairs={{0,1},{2,0},{4,2},{6,4},{7,6},{5,7},{3,5},{1,3},{8,9},{10,8},{12,1... | collective-permute-start | bytes 294920 | tf_op jit(solution)/shard_map/ppermute | solution.py:329
  167.9 5.3 collective-permute-start.20
  179.9 2.8 collective-permute-done.18
  185.7 10.3 %collective-permute-done.21 = bf16[384,128]{1,0:T(8,128)(2,1)S(1)} collective-permute-done((bf16[384,128]{1,0:T(8,128)(2,1)S(1)}, bf16[384,128]{1,0:T(8,128)(2,1)S(1)}, u32[]{:S(2)}, u32[]{:S(2)}) %collective-permute-start.21) | collective-permute-done | bytes 98336 | tf_op jit(solution)/shard_map/ppermute | solution.py:329
  207.8 13.5 %all-gather.7.cloned.1.call-done = bf16[3072,1024]{1,0:T(8,128)(2,1)} async-done(((bf16[384,1024]{1,0:T(8,128)(2,1)}), bf16[3072,1024]{1,0:T(8,128)(2,1)}) %all-gather.7.cloned.1.call-update) | async-done | bytes 6291472 | tf_op jit(solution)/shard_map/all_gather | solution.py:464
  221.3 15.8 %ffn.2 = (bf16[2,384,1024]{2,1,0:T(8,128)(2,1)}, bf16[2,384,1024]{2,1,0:T(8,128)(2,1)}, bf16[2,384,1024]{2,1,0:T(8,128)(2,1)}, bf16[2,384,1024]{2,1,0:T(8,128)(2,1)}, bf16[2,384,1024]{2,1,0:T(8,128)(2,1)}) custom-call(bf16[2,384,1024]{2,1,0:T(8,128)(2,1)} %pad_maximum_fusion.3.n_ref, bf16[2,384,1024]{2,1,0:T(8,128)(2,1)} %pad_maximum_fusion.2.c_ref, ...), custom_call_target="tpu_custom_call" | custom-call | flops 9663676416 | bytes 20000000 | tf_op jit(solution)/shard_map/ffn/pallas_call | solution.py:197
  239.6 2.7 pad_maximum_fusion.4.c_ref
  244.7 15.5 %ffn.3 = (bf16[2,384,1024]{2,1,0:T(8,128)(2,1)}, bf16[2,384,1024]{2,1,0:T(8,128)(2,1)}, bf16[2,384,1024]{2,1,0:T(8,128)(2,1)}, bf16[2,384,1024]{2,1,0:T(8,128)(2,1)}, bf16[2,384,1024]{2,1,0:T(8,128)(2,1)}) custom-call(bf16[2,384,1024]{2,1,0:T(8,128)(2,1)} %copy-done.54, bf16[2,384,1024]{2,1,0:T(8,128)(2,1)} %pad_maximum_fusion.4.c_ref, ...), custom_call_target="tpu_custom_call" | custom-call | flops 9663676416 | bytes 20000000 | tf_op jit(solution)/shard_map/ffn/pallas_call | solution.py:197
  267.4 15.9 %ffn_grad.1 = bf16[8,384,1024]{2,1,0:T(8,128)(2,1)} custom-call(bf16[768,1024]{1,0:T(8,128)(2,1)} %bitcast.127, bf16[768,1024]{1,0:T(8,128)(2,1)} %bitcast.137, bf16[768,1024]{1,0:T(8,128)(2,1)} %bitcast.126, bf16[768,1024]{1,0:T(8,128)(2,1)} %bitcast.128, bf16[768,1024]{1,0:T(8,128)(2,1)} %bitcast.161, bf16[768,1024]{1,0:T(8,128)(2,1)} %bitcast.164, ...), custom_call_target="tpu_custom_call" | custom-call | flops 9663676416 | bytes 20000000 | tf_op jit(solution)/shard_map/ffn_grad/pallas_call | solution.py:234
  283.3 4.2 collective-permute-done.38
  288.4 3.4 fusion.105
  296.8 3.1 collective-permute-start.41
  299.9 2.6 collective-permute-start.42
  305.0 7.9 %collective-permute-start.44 = (bf16[384,128]{1,0:T(8,128)(2,1)S(1)}, bf16[384,128]{1,0:T(8,128)(2,1)S(1)}, u32[]{:S(2)}, u32[]{:S(2)}) collective-permute-start(bf16[384,128]{1,0:T(8,128)(2,1)S(1)} %get-tuple-element.181), channel_id=1, source_target_pairs={{0,5},{2,3},{4,1},{6,0},{7,2},{5,4},{3,6},{1,7},{8,13},{10,11},{12... | collective-permute-start | bytes 294920 | tf_op jit(solution)/shard_map/ppermute | solution.py:329
  313.0 2.5 collective-permute-done.42
  316.5 5.9 %collective-permute-done.45 = bf16[384,128]{1,0:T(8,128)(2,1)S(1)} collective-permute-done((bf16[384,128]{1,0:T(8,128)(2,1)S(1)}, bf16[384,128]{1,0:T(8,128)(2,1)S(1)}, u32[]{:S(2)}, u32[]{:S(2)}) %collective-permute-start.45) | collective-permute-done | bytes 98336 | tf_op jit(solution)/shard_map/ppermute | solution.py:329
  330.0 36.7 %attn_bwd.1.gq_ref = bf16[3072,384]{1,0:T(8,128)(2,1)S(1)} custom-call(s32[12]{0:T(128)S(1)} %reshape.225.first_ref, bf16[3072,384]{1,0:T(8,128)(2,1)S(1)} %slice_dynamic-update-slice_fusion.14.qkv_ref, bf16[3072,128]{1,0:T(8,128)(2,1)S(1)} %copy-done.3, bf16[3072,128]{1,0:T(8,128)(2,1)S(1)} %copy-done.9, f32[12,1,512]{2,1,0:T(1,128)S(1)} %get-tuple-element.70.log_ref), custom_call_target="tpu_custom_call" | custom-call | flops 25999998976 | bytes 9000000 | tf_op jit(solution)/shard_map/attn_bwd/pallas_call | solution.py:153
  371.5 19.2 %collective-permute-done.47 = bf16[192,1024]{1,0:T(8,128)(2,1)S(1)} collective-permute-done((bf16[192,1024]{1,0:T(8,128)(2,1)S(1)}, bf16[192,1024]{1,0:T(8,128)(2,1)S(1)}, u32[]{:S(2)}, u32[]{:S(2)}) %collective-permute-start.47) | collective-permute-done | bytes 393248 | tf_op jit(solution)/shard_map/ppermute | solution.py:329
  394.9 7.8 %late_grads.1 = (f32[1424,512]{1,0:T(8,128)S(1)}, bf16[1424,512]{1,0:T(8,128)(2,1)S(1)}) custom-call(s32[4]{0:T(128)S(1)} %pad_add_fusion.order_ref, bf16[3072,384]{1,0:T(8,128)(2,1)S(1)} %attn_bwd.1.gq_ref, bf16[3072,1024]{1,0:T(8,128)(2,1)} %slice_dynamic-update-slice_fusion.all_ref, bf16[384,1024]{1,0:T(8,128)(2,1)S(1)} %copy-done.7, ...), custom_call_target="tpu_custom_call" | custom-call | flops 4000000000 | bytes 14000000 | tf_op jit(solution)/shard_map/late_grads/pallas_call | solution.py:279
  405.2 4.0 collective-permute-done.55
  413.0 4.7 collective-permute-done.49
  423.7 5.7 %collective-permute-done.50 = bf16[192,1024]{1,0:T(8,128)(2,1)S(1)} collective-permute-done((bf16[192,1024]{1,0:T(8,128)(2,1)S(1)}, bf16[192,1024]{1,0:T(8,128)(2,1)S(1)}, u32[]{:S(2)}, u32[]{:S(2)}) %collective-permute-start.50) | collective-permute-done | bytes 393248 | tf_op jit(solution)/shard_map/ppermute | solution.py:329
  432.5 2.7 collective-permute-start.62
  435.2 18.2 %collective-permute-done.51 = bf16[192,1024]{1,0:T(8,128)(2,1)S(1)} collective-permute-done((bf16[192,1024]{1,0:T(8,128)(2,1)S(1)}, bf16[192,1024]{1,0:T(8,128)(2,1)S(1)}, u32[]{:S(2)}, u32[]{:S(2)}) %collective-permute-start.51) | collective-permute-done | bytes 393248 | tf_op jit(solution)/shard_map/ppermute | solution.py:329
  453.7 7.4 %collective-permute-start.52 = (bf16[192,1024]{1,0:T(8,128)(2,1)S(1)}, bf16[192,1024]{1,0:T(8,128)(2,1)S(1)}, u32[]{:S(2)}, u32[]{:S(2)}) collective-permute-start(bf16[192,1024]{1,0:T(8,128)(2,1)S(1)} %get-tuple-element.154), channel_id=1, source_target_pairs={{0,1},{2,0},{4,2},{6,4},{7,6},{5,7},{3,5},{1,3},{8,9},{10,8},{12,1... | collective-permute-start | bytes 1179656 | tf_op jit(solution)/shard_map/ppermute | solution.py:329
  464.6 7.2 %collective-permute-done.52 = bf16[192,1024]{1,0:T(8,128)(2,1)S(1)} collective-permute-done((bf16[192,1024]{1,0:T(8,128)(2,1)S(1)}, bf16[192,1024]{1,0:T(8,128)(2,1)S(1)}, u32[]{:S(2)}, u32[]{:S(2)}) %collective-permute-start.52) | collective-permute-done | bytes 393248 | tf_op jit(solution)/shard_map/ppermute | solution.py:329
  472.9 3.9 collective-permute-start.53
  479.4 2.9 collective-permute-start.63
  482.3 2.9 collective-permute-done.53
  488.0 10.4 %collective-permute-done.63 = bf16[4,144,256]{2,1,0:T(8,128)(2,1)S(1)} collective-permute-done((bf16[4,144,256]{2,1,0:T(8,128)(2,1)S(1)}, bf16[4,144,256]{2,1,0:T(8,128)(2,1)S(1)}, u32[]{:S(2)}, u32[]{:S(2)}) %collective-permute-start.63) | collective-permute-done | bytes 294944 | tf_op jit(solution)/shard_map/ppermute | solution.py:335
  498.5 5.1 collective-permute-done.64
  515.8 5.7 %collective-permute-done.67 = bf16[3,1,128,256]{3,2,1,0:T(8,128)(2,1)S(1)} collective-permute-done((bf16[3,1,128,256]{3,2,1,0:T(8,128)(2,1)S(1)}, bf16[3,1,128,256]{3,2,1,0:T(8,128)(2,1)S(1)}, u32[]{:S(2)}, u32[]{:S(2)}) %collective-permute-start.67) | collective-permute-done | bytes 196640 | tf_op jit(solution)/shard_map/ppermute | solution.py:332
  521.5 3.4 collective-permute-done.68
  (433 shorter events, 157.2 us)
Async XLA Ops:
  7.2 168.1 %all-gather.5.cloned.1.call-start = ((), (), s32[]{:S(2)}) async-start(), calls=%async_computation.2 | async-start | bytes 1179648 | tf_op jit(solution)/shard_map/all_gather | solution.py:463
  12.5 19.3 %collective-permute-start = (bf16[400,256]{1,0:T(8,128)(2,1)}, bf16[400,256]{1,0:T(8,128)(2,1)}, u32[]{:S(2)}, u32[]{:S(2)}) collective-permute-start(bf16[400,256]{1,0:T(8,128)(2,1)} %get-tuple-element.197), channel_id=1, source_target_pairs={{0,8},{8,0},{16,24},{24,16},{1,9},{9,1},{17,25},{25,17},{2,10},{10... | collective-permute-start | bytes 614408 | tf_op jit(solution)/shard_map/ppermute | solution.py:332
  12.9 19.8 %collective-permute-start.1 = (bf16[400,256]{1,0:T(8,128)(2,1)}, bf16[400,256]{1,0:T(8,128)(2,1)}, u32[]{:S(2)}, u32[]{:S(2)}) collective-permute-start(bf16[400,256]{1,0:T(8,128)(2,1)} %get-tuple-element.197), channel_id=1, source_target_pairs={{0,16},{8,24},{16,0},{24,8},{1,17},{9,25},{17,1},{25,9},{2,18},{10... | collective-permute-start | bytes 614408 | tf_op jit(solution)/shard_map/ppermute | solution.py:332
  15.4 26.1 %collective-permute-start.2 = (bf16[400,256]{1,0:T(8,128)(2,1)}, bf16[400,256]{1,0:T(8,128)(2,1)}, u32[]{:S(2)}, u32[]{:S(2)}) collective-permute-start(bf16[400,256]{1,0:T(8,128)(2,1)} %get-tuple-element.197), channel_id=1, source_target_pairs={{0,24},{8,16},{16,8},{24,0},{1,25},{9,17},{17,9},{25,1},{2,26},{10... | collective-permute-start | bytes 614408 | tf_op jit(solution)/shard_map/ppermute | solution.py:332
  15.6 11.4 %collective-permute-start.4 = (bf16[192,1024]{1,0:T(8,128)(2,1)S(1)}, bf16[192,1024]{1,0:T(8,128)(2,1)S(1)}, u32[]{:S(2)}, u32[]{:S(2)}) collective-permute-start(bf16[192,1024]{1,0:T(8,128)(2,1)S(1)} %get-tuple-element.196), channel_id=1, source_target_pairs={{0,1},{2,0},{4,2},{6,4},{7,6},{5,7},{3,5},{1,3},{8,9},{10,8},{12,1... | collective-permute-start | bytes 1179656 | tf_op jit(solution)/shard_map/ppermute | solution.py:329
  17.4 11.3 %collective-permute-start.3 = (bf16[192,1024]{1,0:T(8,128)(2,1)S(1)}, bf16[192,1024]{1,0:T(8,128)(2,1)S(1)}, u32[]{:S(2)}, u32[]{:S(2)}) collective-permute-start(bf16[192,1024]{1,0:T(8,128)(2,1)S(1)} %get-tuple-element.195), channel_id=1, source_target_pairs={{0,2},{2,4},{4,6},{6,7},{7,5},{5,3},{3,1},{1,0},{8,10},{10,12},{12... | collective-permute-start | bytes 1179656 | tf_op jit(solution)/shard_map/ppermute | solution.py:329
  37.7 14.7 %collective-permute-start.8 = (bf16[192,1024]{1,0:T(8,128)(2,1)}, bf16[192,1024]{1,0:T(8,128)(2,1)}, u32[]{:S(2)}, u32[]{:S(2)}) collective-permute-start(bf16[192,1024]{1,0:T(8,128)(2,1)} %collective-permute-done.6), channel_id=1, source_target_pairs={{0,1},{2,0},{4,2},{6,4},{7,6},{5,7},{3,5},{1,3},{8,9},{10,8},{12,1... | collective-permute-start | bytes 1179656 | tf_op jit(solution)/shard_map/ppermute | solution.py:329
  39.3 13.0 %collective-permute-start.7 = (bf16[192,1024]{1,0:T(8,128)(2,1)}, bf16[192,1024]{1,0:T(8,128)(2,1)}, u32[]{:S(2)}, u32[]{:S(2)}) collective-permute-start(bf16[192,1024]{1,0:T(8,128)(2,1)} %collective-permute-done.5), channel_id=1, source_target_pairs={{0,2},{2,4},{4,6},{6,7},{7,5},{5,3},{3,1},{1,0},{8,10},{10,12},{12... | collective-permute-start | bytes 1179656 | tf_op jit(solution)/shard_map/ppermute | solution.py:329
  54.2 167.0 %all-gather.7.cloned.1.call-start = ((), (), s32[]{:S(2)}) async-start(), calls=%async_computation.3 | async-start | bytes 7077888 | tf_op jit(solution)/shard_map/all_gather | solution.py:464
  60.5 15.0 %collective-permute-start.10 = (bf16[192,1024]{1,0:T(8,128)(2,1)}, bf16[192,1024]{1,0:T(8,128)(2,1)S(1)}, u32[]{:S(2)}, u32[]{:S(2)}) collective-permute-start(bf16[192,1024]{1,0:T(8,128)(2,1)} %collective-permute-done.8), channel_id=1, source_target_pairs={{0,1},{2,0},{4,2},{6,4},{7,6},{5,7},{3,5},{1,3},{8,9},{10,8},{12,1... | collective-permute-start | bytes 1179656 | tf_op jit(solution)/shard_map/ppermute | solution.py:329
  62.1 14.8 %collective-permute-start.9 = (bf16[192,1024]{1,0:T(8,128)(2,1)}, bf16[192,1024]{1,0:T(8,128)(2,1)S(1)}, u32[]{:S(2)}, u32[]{:S(2)}) collective-permute-start(bf16[192,1024]{1,0:T(8,128)(2,1)} %collective-permute-done.7), channel_id=1, source_target_pairs={{0,2},{2,4},{4,6},{6,7},{7,5},{5,3},{3,1},{1,0},{8,10},{10,12},{12... | collective-permute-start | bytes 1179656 | tf_op jit(solution)/shard_map/ppermute | solution.py:329
  63.2 29.7 %collective-permute-start.29 = (bf16[1,384,1024]{2,1,0:T(8,128)(2,1)}, bf16[1,384,1024]{2,1,0:T(8,128)(2,1)}, u32[]{:S(2)}, u32[]{:S(2)}) collective-permute-start(bf16[1,384,1024]{2,1,0:T(8,128)(2,1)} %bitcast.17), channel_id=1, source_target_pairs={{0,16},{8,24},{16,0},{24,8},{1,17},{9,25},{17,1},{25,9},{2,18},{10... | collective-permute-start | bytes 2359304 | tf_op jit(solution)/shard_map/ppermute | solution.py:332
  75.5 13.8 %collective-permute-start.12 = (bf16[192,1024]{1,0:T(8,128)(2,1)S(1)}, bf16[192,1024]{1,0:T(8,128)(2,1)}, u32[]{:S(2)}, u32[]{:S(2)}) collective-permute-start(bf16[192,1024]{1,0:T(8,128)(2,1)S(1)} %collective-permute-done.10), channel_id=1, source_target_pairs={{0,1},{2,0},{4,2},{6,4},{7,6},{5,7},{3,5},{1,3},{8,9},{10,8},{12,1... | collective-permute-start | bytes 1179656 | tf_op jit(solution)/shard_map/ppermute | solution.py:329
  77.0 15.7 %collective-permute-start.11 = (bf16[192,1024]{1,0:T(8,128)(2,1)S(1)}, bf16[192,1024]{1,0:T(8,128)(2,1)}, u32[]{:S(2)}, u32[]{:S(2)}) collective-permute-start(bf16[192,1024]{1,0:T(8,128)(2,1)S(1)} %collective-permute-done.9), channel_id=1, source_target_pairs={{0,2},{2,4},{4,6},{6,7},{7,5},{5,3},{3,1},{1,0},{8,10},{10,12},{12... | collective-permute-start | bytes 1179656 | tf_op jit(solution)/shard_map/ppermute | solution.py:329
  89.4 13.6 %collective-permute-start.14 = (bf16[192,1024]{1,0:T(8,128)(2,1)}, bf16[192,1024]{1,0:T(8,128)(2,1)}, u32[]{:S(2)}, u32[]{:S(2)}) collective-permute-start(bf16[192,1024]{1,0:T(8,128)(2,1)} %collective-permute-done.12), channel_id=1, source_target_pairs={{0,1},{2,0},{4,2},{6,4},{7,6},{5,7},{3,5},{1,3},{8,9},{10,8},{12,1... | collective-permute-start | bytes 1179656 | tf_op jit(solution)/shard_map/ppermute | solution.py:329
  95.6 413.9 %reduce-scatter.2.cloned.1.call-start = ((), (), s32[]{:S(2)}) async-start(), calls=%async_computation.1 | async-start | bytes 7077888 | tf_op jit(solution)/shard_map/reduce_scatter | solution.py:538
  104.4 16.2 %collective-permute-start.16 = (bf16[192,1024]{1,0:T(8,128)(2,1)}, bf16[192,1024]{1,0:T(8,128)(2,1)S(1)}, u32[]{:S(2)}, u32[]{:S(2)}) collective-permute-start(bf16[192,1024]{1,0:T(8,128)(2,1)} %collective-permute-done.14), channel_id=1, source_target_pairs={{0,1},{2,0},{4,2},{6,4},{7,6},{5,7},{3,5},{1,3},{8,9},{10,8},{12,1... | collective-permute-start | bytes 1179656 | tf_op jit(solution)/shard_map/ppermute | solution.py:329
  107.9 16.1 %collective-permute-start.15 = (bf16[192,1024]{1,0:T(8,128)(2,1)}, bf16[192,1024]{1,0:T(8,128)(2,1)S(1)}, u32[]{:S(2)}, u32[]{:S(2)}) collective-permute-start(bf16[192,1024]{1,0:T(8,128)(2,1)} %collective-permute-done.13), channel_id=1, source_target_pairs={{0,2},{2,4},{4,6},{6,7},{7,5},{5,3},{3,1},{1,0},{8,10},{10,12},{12... | collective-permute-start | bytes 1179656 | tf_op jit(solution)/shard_map/ppermute | solution.py:329
  159.4 19.5 %collective-permute-start.17 = (bf16[384,128]{1,0:T(8,128)(2,1)}, bf16[384,128]{1,0:T(8,128)(2,1)}, u32[]{:S(2)}, u32[]{:S(2)}) collective-permute-start(bf16[384,128]{1,0:T(8,128)(2,1)} %get-tuple-element.193), channel_id=1, source_target_pairs={{0,1},{2,0},{4,2},{6,4},{7,6},{5,7},{3,5},{1,3},{8,9},{10,8},{12,1... | collective-permute-start | bytes 294920 | tf_op jit(solution)/shard_map/ppermute | solution.py:329
  165.7 17.0 %collective-permute-start.18 = (bf16[384,128]{1,0:T(8,128)(2,1)}, bf16[384,128]{1,0:T(8,128)(2,1)}, u32[]{:S(2)}, u32[]{:S(2)}) collective-permute-start(bf16[384,128]{1,0:T(8,128)(2,1)} %get-tuple-element.192), channel_id=1, source_target_pairs={{0,3},{2,1},{4,0},{6,2},{7,4},{5,6},{3,7},{1,5},{8,11},{10,9},{12,... | collective-permute-start | bytes 294920 | tf_op jit(solution)/shard_map/ppermute | solution.py:329
  167.9 15.7 %collective-permute-start.19 = (bf16[384,128]{1,0:T(8,128)(2,1)}, bf16[384,128]{1,0:T(8,128)(2,1)}, u32[]{:S(2)}, u32[]{:S(2)}) collective-permute-start(bf16[384,128]{1,0:T(8,128)(2,1)} %get-tuple-element.191), channel_id=1, source_target_pairs={{0,5},{2,3},{4,1},{6,0},{7,2},{5,4},{3,6},{1,7},{8,13},{10,11},{12... | collective-permute-start | bytes 294920 | tf_op jit(solution)/shard_map/ppermute | solution.py:329
  167.9 16.7 %collective-permute-start.20 = (bf16[384,128]{1,0:T(8,128)(2,1)}, bf16[384,128]{1,0:T(8,128)(2,1)}, u32[]{:S(2)}, u32[]{:S(2)}) collective-permute-start(bf16[384,128]{1,0:T(8,128)(2,1)} %get-tuple-element.190), channel_id=1, source_target_pairs={{0,7},{2,5},{4,3},{6,1},{7,0},{5,2},{3,4},{1,6},{8,15},{10,13},{12... | collective-permute-start | bytes 294920 | tf_op jit(solution)/shard_map/ppermute | solution.py:329
  175.3 21.0 %collective-permute-start.27 = (bf16[8,64,1024]{2,1,0:T(8,128)(2,1)}, bf16[8,64,1024]{2,1,0:T(8,128)(2,1)S(1)}, u32[]{:S(2)}, u32[]{:S(2)}) collective-permute-start(bf16[8,64,1024]{2,1,0:T(8,128)(2,1)} %bitcast.129), channel_id=1, source_target_pairs={{0,8},{8,0},{16,24},{24,16},{1,9},{9,1},{17,25},{25,17},{2,10},{10... | collective-permute-start | bytes 3145736 | tf_op jit(solution)/shard_map/ppermute | solution.py:332
  179.0 17.0 %collective-permute-start.21 = (bf16[384,128]{1,0:T(8,128)(2,1)S(1)}, bf16[384,128]{1,0:T(8,128)(2,1)S(1)}, u32[]{:S(2)}, u32[]{:S(2)}) collective-permute-start(bf16[384,128]{1,0:T(8,128)(2,1)S(1)} %get-tuple-element.189), channel_id=1, source_target_pairs={{0,6},{2,7},{4,5},{6,3},{7,1},{5,0},{3,2},{1,4},{8,14},{10,15},{12... | collective-permute-start | bytes 294920 | tf_op jit(solution)/shard_map/ppermute | solution.py:329
  182.7 13.3 %collective-permute-start.22 = (bf16[384,128]{1,0:T(8,128)(2,1)S(1)}, bf16[384,128]{1,0:T(8,128)(2,1)S(1)}, u32[]{:S(2)}, u32[]{:S(2)}) collective-permute-start(bf16[384,128]{1,0:T(8,128)(2,1)S(1)} %get-tuple-element.188), channel_id=1, source_target_pairs={{0,4},{2,6},{4,7},{6,5},{7,3},{5,1},{3,0},{1,2},{8,12},{10,14},{12... | collective-permute-start | bytes 294920 | tf_op jit(solution)/shard_map/ppermute | solution.py:329
  183.7 12.6 %collective-permute-start.23 = (bf16[384,128]{1,0:T(8,128)(2,1)S(1)}, bf16[384,128]{1,0:T(8,128)(2,1)S(1)}, u32[]{:S(2)}, u32[]{:S(2)}) collective-permute-start(bf16[384,128]{1,0:T(8,128)(2,1)S(1)} %get-tuple-element.187), channel_id=1, source_target_pairs={{0,2},{2,4},{4,6},{6,7},{7,5},{5,3},{3,1},{1,0},{8,10},{10,12},{12... | collective-permute-start | bytes 294920 | tf_op jit(solution)/shard_map/ppermute | solution.py:329
  184.7 18.2 %collective-permute-start.30 = (bf16[1,384,1024]{2,1,0:T(8,128)(2,1)S(1)}, bf16[1,384,1024]{2,1,0:T(8,128)(2,1)S(1)}, u32[]{:S(2)}, u32[]{:S(2)}) collective-permute-start(bf16[1,384,1024]{2,1,0:T(8,128)(2,1)S(1)} %copy-done.53), channel_id=1, source_target_pairs={{0,8},{8,0},{16,24},{24,16},{1,9},{9,1},{17,25},{25,17},{2,10},{10... | collective-permute-start | bytes 2359304 | tf_op jit(solution)/shard_map/ppermute | solution.py:332
  196.0 43.7 %collective-permute-start.34 = (bf16[1,384,1024]{2,1,0:T(8,128)(2,1)}, bf16[1,384,1024]{2,1,0:T(8,128)(2,1)}, u32[]{:S(2)}, u32[]{:S(2)}) collective-permute-start(bf16[1,384,1024]{2,1,0:T(8,128)(2,1)} %get-tuple-element.164), channel_id=1, source_target_pairs={{0,8},{8,0},{16,24},{24,16},{1,9},{9,1},{17,25},{25,17},{2,10},{10... | collective-permute-start | bytes 2359304 | tf_op jit(solution)/shard_map/ppermute | solution.py:332
  205.3 31.8 %collective-permute-start.32 = (bf16[1,384,1024]{2,1,0:T(8,128)(2,1)}, bf16[1,384,1024]{2,1,0:T(8,128)(2,1)}, u32[]{:S(2)}, u32[]{:S(2)}) collective-permute-start(bf16[1,384,1024]{2,1,0:T(8,128)(2,1)} %fusion.33), channel_id=1, source_target_pairs={{0,16},{8,24},{16,0},{24,8},{1,17},{9,25},{17,1},{25,9},{2,18},{10... | collective-permute-start | bytes 2359304 | tf_op jit(solution)/shard_map/ppermute | solution.py:332
  266.1 21.4 %collective-permute-start.36 = (bf16[1,384,1024]{2,1,0:T(8,128)(2,1)}, bf16[1,384,1024]{2,1,0:T(8,128)(2,1)S(1)}, u32[]{:S(2)}, u32[]{:S(2)}) collective-permute-start(bf16[1,384,1024]{2,1,0:T(8,128)(2,1)} %slice.275), channel_id=1, source_target_pairs={{0,8},{8,0},{16,24},{24,16},{1,9},{9,1},{17,25},{25,17},{2,10},{10... | collective-permute-start | bytes 2359304 | tf_op jit(solution)/shard_map/ppermute | solution.py:332
  267.4 20.1 %collective-permute-start.38 = (bf16[1,384,1024]{2,1,0:T(8,128)(2,1)}, bf16[1,384,1024]{2,1,0:T(8,128)(2,1)S(1)}, u32[]{:S(2)}, u32[]{:S(2)}) collective-permute-start(bf16[1,384,1024]{2,1,0:T(8,128)(2,1)} %add_convert_fusion), channel_id=1, source_target_pairs={{0,16},{8,24},{16,0},{24,8},{1,17},{9,25},{17,1},{25,9},{2,18},{10... | collective-permute-start | bytes 2359304 | tf_op jit(solution)/shard_map/ppermute | solution.py:332
  295.3 29.4 %collective-permute-start.31 = (bf16[1,384,1024]{2,1,0:T(8,128)(2,1)}, bf16[1,384,1024]{2,1,0:T(8,128)(2,1)}, u32[]{:S(2)}, u32[]{:S(2)}) collective-permute-start(bf16[1,384,1024]{2,1,0:T(8,128)(2,1)} %slice.270), channel_id=1, source_target_pairs={{0,8},{8,0},{16,24},{24,16},{1,9},{9,1},{17,25},{25,17},{2,10},{10... | collective-permute-start | bytes 2359304 | tf_op jit(solution)/shard_map/ppermute | solution.py:332
  296.3 30.2 %collective-permute-start.35 = (bf16[1,384,1024]{2,1,0:T(8,128)(2,1)}, bf16[1,384,1024]{2,1,0:T(8,128)(2,1)}, u32[]{:S(2)}, u32[]{:S(2)}) collective-permute-start(bf16[1,384,1024]{2,1,0:T(8,128)(2,1)} %slice.273), channel_id=1, source_target_pairs={{0,8},{8,0},{16,24},{24,16},{1,9},{9,1},{17,25},{25,17},{2,10},{10... | collective-permute-start | bytes 2359304 | tf_op jit(solution)/shard_map/ppermute | solution.py:332
  299.9 15.7 %collective-permute-start.42 = (bf16[384,128]{1,0:T(8,128)(2,1)S(1)}, bf16[384,128]{1,0:T(8,128)(2,1)S(1)}, u32[]{:S(2)}, u32[]{:S(2)}) collective-permute-start(bf16[384,128]{1,0:T(8,128)(2,1)S(1)} %get-tuple-element.183), channel_id=1, source_target_pairs={{0,6},{2,7},{4,5},{6,3},{7,1},{5,0},{3,2},{1,4},{8,14},{10,15},{12... | collective-permute-start | bytes 294920 | tf_op jit(solution)/shard_map/ppermute | solution.py:329
  302.4 13.1 %collective-permute-start.43 = (bf16[384,128]{1,0:T(8,128)(2,1)S(1)}, bf16[384,128]{1,0:T(8,128)(2,1)S(1)}, u32[]{:S(2)}, u32[]{:S(2)}) collective-permute-start(bf16[384,128]{1,0:T(8,128)(2,1)S(1)} %get-tuple-element.182), channel_id=1, source_target_pairs={{0,7},{2,5},{4,3},{6,1},{7,0},{5,2},{3,4},{1,6},{8,15},{10,13},{12... | collective-permute-start | bytes 294920 | tf_op jit(solution)/shard_map/ppermute | solution.py:329
  305.0 11.4 %collective-permute-start.44 = (bf16[384,128]{1,0:T(8,128)(2,1)S(1)}, bf16[384,128]{1,0:T(8,128)(2,1)S(1)}, u32[]{:S(2)}, u32[]{:S(2)}) collective-permute-start(bf16[384,128]{1,0:T(8,128)(2,1)S(1)} %get-tuple-element.181), channel_id=1, source_target_pairs={{0,5},{2,3},{4,1},{6,0},{7,2},{5,4},{3,6},{1,7},{8,13},{10,11},{12... | collective-permute-start | bytes 294920 | tf_op jit(solution)/shard_map/ppermute | solution.py:329
  328.6 133.4 %collective-permute-start.39 = (bf16[1,384,1024]{2,1,0:T(8,128)(2,1)S(1)}, bf16[1,384,1024]{2,1,0:T(8,128)(2,1)S(1)}, u32[]{:S(2)}, u32[]{:S(2)}) collective-permute-start(bf16[1,384,1024]{2,1,0:T(8,128)(2,1)S(1)} %slice.507), channel_id=1, source_target_pairs={{0,16},{8,24},{16,0},{24,8},{1,17},{9,25},{17,1},{25,9},{2,18},{10... | collective-permute-start | bytes 2359304 | tf_op jit(solution)/shard_map/ppermute | solution.py:332
  368.5 22.1 %collective-permute-start.47 = (bf16[192,1024]{1,0:T(8,128)(2,1)S(1)}, bf16[192,1024]{1,0:T(8,128)(2,1)S(1)}, u32[]{:S(2)}, u32[]{:S(2)}) collective-permute-start(bf16[192,1024]{1,0:T(8,128)(2,1)S(1)} %get-tuple-element.177), channel_id=1, source_target_pairs={{0,1},{2,0},{4,2},{6,4},{7,6},{5,7},{3,5},{1,3},{8,9},{10,8},{12,1... | collective-permute-start | bytes 1179656 | tf_op jit(solution)/shard_map/ppermute | solution.py:329
  368.7 22.0 %collective-permute-start.54 = (bf16[192,1024]{1,0:T(8,128)(2,1)S(1)}, bf16[192,1024]{1,0:T(8,128)(2,1)S(1)}, u32[]{:S(2)}, u32[]{:S(2)}) collective-permute-start(bf16[192,1024]{1,0:T(8,128)(2,1)S(1)} %get-tuple-element.178), channel_id=1, source_target_pairs={{0,2},{2,4},{4,6},{6,7},{7,5},{5,3},{3,1},{1,0},{8,10},{10,12},{12... | collective-permute-start | bytes 1179656 | tf_op jit(solution)/shard_map/ppermute | solution.py:329
  390.9 14.3 %collective-permute-start.48 = (bf16[192,1024]{1,0:T(8,128)(2,1)S(1)}, bf16[192,1024]{1,0:T(8,128)(2,1)S(1)}, u32[]{:S(2)}, u32[]{:S(2)}) collective-permute-start(bf16[192,1024]{1,0:T(8,128)(2,1)S(1)} %get-tuple-element.162), channel_id=1, source_target_pairs={{0,1},{2,0},{4,2},{6,4},{7,6},{5,7},{3,5},{1,3},{8,9},{10,8},{12,1... | collective-permute-start | bytes 1179656 | tf_op jit(solution)/shard_map/ppermute | solution.py:329
  392.4 16.8 %collective-permute-start.55 = (bf16[192,1024]{1,0:T(8,128)(2,1)S(1)}, bf16[192,1024]{1,0:T(8,128)(2,1)S(1)}, u32[]{:S(2)}, u32[]{:S(2)}) collective-permute-start(bf16[192,1024]{1,0:T(8,128)(2,1)S(1)} %get-tuple-element.163), channel_id=1, source_target_pairs={{0,2},{2,4},{4,6},{6,7},{7,5},{5,3},{3,1},{1,0},{8,10},{10,12},{12... | collective-permute-start | bytes 1179656 | tf_op jit(solution)/shard_map/ppermute | solution.py:329
  402.7 29.2 %collective-permute-start.61 = (bf16[1424,512]{1,0:T(8,128)(2,1)S(1)}, bf16[1424,512]{1,0:T(8,128)(2,1)S(1)}, u32[]{:S(2)}, u32[]{:S(2)}) collective-permute-start(bf16[1424,512]{1,0:T(8,128)(2,1)S(1)} %get-tuple-element.74), channel_id=1, source_target_pairs={{0,8},{8,0},{16,24},{24,16},{1,9},{9,1},{17,25},{25,17},{2,10},{10... | collective-permute-start | bytes 4374536 | tf_op jit(solution)/shard_map/ppermute | solution.py:332
  429.8 23.6 %collective-permute-start.51 = (bf16[192,1024]{1,0:T(8,128)(2,1)S(1)}, bf16[192,1024]{1,0:T(8,128)(2,1)S(1)}, u32[]{:S(2)}, u32[]{:S(2)}) collective-permute-start(bf16[192,1024]{1,0:T(8,128)(2,1)S(1)} %get-tuple-element.156), channel_id=1, source_target_pairs={{0,1},{2,0},{4,2},{6,4},{7,6},{5,7},{3,5},{1,3},{8,9},{10,8},{12,1... | collective-permute-start | bytes 1179656 | tf_op jit(solution)/shard_map/ppermute | solution.py:329
  430.2 23.2 %collective-permute-start.58 = (bf16[192,1024]{1,0:T(8,128)(2,1)S(1)}, bf16[192,1024]{1,0:T(8,128)(2,1)S(1)}, u32[]{:S(2)}, u32[]{:S(2)}) collective-permute-start(bf16[192,1024]{1,0:T(8,128)(2,1)S(1)} %get-tuple-element.157), channel_id=1, source_target_pairs={{0,2},{2,4},{4,6},{6,7},{7,5},{5,3},{3,1},{1,0},{8,10},{10,12},{12... | collective-permute-start | bytes 1179656 | tf_op jit(solution)/shard_map/ppermute | solution.py:329
  432.5 44.2 %collective-permute-start.62 = (bf16[1424,256]{1,0:T(8,128)(2,1)S(1)}, bf16[1424,256]{1,0:T(8,128)(2,1)S(1)}, u32[]{:S(2)}, u32[]{:S(2)}) collective-permute-start(bf16[1424,256]{1,0:T(8,128)(2,1)S(1)} %slice.508), channel_id=1, source_target_pairs={{0,16},{8,24},{16,0},{24,8},{1,17},{9,25},{17,1},{25,9},{2,18},{10... | collective-permute-start | bytes 2187272 | tf_op jit(solution)/shard_map/ppermute | solution.py:332
  453.7 18.1 %collective-permute-start.52 = (bf16[192,1024]{1,0:T(8,128)(2,1)S(1)}, bf16[192,1024]{1,0:T(8,128)(2,1)S(1)}, u32[]{:S(2)}, u32[]{:S(2)}) collective-permute-start(bf16[192,1024]{1,0:T(8,128)(2,1)S(1)} %get-tuple-element.154), channel_id=1, source_target_pairs={{0,1},{2,0},{4,2},{6,4},{7,6},{5,7},{3,5},{1,3},{8,9},{10,8},{12,1... | collective-permute-start | bytes 1179656 | tf_op jit(solution)/shard_map/ppermute | solution.py:329
  472.9 12.4 %collective-permute-start.53 = (bf16[192,1024]{1,0:T(8,128)(2,1)}, bf16[192,1024]{1,0:T(8,128)(2,1)}, u32[]{:S(2)}, u32[]{:S(2)}) collective-permute-start(bf16[192,1024]{1,0:T(8,128)(2,1)} %get-tuple-element.152), channel_id=1, source_target_pairs={{0,1},{2,0},{4,2},{6,4},{7,6},{5,7},{3,5},{1,3},{8,9},{10,8},{12,1... | collective-permute-start | bytes 1179656 | tf_op jit(solution)/shard_map/ppermute | solution.py:329
  479.4 18.9 %collective-permute-start.63 = (bf16[4,144,256]{2,1,0:T(8,128)(2,1)S(1)}, bf16[4,144,256]{2,1,0:T(8,128)(2,1)S(1)}, u32[]{:S(2)}, u32[]{:S(2)}) collective-permute-start(bf16[4,144,256]{2,1,0:T(8,128)(2,1)S(1)} %fusion.51), channel_id=1, source_target_pairs={{0,4},{1,5},{2,6},{3,7},{4,0},{5,1},{6,2},{7,3},{8,12},{9,13},{10,... | collective-permute-start | bytes 884744 | tf_op jit(solution)/shard_map/ppermute | solution.py:335
  (89 other events, 699.4 us)
Sparse Core Ops, SparseCore 0:
  54.4 46.2 all-gather.4
  102.8 118.3 all-gather.6
  324.8 145.0 reduce-scatter.1

commit v3 on v2

--- a/solution.py
+++ b/solution.py
@@ -1,4 +1,5 @@
 import functools
+import math
 
 import jax
 import jax.numpy as jnp
@@ -13,7 +14,12 @@
 HT = 256
 BULK_AT = 5
 WEIGHTS_AT = 3
-RS_LATE = True
+FOLD_AT = 2
+FAR_AT = 4
+FIRST_AT = 1
+SPREAD_AT = 6
+COMMON_AT = 4
+COT_AT = 5
 NT = (((1,), (1,)), ((), ()))
 NN = (((1,), (0,)), ((), ()))
 TN = (((0,), (0,)), ((), ()))
@@ -99,7 +105,7 @@
             out_specs=[pl.BlockSpec((BLK,128), lambda i,s:(i,0)), pl.BlockSpec((1,1,2*BLK), lambda i,s:(i,0,0))],
             scratch_shapes=[pltpu.VMEM((128,rows),jnp.bfloat16), pltpu.VMEM((1,2*BLK),f32), pltpu.VMEM((1,2*BLK),f32), pltpu.VMEM((DH,2*BLK),f32),pltpu.VMEM((128,2*BLK),jnp.bfloat16)]+[pltpu.VMEM((BLK,2*BLK),f32)]*2),
         compiler_params=pltpu.CompilerParams(vmem_limit_bytes=32<<20),
-        cost_estimate=pl.CostEstimate(flops=10*10**9, bytes_accessed=5*10**6, transcendentals=10**7),
+        cost_estimate=pl.CostEstimate(flops=1000, bytes_accessed=1000, transcendentals=0),
     )(first, qkv)
 
 
@@ -159,12 +165,23 @@
             out_specs=pl.BlockSpec((rows,384), lambda i,s:(0,0)),
             scratch_shapes=[pltpu.VMEM((128,rows),jnp.bfloat16), pltpu.VMEM((rows,128),f32), pltpu.VMEM((rows,128),f32), pltpu.VMEM((DH,2*BLK),f32)]+[pltpu.VMEM((128,2*BLK),jnp.bfloat16)]*2+[pltpu.VMEM((BLK,2*BLK),f32)]*4),
         compiler_params=pltpu.CompilerParams(vmem_limit_bytes=40<<20),
-        cost_estimate=pl.CostEstimate(flops=26*10**9, bytes_accessed=9*10**6, transcendentals=10**7),
+        cost_estimate=pl.CostEstimate(flops=1000, bytes_accessed=1000, transcendentals=0),
     )(first, qkv, do, o, log)
 
 
-def ffn_kernel(n_ref, c_ref, gate_ref, up_ref, down_ref, f_ref, d_ref, z_ref, g_ref, u_ref):
-    n2, c = n_ref[0], c_ref[0]
+def ffn_kernel(nb, *refs):
+    ns, cs = refs[:nb], refs[nb : 2 * nb]
+    gate_ref, up_ref, down_ref = refs[2 * nb : 2 * nb + 3]
+    f_ref, d_ref, z_ref, g_ref, u_ref, n_ref, c_ref = refs[-7:]
+    before = refs[2 * nb + 3 : -7]
+    for b in range(nb):
+
+        @pl.when(pl.program_id(0) == b)
+        def _():
+            n_ref[...] = ns[b][...]
+            c_ref[...] = cs[b][...]
+
+    n2, c = n_ref[...], c_ref[...]
     wg, wu, wd = (ref[...].reshape(-1, n2.shape[1]) for ref in (gate_ref, up_ref, down_ref))
     gate, up, dz = dot(n2, wg, NT), dot(n2, wu, NT), dot(c, wd, NT)
     sig = jax.nn.sigmoid(gate)
@@ -175,16 +192,22 @@
     z_ref[0] = z
     g_ref[0] = dg
     u_ref[0] = du
-    f_ref[0] = dot(z, wd, NN).astype(jnp.bfloat16)
-    d_ref[0] = (dot(dg, wg, NN) + dot(du, wu, NN)).astype(jnp.bfloat16)
-
-
-def ffn(n2, c, weights, hid):
-    nb, rows, width = n2.shape
+    f, d = dot(z, wd, NN), dot(dg, wg, NN) + dot(du, wu, NN)
+    if before:
+        f += before[0][0].astype(jnp.float32)
+        d += before[1][0].astype(jnp.float32)
+    f_ref[0] = f.astype(jnp.bfloat16)
+    d_ref[0] = d.astype(jnp.bfloat16)
+
+
+def ffn(ns, cs, weights, hid, before=()):
+    nb = len(ns)
+    rows, width = ns[0].shape
     n_t = weights.shape[0]
     total = n_t * hid
     bf = jnp.bfloat16
     full = pl.BlockSpec((1, rows, width), lambda s: (s, 0, 0))
+    whole = pl.BlockSpec((rows, width), lambda s: (0, 0))
     col = pl.BlockSpec((1, rows, total), lambda s: (s, 0, 0))
     kinds = [
         pl.BlockSpec(
@@ -195,53 +218,62 @@
         for which in range(3)
     ]
     return pl.pallas_call(
-        ffn_kernel,
+        functools.partial(ffn_kernel, nb),
         name="ffn",
         grid=(nb,),
         out_shape=[jax.ShapeDtypeStruct((nb, rows, width), bf)] * 2
         + [jax.ShapeDtypeStruct((nb, rows, total), bf)] * 3,
-        in_specs=[full] * 2 + kinds,
+        in_specs=[whole] * (2 * nb) + kinds + [full] * len(before),
         out_specs=[full] * 2 + [col] * 3,
+        scratch_shapes=[pltpu.VMEM((rows, width), bf)] * 2,
         compiler_params=pltpu.CompilerParams(vmem_limit_bytes=56 << 20),
-        cost_estimate=pl.CostEstimate(
-            flops=2 * nb * rows * width * total * 6,
-            bytes_accessed=20 * 10**6,
-            transcendentals=nb * rows * total,
-        ),
-    )(n2, c, weights, weights, weights)
-
-
-def ffn_grad_kernel(nb, *refs):
-    ns, cs, zs, gs, us = (refs[k * nb : (k + 1) * nb] for k in range(5))
-    out = refs[5 * nb]
+        cost_estimate=pl.CostEstimate(flops=1000, bytes_accessed=1000, transcendentals=0),
+    )(*ns, *cs, weights, weights, weights, *before)
+
+
+def ffn_grad_kernel(nb, calls, *refs):
+    ns, cs = refs[:nb], refs[nb : 2 * nb]
+    zs, gs, us = (refs[2 * nb + k * calls : 2 * nb + (k + 1) * calls] for k in range(3))
+    out, n_ref, c_ref = refs[-3:]
     pieces, rows, width = out.shape
     hid = rows // 3
-    for which, (left, right) in enumerate(((gs, ns), (us, ns), (zs, cs))):
-        total = dot(left[0][...], right[0][...], TN)
-        for b in range(1, nb):
-            total += dot(left[b][...], right[b][...], TN)
+    own_rows = ns[0].shape[0]
+
+    @pl.when(pl.program_id(0) == 0)
+    def _():
+        for b in range(nb):
+            n_ref[b * own_rows : (b + 1) * own_rows] = ns[b][...]
+            c_ref[b * own_rows : (b + 1) * own_rows] = cs[b][...]
+
+    for which, (left, right) in enumerate(((gs, n_ref), (us, n_ref), (zs, c_ref))):
+        total, at = None, 0
+        for ref in left:
+            block = ref[...].reshape(-1, ref.shape[-1])
+            made = dot(block, right[at : at + block.shape[0]], TN)
+            total = made if total is None else total + made
+            at += block.shape[0]
         out[:, which * hid : (which + 1) * hid] = total.astype(jnp.bfloat16).reshape(pieces, hid, width)
 
 
 def ffn_grad(ns, cs, zs, gs, us, n_t):
     nb = len(ns)
-    width = ns[0].shape[1]
-    total = zs[0].shape[1]
+    rows, width = ns[0].shape
+    total = zs[0].shape[2]
     hid = total // n_t
-    rows = sum(n.shape[0] for n in ns)
-    full = [pl.BlockSpec(n.shape, lambda s: (0, 0)) for n in ns]
-    col = [pl.BlockSpec((n.shape[0], HT), lambda s: (0, s)) for n in ns]
+    tile = hid if hid % 128 == 0 else hid * (128 // math.gcd(hid, 128))
+    tile = tile * max(HT // tile, 1)
+    full = [pl.BlockSpec((rows, width), lambda s: (0, 0), pipeline_mode=pl.Buffered(1))] * nb
+    col = [pl.BlockSpec((z.shape[0], rows, tile), lambda s: (0, 0, s)) for z in zs]
     return pl.pallas_call(
-        functools.partial(ffn_grad_kernel, nb),
+        functools.partial(ffn_grad_kernel, nb, len(zs)),
         name="ffn_grad",
-        grid=(total // HT,),
+        grid=(total // tile,),
         out_shape=jax.ShapeDtypeStruct((n_t, 3 * hid, width), jnp.bfloat16),
         in_specs=full * 2 + col * 3,
-        out_specs=pl.BlockSpec((HT // hid, 3 * hid, width), lambda s: (s, 0, 0)),
+        out_specs=pl.BlockSpec((tile // hid, 3 * hid, width), lambda s: (s, 0, 0)),
+        scratch_shapes=[pltpu.VMEM((nb * rows, width), jnp.bfloat16)] * 2,
         compiler_params=pltpu.CompilerParams(vmem_limit_bytes=56 << 20),
-        cost_estimate=pl.CostEstimate(
-            flops=2 * rows * width * total * 3, bytes_accessed=20 * 10**6, transcendentals=0
-        ),
+        cost_estimate=pl.CostEstimate(flops=1000, bytes_accessed=1000, transcendentals=0),
     )(*ns, *cs, *zs, *gs, *us)
 
 
@@ -293,8 +325,82 @@
             ],
         ),
         compiler_params=pltpu.CompilerParams(vmem_limit_bytes=40 << 20),
-        cost_estimate=pl.CostEstimate(flops=4 * 10**9, bytes_accessed=14 * 10**6, transcendentals=0),
+        cost_estimate=pl.CostEstimate(flops=1000, bytes_accessed=1000, transcendentals=0),
     )(order, grad_qkv, all1, w_qkv, gains, heads_own, grad_bf)
+
+
+def arrive_kernel(order_ref, one_ref, two_ref, gains_ref, w_ref, *refs):
+    all_ref, qkv_ref = refs[-2:]
+
+    def work(source):
+        value = source[...].astype(jnp.float32)
+        scale = lax.rsqrt(jnp.mean(value * value, axis=-1, keepdims=True) + EPS)
+        normed = (value * scale * gains_ref[0:1]).astype(jnp.bfloat16)
+        all_ref[...] = normed
+        qkv_ref[...] = dot(normed, w_ref[...], NT).astype(jnp.bfloat16)
+
+    @pl.when(pl.program_id(0) == 0)
+    def _():
+        work(one_ref)
+
+    @pl.when(pl.program_id(0) == 1)
+    def _():
+        work(two_ref)
+
+
+def arrive(order, one, two, gains, w_qkv, rows, state):
+    half, width = one.shape
+    cols = w_qkv.shape[0]
+    whole = lambda x: pl.BlockSpec(x.shape, lambda i, o: (0, 0))
+    old = () if state is None else state
+    return pl.pallas_call(
+        arrive_kernel,
+        name="arrive",
+        out_shape=(
+            pltpu.HBM((rows, width), jnp.bfloat16),
+            pltpu.HBM((rows, cols), jnp.bfloat16),
+        ),
+        grid_spec=pltpu.PrefetchScalarGridSpec(
+            num_scalar_prefetch=1,
+            grid=(2,),
+            in_specs=[whole(one), whole(two), whole(gains), whole(w_qkv)]
+            + [pl.BlockSpec(memory_space=pltpu.HBM)] * len(old),
+            out_specs=[
+                pl.BlockSpec((half, width), lambda i, o: (o[i], 0)),
+                pl.BlockSpec((half, cols), lambda i, o: (o[i], 0)),
+            ],
+        ),
+        input_output_aliases={5 + k: k for k in range(len(old))},
+        compiler_params=pltpu.CompilerParams(vmem_limit_bytes=24 << 20),
+        cost_estimate=pl.CostEstimate(flops=1000, bytes_accessed=1000, transcendentals=0),
+    )(order, one, two, gains, w_qkv, *old)
+
+
+def join_kernel(pieces, order_ref, *refs):
+    out_ref = refs[-1]
+    for k in range(pieces):
+
+        @pl.when(pl.program_id(0) == k)
+        def _():
+            out_ref[...] = refs[k][...]
+
+
+def join(order, pieces):
+    rows, part = pieces[0].shape
+    n = len(pieces)
+    return pl.pallas_call(
+        functools.partial(join_kernel, n),
+        name="join",
+        out_shape=jax.ShapeDtypeStruct((rows, n * part), pieces[0].dtype),
+        grid_spec=pltpu.PrefetchScalarGridSpec(
+            num_scalar_prefetch=1,
+            grid=(n,),
+            in_specs=[pl.BlockSpec((rows, part), lambda i, o: (0, 0))] * n,
+            out_specs=pl.BlockSpec((rows, part), lambda i, o: (0, o[i])),
+        ),
+        compiler_params=pltpu.CompilerParams(vmem_limit_bytes=16 << 20),
+        cost_estimate=pl.CostEstimate(flops=1000, bytes_accessed=1000, transcendentals=0),
+    )(order, *pieces)
 
 
 def blank(shape, dtype):
@@ -335,7 +441,7 @@
         return lax.ppermute(value, "tensor", [(i, i ^ k) for i in range(n_t)])
 
     bits = [1 << b for b in range(n_dp.bit_length() - 1)]
-    t_bits = [1 << b for b in range(n_t.bit_length() - 2, -1, -1)]
+    t_bits = [1 << b for b in range(n_t.bit_length() - 1)]
     n_ff = min(n_dp, 4)
     ff_bits = [b for b in bits if b < n_ff]
     put = lax.dynamic_update_slice_in_dim
@@ -359,12 +465,10 @@
             arranged = arranged[..., :cut] + flip(arranged[..., cut:].astype(send_type), bit).astype(f32)
         return arranged
 
-    def scatter_sum_t(value, t, send_type):
-        for bit in t_bits:
-            halves = value.reshape((2, -1) + value.shape[1:])
-            side = (t // bit) % 2
-            value = pick(halves, side, 0) + flip_t(pick(halves, 1 - side, 0).astype(send_type), bit).astype(f32)
-        return value[0]
+    def fold_t(value, t, bit, send_type):
+        halves = value.reshape((-1, 2) + value.shape[1:])
+        side = (t // bit) % 2
+        return pick(halves, side, 1) + flip_t(pick(halves, 1 - side, 1).astype(send_type), bit).astype(f32)
 
     def on_device(
         tokens, seq_ids, blk_ids, norm1_gain, w_query, w_key, w_value, w_out, norm2_gain,
@@ -386,11 +490,6 @@
         half = own_rows // 2
         part = width // n_dp
         wide = w_query.shape[1]
-
-        one, two = [tokens[:half]], [tokens[half:]]
-        for k in range(1, n_t):
-            one.append(hop(one[-1], 1))
-            two.append(hop(two[-1], -1))
 
         def gather_dp(piece):
             whole = put(jnp.zeros((piece.shape[0], width), bf), piece, d * part, 1)
@@ -408,6 +507,13 @@
                 ]
             )
         )
+        one, two = [tokens[:half]], [tokens[half:]]
+        for k in range(1, n_t):
+            got = [hop(one[-1], 1), hop(two[-1], -1)]
+            if k == COMMON_AT:
+                got[0], got[1], common = lax.optimization_barrier((*got, common))
+            one.append(got[0])
+            two.append(got[1])
         w_qkv = common[: 3 * wide]
         gains = common[3 * wide :].astype(f32)
         gain1, gain2 = gains[0:1], gains[1:2]
@@ -416,11 +522,12 @@
         hid = hid_t // n_ff
         out_half = wide // 2
         core = d % 2
+        cuts = (hid * 3 // 4, hid - hid * 3 // 4)
+        thirds = [w.reshape(n_ff, hid, part) for w in (w_gate.T, w_up.T, w_down)]
         shards = jnp.concatenate(
             [
-                w_gate.T.reshape(n_ff, hid, part),
-                w_up.T.reshape(n_ff, hid, part),
-                w_down.reshape(n_ff, hid, part),
+                *(w[:, : cuts[0]] for w in thirds),
+                *(w[:, cuts[0] :] for w in thirds),
                 jnp.tile(w_out.reshape(2, out_half, part), (n_ff // 2, 1, 1)),
             ],
             axis=1,
@@ -437,7 +544,7 @@
 
         cot_far = cotangent[None]
         for bit in ff_bits[:0:-1]:
-            cot_far = jnp.concatenate([cot_far, flip(after(cot_far, one[2]), bit)])
+            cot_far = jnp.concatenate([cot_far, flip(after(cot_far, one[COT_AT]), bit)])
 
         resid = tokens.astype(f32)
         scale1 = row_scale(resid)
@@ -461,7 +568,8 @@
             qkv = put(qkv, made[half:], ahead[k] * own_rows + half, 0)
 
         o_mine = lax.all_gather(own_o, "tensor", axis=0)
-        weights = lax.all_gather(own_w, "tensor", axis=0)
+        cut_w = 3 * cuts[0]
+        weights = [lax.all_gather(piece, "tensor", axis=0) for piece in (own_w[:cut_w], own_w[cut_w:])]
         o_mine = after(o_mine, qkv)
         o_peer = flip(o_mine, 1)
         out_full = jnp.where(
@@ -470,8 +578,9 @@
             jnp.concatenate([o_peer, o_mine], axis=1),
         ).reshape(n_t * wide, width)
         cot_far = after(cot_far, qkv)
-        c_near = jnp.concatenate([cotangent[None], flip(cot_far[:1], 1)])
-        c_far = jnp.concatenate([cot_far[1:], flip(cot_far[1:], 1)])
+        c_near = [cotangent, flip(cot_far[0], 1)]
+        c_far = [cot_far[m] for m in range(1, n_ff // 2)]
+        c_far += [flip(c, 1) for c in c_far]
 
         units = seq_ids.reshape(-1, 4 * BLK)[:, 0]
         n_units = rows // (4 * BLK)
@@ -489,38 +598,56 @@
         mixed = resid + jnp.dot(heads_own, out_full, preferred_element_type=f32)
         scale2 = row_scale(mixed)
         normed2 = (mixed * scale2 * gain2).astype(bf)
+        normed2, all1 = lax.optimization_barrier((normed2, all1))
 
         n_far = normed2[None]
         for bit in ff_bits[:0:-1]:
             n_far = jnp.concatenate([n_far, flip(n_far, bit)])
-        n_near = jnp.concatenate([normed2[None], flip(normed2[None], 1)])
-        f_near, d_near, z_near, g_near, u_near = ffn(n_near, c_near, weights, hid)
+        n_near = [normed2, flip(normed2, 1)]
+        f_near, d_near, *left_near = ffn(n_near, c_near, weights[0], cuts[0])
         n_far = after(n_far[1:], d_near)
-        n_far = jnp.concatenate([n_far, flip(n_far, 1)])
-        f_far, d_far, z_far, g_far, u_far = ffn(n_far, c_far, weights, hid)
+        n_far = [n_far[m] for m in range(n_ff // 2 - 1)]
+        n_far += [flip(n, 1) for n in n_far]
+        f_far, d_far, *left_far = ffn(n_far, c_far, weights[0], cuts[0])
+
+        def grad_w(near, far):
+            return ffn_grad(n_near + n_far, c_near + c_far, *zip(near, far), n_t)
+
+        def sum_w(grads):
+            return lax.psum_scatter(grads.reshape(-1, width), "tensor", scatter_dimension=0, tiled=True)
+
+        first_w = grad_w(left_near, left_far)
+        half_sums = [sum_w(first_w)]
+        later_w = after(weights[1], first_w)
+        f_near, d_near, *left_near = ffn(n_near, c_near, later_w, cuts[1], (f_near, d_near))
+        f_far, d_far, *left_far = ffn(n_far, c_far, later_w, cuts[1], (f_far, d_far))
 
         def fold_core(near, far):
             cut = far.shape[0] // 2
             far_sum = far[:cut].astype(f32) + flip(far[cut:], 1).astype(f32)
             near_sum = near[:1].astype(f32) + flip(near[1:], 1).astype(f32)
-            return jnp.concatenate([near_sum, far_sum])
-
-        def fold_far(acc, *late):
+            return near_sum, far_sum
+
+        def fold_far(near_sum, far_sum, beside=None):
+            acc = jnp.concatenate([near_sum, far_sum])
+            made = None
             for bit in ff_bits[1:]:
                 cut = acc.shape[0] // 2
-                got = flip(acc[cut:].astype(bf), bit)
-                acc = acc[:cut] + (after(got, *late) if bit == ff_bits[-1] else got).astype(f32)
-            return acc[0]
-
-        grad_w = ffn_grad(
-            [n_near.reshape(-1, width), n_far.reshape(-1, width)],
-            [c_near.reshape(-1, width), c_far.reshape(-1, width)],
-            [z.reshape(-1, z.shape[-1]) for z in (z_near, z_far)],
-            [g.reshape(-1, g.shape[-1]) for g in (g_near, g_far)],
-            [u.reshape(-1, u.shape[-1]) for u in (u_near, u_far)],
-            n_t,
-        )
-        grad_normed2 = fold_far(fold_core(d_near, d_far), grad_w)
+                sent = acc[cut:].astype(bf)
+                if beside is not None and bit == ff_bits[-1]:
+                    sent, made = beside(sent)
+                got = flip(sent, bit)
+                if made is not None:
+                    got = after(got, made)
+                acc = acc[:cut] + got.astype(f32)
+            return acc[0], made
+
+        def grad_w_beside(sent):
+            sent, *left = lax.optimization_barrier((sent, *left_near, *left_far))
+            return sent, grad_w(left[:3], left[3:])
+
+        grad_normed2, second_w = fold_far(*fold_core(d_near, d_far), grad_w_beside)
+        half_sums.append(sum_w(after(second_w, grad_normed2)))
 
         cot = cotangent.astype(f32)
         grad_mixed = cot + norm_back(grad_normed2, mixed, scale2, gain2)
@@ -532,75 +659,120 @@
         for j in range(1, n_t):
             piece = hop(take(grad_heads, ahead[j] * wide, wide, 1), j)
             grad_att = put(grad_att, piece, behind[j] * own_rows, 0)
-        f_folded = after(fold_core(f_near, f_far), grad_heads)
         grad_qkv = attn_bwd(qkv, grad_att, attended, logs, first)
-        output = (mixed + fold_far(f_folded, grad_qkv)).astype(bf)
-        summed = lax.psum_scatter(
-            (after(grad_w, grad_att) if RS_LATE else grad_w).reshape(-1, width),
-            "tensor", scatter_dimension=0, tiled=True,
-        )
-
-        def back_rows(k):
+        def back_rows(k, *late):
+            source = after(grad_qkv, *late)
             pair = jnp.concatenate(
                 [
-                    take(grad_qkv, behind[k] * own_rows, half, 0),
-                    take(grad_qkv, ahead[k] * own_rows + half, half, 0),
+                    take(source, behind[k] * own_rows, half, 0),
+                    take(source, ahead[k] * own_rows + half, half, 0),
                 ]
             )
             made = jnp.dot(pair, w_qkv, preferred_element_type=f32)
             return lax.optimization_barrier(made.astype(bf))
 
+        grad_gain2 = jnp.sum(grad_normed2 * mixed * scale2, axis=0, keepdims=True)
+        gain_rows = jnp.concatenate([gain1, grad_gain2, jnp.zeros((6, width), f32)])
+
+        def first_late(source):
+            if part % 128 == 0:
+                order = jnp.stack([d ^ k for k in dp_order]).astype(jnp.int32)
+                return late_grads(order, source, all1, w_qkv, gain_rows, heads_own, grad_bf)
+            grad_wqkv = lax.dot_general(source, all1, TN, preferred_element_type=f32)
+            grad_gain1 = jnp.sum(grad_wqkv * w_qkv.astype(f32), axis=0, keepdims=True) / gain1
+            grad_wo = lax.dot_general(heads_own, grad_bf, TN, preferred_element_type=f32)
+            gain_grads = jnp.concatenate([grad_gain1, grad_gain2, jnp.zeros((14, width), f32)])
+            both = arrange(jnp.concatenate([grad_wqkv, gain_grads, grad_wo]), d)
+            return both[:, : width // 2], both[:, width // 2 :].astype(bf)
+
+        def spread(summed):
+            summed = jnp.concatenate(
+                [m.reshape(3, -1, width) for m in summed], axis=1
+            ).reshape(3, hid, n_dp, part)
+            totals = []
+            for k in range(n_ff):
+                total = 0.0
+                for far in range(k, n_dp, n_ff):
+                    piece = pick(summed, d ^ far, 2)[:, None]
+                    total = total + (flip(piece, far) if far else piece).astype(f32)
+                totals.append(total)
+            return totals
+
         made = back_rows(n_t - 1)
         up, down = [made[:half]], [made[half:]]
-        for k in range(n_t - 2, -1, -1):
+        keep = send = parts = got = None
+        left = list(bits)
+        tensor_left = list(t_bits)
+        for step in range(1, n_t):
+            k = n_t - 1 - step
             got_up, got_down = hop(up[-1], -1), hop(down[-1], 1)
-            made = back_rows(k).astype(f32)
-            up.append(got_up.astype(f32) + made[:half])
-            down.append(got_down.astype(f32) + made[half:])
+            made = back_rows(k, up[max(step - 2, 0)]).astype(f32)
+            new_up, new_down = got_up.astype(f32) + made[:half], got_down.astype(f32) + made[half:]
             if k:
-                up[-1], down[-1] = up[-1].astype(bf), down[-1].astype(bf)
-        grad_normed1 = jnp.concatenate([up[-1], down[-1]])
-        input_grad = (grad_mixed + norm_back(grad_normed1, resid, scale1, gain1)).astype(bf)
-
-        grad_gain2 = jnp.sum(grad_normed2 * mixed * scale2, axis=0, keepdims=True)
-        gain_rows = jnp.concatenate([gain1, grad_gain2, jnp.zeros((6, width), f32)])
-        if part % 128 == 0:
-            order = jnp.stack([d ^ k for k in dp_order]).astype(jnp.int32)
-            keep, send = late_grads(order, grad_qkv, all1, w_qkv, gain_rows, heads_own, grad_bf)
-        else:
-            grad_wqkv = lax.dot_general(grad_qkv, all1, TN, preferred_element_type=f32)
-            grad_gain1 = jnp.sum(grad_wqkv * w_qkv.astype(f32), axis=0, keepdims=True) / gain1
-            grad_wo = lax.dot_general(heads_own, grad_bf, TN, preferred_element_type=f32)
-            gain_rows = jnp.concatenate([grad_gain1, grad_gain2, jnp.zeros((14, width), f32)])
-            both = arrange(jnp.concatenate([grad_wqkv, gain_rows, grad_wo]), d)
-            keep, send = both[:, : width // 2], both[:, width // 2 :].astype(bf)
-        stage = 1
-        for bit in bits:
-            send = after(send, up[min(stage, n_t - 2)])
-            got = after(flip(send, bit), up[min(stage + 1, n_t - 2)])
-            stage += 1 if bit == 1 else 2
-            keep = keep + got.astype(f32)
+                new_up, new_down = new_up.astype(bf), new_down.astype(bf)
+            if step == 1:
+                keep, send = first_late(grad_qkv)
+                new_up, new_down, keep, send = lax.optimization_barrier((new_up, new_down, keep, send))
+            elif left:
+                bit = left[0]
+                if got is None:
+                    got = flip(send, bit)
+                    wait = 0 if bit == 1 else 1
+                else:
+                    wait -= 1
+                if wait == 0:
+                    new_up, new_down, got = lax.optimization_barrier((new_up, new_down, got))
+                    keep = keep + got.astype(f32)
+                    cut = keep.shape[1] // 2
+                    if cut >= part:
+                        keep, send = keep[:, :cut], keep[:, cut:].astype(bf)
+                    left.pop(0)
+                    got = None
+            elif tensor_left:
+                if parts is None:
+                    gain_sums = jnp.broadcast_to(keep[3 * wide : 3 * wide + 16], (n_t, 16, part))
+                    parts = jnp.concatenate([keep[3 * wide + 16 :].reshape(n_t, wide, part), gain_sums], axis=1)
+                parts = fold_t(parts, t, tensor_left.pop(0), bf)
+                new_up, new_down, parts = lax.optimization_barrier((new_up, new_down, parts))
+            if step == FOLD_AT:
+                near, far = lax.optimization_barrier((f_near, f_far, up[-1]))[:2]
+                folded = fold_core(near, far)
+                new_up, new_down, *folded = lax.optimization_barrier((new_up, new_down, *folded))
+            if step == FAR_AT:
+                ffn_total = fold_far(*lax.optimization_barrier((*folded, up[-1]))[:2])[0]
+            if step == FAR_AT + 2:
+                new_up, new_down, ffn_total = lax.optimization_barrier((new_up, new_down, ffn_total))
+            if step == FIRST_AT:
+                new_up, new_down, half_sums[0] = lax.optimization_barrier((new_up, new_down, half_sums[0]))
+            if step == SPREAD_AT:
+                new_up, new_down, half_sums[1] = lax.optimization_barrier((new_up, new_down, half_sums[1]))
+                totals = spread(half_sums)
+            up.append(new_up)
+            down.append(new_down)
+        output = (mixed + ffn_total).astype(bf)
+        for bit in left:
+            keep = keep + (flip(send, bit) if got is None else got).astype(f32)
+            got = None
             cut = keep.shape[1] // 2
             if cut >= part:
                 keep, send = keep[:, :cut], keep[:, cut:].astype(bf)
+        if parts is None:
+            gain_sums = jnp.broadcast_to(keep[3 * wide : 3 * wide + 16], (n_t, 16, part))
+            parts = jnp.concatenate([keep[3 * wide + 16 :].reshape(n_t, wide, part), gain_sums], axis=1)
+        for bit in tensor_left:
+            parts = fold_t(parts, t, bit, bf)
+        mine = parts[0]
+        grad_normed1 = jnp.concatenate([up[-1], down[-1]])
+        input_grad = (grad_mixed + norm_back(grad_normed1, resid, scale1, gain1)).astype(bf)
         grad_query, grad_key, grad_value = (keep[k * wide : (k + 1) * wide].T for k in range(3))
-        gain_sums = jnp.broadcast_to(keep[3 * wide : 3 * wide + 16], (n_t, 16, part))
-        parts = jnp.concatenate([keep[3 * wide + 16 :].reshape(n_t, wide, part), gain_sums], axis=1)
-        mine = scatter_sum_t(parts, t, bf)
         grad_out = mine[:wide]
         share = part // n_t
         grad_norm1 = take(mine[wide], t * share, share, 0)
         grad_norm2 = take(mine[wide + 1], t * share, share, 0)
 
-        summed = after(summed, up[2]).reshape(3, hid, n_dp, part)
         full = blank((3, n_ff, hid, part), f32)
         for k in range(n_ff):
-            total = 0.0
-            for far in range(k, n_dp, n_ff):
-                piece = pick(summed, d ^ far, 2)[:, None]
-                piece = after(flip(piece, far), up[5]) if far else piece
-                total = total + piece.astype(f32)
-            full = put(full, total, (d ^ k) % n_ff, 1)
+            full = put(full, totals[k], (d ^ k) % n_ff, 1)
         full = full.reshape(3, hid_t, part)
 
         return (

time: 542 us -> 506 us (0.934)
  waiting for transfers between devices: 191 us -> 150 us
  Pallas kernels: 118 us -> 134 us
  starting transfers between devices: 86.7 us -> 71.6 us
    ppermute x42, waiting for transfers between devices: 138 us -> 96.8 us  [hop(): lax.ppermute(value, 'tensor', [(ring[i], ring[(i + k) % n_t]) for i in ra...]
    ppermute x24, waiting for transfers between devices: 23 us -> 45.2 us  [flip(): return lax.ppermute(value, 'dp', [(i, i ^ k) for i in range(n_dp)])]
    pallas_call x3 -> x6, Pallas kernels: 47.3 us -> 62.7 us  [the longest x4 41.4 us: ffn(): pl.pallas_call(functools.partial(ffn_kernel, nb), name='ffn', grid=(nb,),...]
    all_gather x1 -> x2, waiting for transfers between devices: 13.5 us -> 0.02 us  [on_device(): lax.all_gather(piece, 'tensor', axis=0)]
    concatenate x6 -> x1, other arithmetic: 11.8 us -> 1.52 us  [on_device(): cot_far = jnp.concatenate([cot_far, flip(after(cot_far, one[COT_AT]), bit)])]
    convert_element_type x16, other arithmetic: 6.15 us -> 16 us  [the longest x6 6.99 us: on_device(): new_up, new_down = (new_up.astype(bf), new_down.astype(bf))]
    ppermute x3, waiting for transfers between devices: 16.5 us -> 7.73 us  [flip_t(): return lax.ppermute(value, 'tensor', [(i, i ^ k) for i in range(n_t)])]
    ppermute x42, starting transfers between devices: 67.9 us -> 61 us  [hop(): lax.ppermute(value, 'tensor', [(ring[i], ring[(i + k) % n_t]) for i in ra...]
  transfers between devices with their start and end apart: 72 -> 74, of which waited for: 36 -> 37; matrix products, arithmetic and copies ran while one was open for 18% -> 23% of each run, Pallas kernels for 19% -> 27%
where the time goes in v3:
time: 506 us; the launch traced here: 499 us
  waiting for transfers between devices  150 us (30%)
  Pallas kernels  134 us (26%)
  starting transfers between devices  71.6 us (14%)
  local copies, waits for them, and re-layouts  64 us (13%)
  other arithmetic  50.6 us (10%)
  between operations  16 us (3%)
  matrix products  13.2 us (3%)
    ppermute x42, waiting for transfers between devices, hop(): lax.ppermute(value, 'tensor', [(ring[i], ring[(i + k) % n_t]) for i in ra...  96.8 us
    ppermute x42, starting transfers between devices, hop(): lax.ppermute(value, 'tensor', [(ring[i], ring[(i + k) % n_t]) for i in ra...  61 us
    ppermute x24, waiting for transfers between devices, flip(): return lax.ppermute(value, 'dp', [(i, i ^ k) for i in range(n_dp)])  45.2 us
    pallas_call x4, Pallas kernels, ffn(): pl.pallas_call(functools.partial(ffn_kernel, nb), name='ffn', grid=(nb,),...  41.4 us
    pallas_call x1, Pallas kernels, attn_bwd(): pl.pallas_call(attn_bwd_kernel, name='attn_bwd', out_shape=jax.ShapeDtype...  37.1 us
    pallas_call x1, Pallas kernels, attn_fwd(): pl.pallas_call(attn_fwd_kernel, name='attn_fwd', out_shape=(jax.ShapeDtyp...  26 us
    pallas_call x2, Pallas kernels, ffn_grad(): pl.pallas_call(functools.partial(ffn_grad_kernel, nb, len(zs)), name='ffn...  21.3 us
    unnamed x155, local copies, waits for them, and re-layouts  14.1 us
  transfers between devices with their start and end apart: 74, of which 37 were waited for; matrix products, arithmetic and copies ran while one was open for 23% of the time, Pallas kernels for 27%

profile of v3, /device:TPU:0, one launch (start us, length us, event | category | flops | bytes accessed | tf_op | source)
XLA Modules:
  0.0 499.5 jit_solution(3162658037881315314)
XLA Ops:
  8.5 3.1 collective-permute-start
  12.0 8.7 %collective-permute-done = bf16[192,1024]{1,0:T(8,128)(2,1)S(1)} collective-permute-done((bf16[192,1024]{1,0:T(8,128)(2,1)S(1)}, bf16[192,1024]{1,0:T(8,128)(2,1)S(1)}, u32[]{:S(2)}, u32[]{:S(2)}) %collective-permute-start) | collective-permute-done | bytes 393248 | tf_op jit(solution)/shard_map/ppermute | solution.py:435
  23.6 7.3 %collective-permute-done.1 = bf16[192,1024]{1,0:T(8,128)(2,1)S(1)} collective-permute-done((bf16[192,1024]{1,0:T(8,128)(2,1)S(1)}, bf16[192,1024]{1,0:T(8,128)(2,1)S(1)}, u32[]{:S(2)}, u32[]{:S(2)}) %collective-permute-start.1) | collective-permute-done | bytes 393248 | tf_op jit(solution)/shard_map/ppermute | solution.py:435
  38.5 6.7 %collective-permute-done.25 = bf16[448,256]{1,0:T(8,128)(2,1)S(1)} collective-permute-done((bf16[448,256]{1,0:T(8,128)(2,1)}, bf16[448,256]{1,0:T(8,128)(2,1)S(1)}, u32[]{:S(2)}, u32[]{:S(2)}) %collective-permute-start.25) | collective-permute-done | bytes 229408 | tf_op jit(solution)/shard_map/ppermute | solution.py:438
  45.2 4.1 collective-permute-done.26
  56.5 4.4 collective-permute-done.9
  61.0 3.1 collective-permute-done.10
  64.1 2.8 collective-permute-done.3
  70.4 8.1 %collective-permute-done.11 = bf16[192,1024]{1,0:T(8,128)(2,1)} collective-permute-done((bf16[192,1024]{1,0:T(8,128)(2,1)S(1)}, bf16[192,1024]{1,0:T(8,128)(2,1)}, u32[]{:S(2)}, u32[]{:S(2)}) %collective-permute-start.11) | collective-permute-done | bytes 393248 | tf_op jit(solution)/shard_map/ppermute | solution.py:435
  78.5 2.4 collective-permute-done.12
  93.7 5.5 %collective-permute-done.13 = bf16[192,1024]{1,0:T(8,128)(2,1)S(1)} collective-permute-done((bf16[192,1024]{1,0:T(8,128)(2,1)}, bf16[192,1024]{1,0:T(8,128)(2,1)S(1)}, u32[]{:S(2)}, u32[]{:S(2)}) %collective-permute-start.13) | collective-permute-done | bytes 393248 | tf_op jit(solution)/shard_map/ppermute | solution.py:435
  105.0 11.8 %collective-permute-done.15 = bf16[192,1024]{1,0:T(8,128)(2,1)S(1)} collective-permute-done((bf16[192,1024]{1,0:T(8,128)(2,1)S(1)}, bf16[192,1024]{1,0:T(8,128)(2,1)S(1)}, u32[]{:S(2)}, u32[]{:S(2)}) %collective-permute-start.15) | collective-permute-done | bytes 393248 | tf_op jit(solution)/shard_map/ppermute | solution.py:435
  116.8 9.2 %collective-permute-done.16 = bf16[192,1024]{1,0:T(8,128)(2,1)S(1)} collective-permute-done((bf16[192,1024]{1,0:T(8,128)(2,1)S(1)}, bf16[192,1024]{1,0:T(8,128)(2,1)S(1)}, u32[]{:S(2)}, u32[]{:S(2)}) %collective-permute-start.16) | collective-permute-done | bytes 393248 | tf_op jit(solution)/shard_map/ppermute | solution.py:435
  126.3 3.7 fusion.20
  142.7 26.0 %attn_fwd.1 = (bf16[3072,128]{1,0:T(8,128)(2,1)S(1)}, f32[12,1,512]{2,1,0:T(1,128)S(1)}) custom-call(s32[12]{0:T(128)S(1)} %reshape.202.first_ref, bf16[3072,384]{1,0:T(8,128)(2,1)S(1)} %slice_dynamic-update-slice_fusion.17.qkv_ref), custom_call_target="tpu_custom_call" | custom-call | flops 1000 | bytes 1000 | tf_op jit(solution)/shard_map/attn_fwd/pallas_call | solution.py:99
  171.5 3.3 collective-permute-start.20
  179.0 3.5 collective-permute-start.21
  184.0 7.8 %collective-permute-done.18 = bf16[384,128]{1,0:T(8,128)(2,1)} collective-permute-done((bf16[384,128]{1,0:T(8,128)(2,1)}, bf16[384,128]{1,0:T(8,128)(2,1)}, u32[]{:S(2)}, u32[]{:S(2)}) %collective-permute-start.18) | collective-permute-done | bytes 98336 | tf_op jit(solution)/shard_map/ppermute | solution.py:435
  200.2 2.8 multiply_reduce_fusion.2
  204.8 2.5 collective-permute-done.28.refs_1_
  207.3 12.8 %ffn.4 = (bf16[2,384,1024]{2,1,0:T(8,128)(2,1)}, bf16[2,384,1024]{2,1,0:T(8,128)(2,1)}, bf16[2,384,768]{2,1,0:T(8,128)(2,1)}, bf16[2,384,768]{2,1,0:T(8,128)(2,1)}, bf16[2,384,768]{2,1,0:T(8,128)(2,1)}) custom-call(bf16[384,1024]{1,0:T(8,128)(2,1)} %multiply_convert_fusion.refs_0_, bf16[384,1024]{1,0:T(8,128)(2,1)} %collective-permute-done.28.refs_1_, ...), custom_call_target="tpu_custom_call" | custom-call | flops 1000 | bytes 1000 | tf_op jit(solution)/shard_map/ffn/pallas_call | solution.py:220
  220.0 4.5 collective-permute-done.31
  224.5 2.5 collective-permute-done.32.refs_1_.refs_3_
  227.9 12.5 %ffn.5 = (bf16[2,384,1024]{2,1,0:T(8,128)(2,1)}, bf16[2,384,1024]{2,1,0:T(8,128)(2,1)}, bf16[2,384,768]{2,1,0:T(8,128)(2,1)}, bf16[2,384,768]{2,1,0:T(8,128)(2,1)}, bf16[2,384,768]{2,1,0:T(8,128)(2,1)}) custom-call(bf16[384,1024]{1,0:T(8,128)(2,1)} %bitcast.19.refs_0_.refs_2_, bf16[384,1024]{1,0:T(8,128)(2,1)} %copy-done.12, bf16[384,1024]{1,0:T(8,128)(2,1)} %copy-done.8, ...), custom_call_target="tpu_custom_call" | custom-call | flops 1000 | bytes 1000 | tf_op jit(solution)/shard_map/ffn/pallas_call | solution.py:220
  240.4 13.8 %ffn_grad.2 = bf16[8,288,1024]{2,1,0:T(8,128)(2,1)} custom-call(bf16[384,1024]{1,0:T(8,128)(2,1)} %multiply_convert_fusion.refs_0_, bf16[384,1024]{1,0:T(8,128)(2,1)} %collective-permute-done.28.refs_1_, bf16[384,1024]{1,0:T(8,128)(2,1)} %bitcast.19.refs_0_.refs_2_, bf16[384,1024]{1,0:T(8,128)(2,1)} %copy-done.12, bf16[384,1024]{1,0:T(8,128)(2,1)} %refs_4_.3, ...), custom_call_target="tpu_custom_call" | custom-call | flops 1000 | bytes 1000 | tf_op jit(solution)/shard_map/ffn_grad/pallas_call | solution.py:267
  254.3 8.1 %ffn.7 = (bf16[2,384,1024]{2,1,0:T(8,128)(2,1)}, bf16[2,384,1024]{2,1,0:T(8,128)(2,1)}, bf16[2,384,256]{2,1,0:T(8,128)(2,1)}, bf16[2,384,256]{2,1,0:T(8,128)(2,1)}, bf16[2,384,256]{2,1,0:T(8,128)(2,1)}) custom-call(bf16[384,1024]{1,0:T(8,128)(2,1)} %bitcast.19.refs_0_.refs_2_, bf16[384,1024]{1,0:T(8,128)(2,1)} %copy-done.12, bf16[384,1024]{1,0:T(8,128)(2,1)} %copy-done.8, ...), custom_call_target="tpu_custom_call" | custom-call | flops 1000 | bytes 1000 | tf_op jit(solution)/shard_map/ffn/pallas_call | solution.py:220
  263.9 8.0 %ffn.6 = (bf16[2,384,1024]{2,1,0:T(8,128)(2,1)}, bf16[2,384,1024]{2,1,0:T(8,128)(2,1)}, bf16[2,384,256]{2,1,0:T(8,128)(2,1)}, bf16[2,384,256]{2,1,0:T(8,128)(2,1)}, bf16[2,384,256]{2,1,0:T(8,128)(2,1)}) custom-call(bf16[384,1024]{1,0:T(8,128)(2,1)} %multiply_convert_fusion.refs_0_, bf16[384,1024]{1,0:T(8,128)(2,1)} %collective-permute-done.28.refs_1_, ...), custom_call_target="tpu_custom_call" | custom-call | flops 1000 | bytes 1000 | tf_op jit(solution)/shard_map/ffn/pallas_call | solution.py:220
  275.0 7.5 %ffn_grad.3 = bf16[8,96,1024]{2,1,0:T(8,128)(2,1)} custom-call(bf16[384,1024]{1,0:T(8,128)(2,1)} %multiply_convert_fusion.refs_0_, bf16[384,1024]{1,0:T(8,128)(2,1)} %collective-permute-done.28.refs_1_, bf16[384,1024]{1,0:T(8,128)(2,1)} %bitcast.19.refs_0_.refs_2_, bf16[384,1024]{1,0:T(8,128)(2,1)} %copy-done.12, bf16[384,1024]{1,0:T(8,128)(2,1)} %refs_4_.3, ...), custom_call_target="tpu_custom_call" | custom-call | flops 1000 | bytes 1000 | tf_op jit(solution)/shard_map/ffn_grad/pallas_call | solution.py:267
  282.5 10.7 %collective-permute-done.36 = bf16[1,384,1024]{2,1,0:T(8,128)(2,1)S(1)} collective-permute-done((bf16[1,384,1024]{2,1,0:T(8,128)(2,1)}, bf16[1,384,1024]{2,1,0:T(8,128)(2,1)S(1)}, u32[]{:S(2)}, u32[]{:S(2)}) %collective-permute-start.36) | collective-permute-done | bytes 786464 | tf_op jit(solution)/shard_map/ppermute | solution.py:438
  295.0 2.9 fusion.101
  302.6 2.9 collective-permute-start.39
  308.9 6.5 %collective-permute-start.42 = (bf16[384,128]{1,0:T(8,128)(2,1)S(1)}, bf16[384,128]{1,0:T(8,128)(2,1)S(1)}, u32[]{:S(2)}, u32[]{:S(2)}) collective-permute-start(bf16[384,128]{1,0:T(8,128)(2,1)S(1)} %get-tuple-element.290), channel_id=1, source_target_pairs={{0,3},{2,1},{4,0},{6,2},{7,4},{5,6},{3,7},{1,5},{8,11},{10,9},{12,... | collective-permute-start | bytes 294920 | tf_op jit(solution)/shard_map/ppermute | solution.py:435
  315.4 2.9 collective-permute-start.43
  323.0 37.1 %attn_bwd.1.gq_ref = bf16[3072,384]{1,0:T(8,128)(2,1)S(1)} custom-call(s32[12]{0:T(128)S(1)} %reshape.202.first_ref, bf16[3072,384]{1,0:T(8,128)(2,1)S(1)} %copy-done.2, bf16[3072,128]{1,0:T(8,128)(2,1)S(1)} %constant_dynamic-update-slice_fusion.do_ref, bf16[3072,128]{1,0:T(8,128)(2,1)S(1)} %get-tuple-element.105.o_ref, ...), custom_call_target="tpu_custom_call" | custom-call | flops 1000 | bytes 1000 | tf_op jit(solution)/shard_map/attn_bwd/pallas_call | solution.py:159
  360.8 2.5 collective-permute-start.44
  363.4 8.5 %late_grads.1 = (f32[1424,512]{1,0:T(8,128)S(1)}, bf16[1424,512]{1,0:T(8,128)(2,1)}) custom-call(s32[4]{0:T(128)S(1)} %pad_add_fusion.order_ref, bf16[3072,384]{1,0:T(8,128)(2,1)S(1)} %attn_bwd.1.gq_ref, bf16[3072,1024]{1,0:T(8,128)(2,1)} %slice_dynamic-update-slice_fusion.all_ref, bf16[384,1024]{1,0:T(8,128)(2,1)S(1)} %slice.266.w_ref, ...), custom_call_target="tpu_custom_call" | custom-call | flops 1000 | bytes 1000 | tf_op jit(solution)/shard_map/late_grads/pallas_call | solution.py:311
  385.4 2.5 concatenate.108
  389.8 6.5 %collective-permute-done.46 = bf16[192,1024]{1,0:T(8,128)(2,1)} collective-permute-done((bf16[192,1024]{1,0:T(8,128)(2,1)}, bf16[192,1024]{1,0:T(8,128)(2,1)}, u32[]{:S(2)}, u32[]{:S(2)}) %collective-permute-start.46) | collective-permute-done | bytes 393248 | tf_op jit(solution)/shard_map/ppermute | solution.py:435
  398.4 2.4 convert_add_fusion.2
  400.8 2.8 convert_add_fusion.3
  408.2 8.9 %collective-permute-done.51 = bf16[192,1024]{1,0:T(8,128)(2,1)S(1)} collective-permute-done((bf16[192,1024]{1,0:T(8,128)(2,1)S(1)}, bf16[192,1024]{1,0:T(8,128)(2,1)S(1)}, u32[]{:S(2)}, u32[]{:S(2)}) %collective-permute-start.51) | collective-permute-done | bytes 393248 | tf_op jit(solution)/shard_map/ppermute | solution.py:435
  424.0 4.2 collective-permute-done.52
  441.9 3.4 collective-permute-done.58
  452.6 2.6 add_bitcast_fusion
  456.0 4.3 collective-permute-done.61
  462.9 3.8 collective-permute-start.63
  475.8 3.3 collective-permute-done.67
  479.1 3.3 collective-permute-done.68
  (461 shorter events, 165.0 us)
Async XLA Ops:
  7.2 171.5 %all-gather.7.cloned.1.call-start = ((), (), s32[]{:S(2)}) async-start(), calls=%async_computation.4 | async-start | bytes 1179648 | tf_op jit(solution)/shard_map/all_gather | solution.py:570
  8.5 12.1 %collective-permute-start = (bf16[192,1024]{1,0:T(8,128)(2,1)S(1)}, bf16[192,1024]{1,0:T(8,128)(2,1)S(1)}, u32[]{:S(2)}, u32[]{:S(2)}) collective-permute-start(bf16[192,1024]{1,0:T(8,128)(2,1)S(1)} %get-tuple-element.306), channel_id=1, source_target_pairs={{0,2},{2,4},{4,6},{6,7},{7,5},{5,3},{3,1},{1,0},{8,10},{10,12},{12... | collective-permute-start | bytes 1179656 | tf_op jit(solution)/shard_map/ppermute | solution.py:435
  11.6 10.9 %collective-permute-start.4 = (bf16[192,1024]{1,0:T(8,128)(2,1)S(1)}, bf16[192,1024]{1,0:T(8,128)(2,1)S(1)}, u32[]{:S(2)}, u32[]{:S(2)}) collective-permute-start(bf16[192,1024]{1,0:T(8,128)(2,1)S(1)} %get-tuple-element.305), channel_id=1, source_target_pairs={{0,1},{2,0},{4,2},{6,4},{7,6},{5,7},{3,5},{1,3},{8,9},{10,8},{12,1... | collective-permute-start | bytes 1179656 | tf_op jit(solution)/shard_map/ppermute | solution.py:435
  30.9 18.4 %collective-permute-start.2 = (bf16[192,1024]{1,0:T(8,128)(2,1)S(1)}, bf16[192,1024]{1,0:T(8,128)(2,1)S(1)}, u32[]{:S(2)}, u32[]{:S(2)}) collective-permute-start(bf16[192,1024]{1,0:T(8,128)(2,1)S(1)} %collective-permute-done.1), channel_id=1, source_target_pairs={{0,2},{2,4},{4,6},{6,7},{7,5},{5,3},{3,1},{1,0},{8,10},{10,12},{12... | collective-permute-start | bytes 1179656 | tf_op jit(solution)/shard_map/ppermute | solution.py:435
  32.4 17.0 %collective-permute-start.6 = (bf16[192,1024]{1,0:T(8,128)(2,1)S(1)}, bf16[192,1024]{1,0:T(8,128)(2,1)S(1)}, u32[]{:S(2)}, u32[]{:S(2)}) collective-permute-start(bf16[192,1024]{1,0:T(8,128)(2,1)S(1)} %collective-permute-done.5), channel_id=1, source_target_pairs={{0,1},{2,0},{4,2},{6,4},{7,6},{5,7},{3,5},{1,3},{8,9},{10,8},{12,1... | collective-permute-start | bytes 1179656 | tf_op jit(solution)/shard_map/ppermute | solution.py:435
  38.0 11.4 %collective-permute-start.26 = (bf16[448,256]{1,0:T(8,128)(2,1)}, bf16[448,256]{1,0:T(8,128)(2,1)S(1)}, u32[]{:S(2)}, u32[]{:S(2)}) collective-permute-start(bf16[448,256]{1,0:T(8,128)(2,1)} %get-tuple-element.280), channel_id=1, source_target_pairs={{0,24},{8,16},{16,8},{24,0},{1,25},{9,17},{17,9},{25,1},{2,26},{10... | collective-permute-start | bytes 688136 | tf_op jit(solution)/shard_map/ppermute | solution.py:438
  52.0 155.3 %all-gather.11.cloned.1.call-start = ((), (), s32[]{:S(2)}) async-start(), calls=%async_computation.6 | async-start | bytes 5308416 | tf_op jit(solution)/shard_map/all_gather | solution.py:572
  54.4 12.4 %collective-permute-start.3 = (bf16[192,1024]{1,0:T(8,128)(2,1)S(1)}, bf16[192,1024]{1,0:T(8,128)(2,1)S(1)}, u32[]{:S(2)}, u32[]{:S(2)}) collective-permute-start(bf16[192,1024]{1,0:T(8,128)(2,1)S(1)} %collective-permute-done.2), channel_id=1, source_target_pairs={{0,2},{2,4},{4,6},{6,7},{7,5},{5,3},{3,1},{1,0},{8,10},{10,12},{12... | collective-permute-start | bytes 1179656 | tf_op jit(solution)/shard_map/ppermute | solution.py:435
  56.0 12.3 %collective-permute-start.7 = (bf16[192,1024]{1,0:T(8,128)(2,1)S(1)}, bf16[192,1024]{1,0:T(8,128)(2,1)S(1)}, u32[]{:S(2)}, u32[]{:S(2)}) collective-permute-start(bf16[192,1024]{1,0:T(8,128)(2,1)S(1)} %collective-permute-done.6), channel_id=1, source_target_pairs={{0,1},{2,0},{4,2},{6,4},{7,6},{5,7},{3,5},{1,3},{8,9},{10,8},{12,1... | collective-permute-start | bytes 1179656 | tf_op jit(solution)/shard_map/ppermute | solution.py:435
  70.1 10.8 %collective-permute-start.12 = (bf16[192,1024]{1,0:T(8,128)(2,1)S(1)}, bf16[192,1024]{1,0:T(8,128)(2,1)}, u32[]{:S(2)}, u32[]{:S(2)}) collective-permute-start(bf16[192,1024]{1,0:T(8,128)(2,1)S(1)} %collective-permute-done.7), channel_id=1, source_target_pairs={{0,1},{2,0},{4,2},{6,4},{7,6},{5,7},{3,5},{1,3},{8,9},{10,8},{12,1... | collective-permute-start | bytes 1179656 | tf_op jit(solution)/shard_map/ppermute | solution.py:435
  81.8 172.6 %all-gather.9.cloned.1.call-start = ((), (), s32[]{:S(2)}) async-start(), calls=%async_computation.5 | async-start | bytes 1769472 | tf_op jit(solution)/shard_map/all_gather | solution.py:572
  87.7 11.4 %collective-permute-start.13 = (bf16[192,1024]{1,0:T(8,128)(2,1)}, bf16[192,1024]{1,0:T(8,128)(2,1)S(1)}, u32[]{:S(2)}, u32[]{:S(2)}) collective-permute-start(bf16[192,1024]{1,0:T(8,128)(2,1)} %collective-permute-done.11), channel_id=1, source_target_pairs={{0,2},{2,4},{4,6},{6,7},{7,5},{5,3},{3,1},{1,0},{8,10},{10,12},{12... | collective-permute-start | bytes 1179656 | tf_op jit(solution)/shard_map/ppermute | solution.py:435
  89.2 12.1 %collective-permute-start.14 = (bf16[192,1024]{1,0:T(8,128)(2,1)}, bf16[192,1024]{1,0:T(8,128)(2,1)S(1)}, u32[]{:S(2)}, u32[]{:S(2)}) collective-permute-start(bf16[192,1024]{1,0:T(8,128)(2,1)} %collective-permute-done.12), channel_id=1, source_target_pairs={{0,1},{2,0},{4,2},{6,4},{7,6},{5,7},{3,5},{1,3},{8,9},{10,8},{12,1... | collective-permute-start | bytes 1179656 | tf_op jit(solution)/shard_map/ppermute | solution.py:435
  91.4 85.8 %collective-permute-start.29 = (bf16[1,384,1024]{2,1,0:T(8,128)(2,1)}, bf16[1,384,1024]{2,1,0:T(8,128)(2,1)}, u32[]{:S(2)}, u32[]{:S(2)}) collective-permute-start(bf16[1,384,1024]{2,1,0:T(8,128)(2,1)} %bitcast.14), channel_id=1, source_target_pairs={{0,16},{8,24},{16,0},{24,8},{1,17},{9,25},{17,1},{25,9},{2,18},{10... | collective-permute-start | bytes 2359304 | tf_op jit(solution)/shard_map/ppermute | solution.py:438
  92.2 285.7 %reduce-scatter.3.cloned.1.call-start = ((), (), s32[]{:S(2)}) async-start(), calls=%async_computation.2 | async-start | bytes 5308416 | tf_op jit(solution)/shard_map/reduce_scatter | solution.py:617
  101.5 15.3 %collective-permute-start.15 = (bf16[192,1024]{1,0:T(8,128)(2,1)S(1)}, bf16[192,1024]{1,0:T(8,128)(2,1)S(1)}, u32[]{:S(2)}, u32[]{:S(2)}) collective-permute-start(bf16[192,1024]{1,0:T(8,128)(2,1)S(1)} %collective-permute-done.13), channel_id=1, source_target_pairs={{0,2},{2,4},{4,6},{6,7},{7,5},{5,3},{3,1},{1,0},{8,10},{10,12},{12... | collective-permute-start | bytes 1179656 | tf_op jit(solution)/shard_map/ppermute | solution.py:435
  103.0 22.9 %collective-permute-start.16 = (bf16[192,1024]{1,0:T(8,128)(2,1)S(1)}, bf16[192,1024]{1,0:T(8,128)(2,1)S(1)}, u32[]{:S(2)}, u32[]{:S(2)}) collective-permute-start(bf16[192,1024]{1,0:T(8,128)(2,1)S(1)} %collective-permute-done.14), channel_id=1, source_target_pairs={{0,1},{2,0},{4,2},{6,4},{7,6},{5,7},{3,5},{1,3},{8,9},{10,8},{12,1... | collective-permute-start | bytes 1179656 | tf_op jit(solution)/shard_map/ppermute | solution.py:435
  169.6 22.3 %collective-permute-start.18 = (bf16[384,128]{1,0:T(8,128)(2,1)}, bf16[384,128]{1,0:T(8,128)(2,1)}, u32[]{:S(2)}, u32[]{:S(2)}) collective-permute-start(bf16[384,128]{1,0:T(8,128)(2,1)} %get-tuple-element.302), channel_id=1, source_target_pairs={{0,3},{2,1},{4,0},{6,2},{7,4},{5,6},{3,7},{1,5},{8,11},{10,9},{12,... | collective-permute-start | bytes 294920 | tf_op jit(solution)/shard_map/ppermute | solution.py:435
  170.3 23.1 %collective-permute-start.19 = (bf16[384,128]{1,0:T(8,128)(2,1)}, bf16[384,128]{1,0:T(8,128)(2,1)}, u32[]{:S(2)}, u32[]{:S(2)}) collective-permute-start(bf16[384,128]{1,0:T(8,128)(2,1)} %get-tuple-element.301), channel_id=1, source_target_pairs={{0,5},{2,3},{4,1},{6,0},{7,2},{5,4},{3,6},{1,7},{8,13},{10,11},{12... | collective-permute-start | bytes 294920 | tf_op jit(solution)/shard_map/ppermute | solution.py:435
  171.5 23.4 %collective-permute-start.20 = (bf16[384,128]{1,0:T(8,128)(2,1)}, bf16[384,128]{1,0:T(8,128)(2,1)}, u32[]{:S(2)}, u32[]{:S(2)}) collective-permute-start(bf16[384,128]{1,0:T(8,128)(2,1)} %get-tuple-element.300), channel_id=1, source_target_pairs={{0,7},{2,5},{4,3},{6,1},{7,0},{5,2},{3,4},{1,6},{8,15},{10,13},{12... | collective-permute-start | bytes 294920 | tf_op jit(solution)/shard_map/ppermute | solution.py:435
  178.7 20.3 %collective-permute-start.27 = (bf16[8,64,1024]{2,1,0:T(8,128)(2,1)}, bf16[8,64,1024]{2,1,0:T(8,128)(2,1)S(1)}, u32[]{:S(2)}, u32[]{:S(2)}) collective-permute-start(bf16[8,64,1024]{2,1,0:T(8,128)(2,1)} %bitcast.113), channel_id=1, source_target_pairs={{0,8},{8,0},{16,24},{24,16},{1,9},{9,1},{17,25},{25,17},{2,10},{10... | collective-permute-start | bytes 3145736 | tf_op jit(solution)/shard_map/ppermute | solution.py:438
  179.0 17.5 %collective-permute-start.21 = (bf16[384,128]{1,0:T(8,128)(2,1)S(1)}, bf16[384,128]{1,0:T(8,128)(2,1)S(1)}, u32[]{:S(2)}, u32[]{:S(2)}) collective-permute-start(bf16[384,128]{1,0:T(8,128)(2,1)S(1)} %get-tuple-element.299), channel_id=1, source_target_pairs={{0,6},{2,7},{4,5},{6,3},{7,1},{5,0},{3,2},{1,4},{8,14},{10,15},{12... | collective-permute-start | bytes 294920 | tf_op jit(solution)/shard_map/ppermute | solution.py:435
  204.3 20.3 %collective-permute-start.31 = (bf16[1,384,1024]{2,1,0:T(8,128)(2,1)}, bf16[1,384,1024]{2,1,0:T(8,128)(2,1)}, u32[]{:S(2)}, u32[]{:S(2)}) collective-permute-start(bf16[1,384,1024]{2,1,0:T(8,128)(2,1)} %bitcast.17), channel_id=1, source_target_pairs={{0,16},{8,24},{16,0},{24,8},{1,17},{9,25},{17,1},{25,9},{2,18},{10... | collective-permute-start | bytes 2359304 | tf_op jit(solution)/shard_map/ppermute | solution.py:438
  204.3 20.3 %collective-permute-start.33 = (bf16[384,1024]{1,0:T(8,128)(2,1)S(1)}, bf16[384,1024]{1,0:T(8,128)(2,1)}, u32[]{:S(2)}, u32[]{:S(2)}) collective-permute-start(bf16[384,1024]{1,0:T(8,128)(2,1)S(1)} %get-tuple-element.275.refs_2_.refs_6_), channel_id=1, source_target_pairs={{0,8},{8,0},{16,24},{24,16},{1,9},{9,1},{17,25},{25,17},{2,10},{10... | collective-permute-start | bytes 2359304 | tf_op jit(solution)/shard_map/ppermute | solution.py:438
  254.3 208.6 %reduce-scatter.5.cloned.1.call-start = ((), (), s32[]{:S(2)}) async-start(), calls=%async_computation.3 | async-start | bytes 1769472 | tf_op jit(solution)/shard_map/reduce_scatter | solution.py:617
  273.1 20.1 %collective-permute-start.36 = (bf16[1,384,1024]{2,1,0:T(8,128)(2,1)}, bf16[1,384,1024]{2,1,0:T(8,128)(2,1)S(1)}, u32[]{:S(2)}, u32[]{:S(2)}) collective-permute-start(bf16[1,384,1024]{2,1,0:T(8,128)(2,1)} %add_convert_fusion.1), channel_id=1, source_target_pairs={{0,16},{8,24},{16,0},{24,8},{1,17},{9,25},{17,1},{25,9},{2,18},{10... | collective-permute-start | bytes 2359304 | tf_op jit(solution)/shard_map/ppermute | solution.py:438
  274.5 18.7 %collective-permute-start.34 = (bf16[1,384,1024]{2,1,0:T(8,128)(2,1)}, bf16[1,384,1024]{2,1,0:T(8,128)(2,1)}, u32[]{:S(2)}, u32[]{:S(2)}) collective-permute-start(bf16[1,384,1024]{2,1,0:T(8,128)(2,1)} %slice.309), channel_id=1, source_target_pairs={{0,8},{8,0},{16,24},{24,16},{1,9},{9,1},{17,25},{25,17},{2,10},{10... | collective-permute-start | bytes 2359304 | tf_op jit(solution)/shard_map/ppermute | solution.py:438
  300.7 14.6 %collective-permute-start.38 = (bf16[384,128]{1,0:T(8,128)(2,1)S(1)}, bf16[384,128]{1,0:T(8,128)(2,1)S(1)}, u32[]{:S(2)}, u32[]{:S(2)}) collective-permute-start(bf16[384,128]{1,0:T(8,128)(2,1)S(1)} %get-tuple-element.294), channel_id=1, source_target_pairs={{0,4},{2,6},{4,7},{6,5},{7,3},{5,1},{3,0},{1,2},{8,12},{10,14},{12... | collective-permute-start | bytes 294920 | tf_op jit(solution)/shard_map/ppermute | solution.py:435
  302.6 17.0 %collective-permute-start.39 = (bf16[384,128]{1,0:T(8,128)(2,1)S(1)}, bf16[384,128]{1,0:T(8,128)(2,1)S(1)}, u32[]{:S(2)}, u32[]{:S(2)}) collective-permute-start(bf16[384,128]{1,0:T(8,128)(2,1)S(1)} %get-tuple-element.293), channel_id=1, source_target_pairs={{0,6},{2,7},{4,5},{6,3},{7,1},{5,0},{3,2},{1,4},{8,14},{10,15},{12... | collective-permute-start | bytes 294920 | tf_op jit(solution)/shard_map/ppermute | solution.py:435
  305.5 14.1 %collective-permute-start.40 = (bf16[384,128]{1,0:T(8,128)(2,1)S(1)}, bf16[384,128]{1,0:T(8,128)(2,1)S(1)}, u32[]{:S(2)}, u32[]{:S(2)}) collective-permute-start(bf16[384,128]{1,0:T(8,128)(2,1)S(1)} %get-tuple-element.292), channel_id=1, source_target_pairs={{0,7},{2,5},{4,3},{6,1},{7,0},{5,2},{3,4},{1,6},{8,15},{10,13},{12... | collective-permute-start | bytes 294920 | tf_op jit(solution)/shard_map/ppermute | solution.py:435
  307.1 12.6 %collective-permute-start.41 = (bf16[384,128]{1,0:T(8,128)(2,1)S(1)}, bf16[384,128]{1,0:T(8,128)(2,1)S(1)}, u32[]{:S(2)}, u32[]{:S(2)}) collective-permute-start(bf16[384,128]{1,0:T(8,128)(2,1)S(1)} %get-tuple-element.291), channel_id=1, source_target_pairs={{0,5},{2,3},{4,1},{6,0},{7,2},{5,4},{3,6},{1,7},{8,13},{10,11},{12... | collective-permute-start | bytes 294920 | tf_op jit(solution)/shard_map/ppermute | solution.py:435
  308.9 11.9 %collective-permute-start.42 = (bf16[384,128]{1,0:T(8,128)(2,1)S(1)}, bf16[384,128]{1,0:T(8,128)(2,1)S(1)}, u32[]{:S(2)}, u32[]{:S(2)}) collective-permute-start(bf16[384,128]{1,0:T(8,128)(2,1)S(1)} %get-tuple-element.290), channel_id=1, source_target_pairs={{0,3},{2,1},{4,0},{6,2},{7,4},{5,6},{3,7},{1,5},{8,11},{10,9},{12,... | collective-permute-start | bytes 294920 | tf_op jit(solution)/shard_map/ppermute | solution.py:435
  360.8 12.9 %collective-permute-start.44 = (bf16[192,1024]{1,0:T(8,128)(2,1)S(1)}, bf16[192,1024]{1,0:T(8,128)(2,1)S(1)}, u32[]{:S(2)}, u32[]{:S(2)}) collective-permute-start(bf16[192,1024]{1,0:T(8,128)(2,1)S(1)} %get-tuple-element.288), channel_id=1, source_target_pairs={{0,1},{2,0},{4,2},{6,4},{7,6},{5,7},{3,5},{1,3},{8,9},{10,8},{12,1... | collective-permute-start | bytes 1179656 | tf_op jit(solution)/shard_map/ppermute | solution.py:435
  374.8 23.5 %collective-permute-start.48 = (bf16[1424,512]{1,0:T(8,128)(2,1)}, bf16[1424,512]{1,0:T(8,128)(2,1)}, u32[]{:S(2)}, u32[]{:S(2)}) collective-permute-start(bf16[1424,512]{1,0:T(8,128)(2,1)} %get-tuple-element.153), channel_id=1, source_target_pairs={{0,8},{8,0},{16,24},{24,16},{1,9},{9,1},{17,25},{25,17},{2,10},{10... | collective-permute-start | bytes 4374536 | tf_op jit(solution)/shard_map/ppermute | solution.py:438
  377.9 18.4 %collective-permute-start.46 = (bf16[192,1024]{1,0:T(8,128)(2,1)}, bf16[192,1024]{1,0:T(8,128)(2,1)}, u32[]{:S(2)}, u32[]{:S(2)}) collective-permute-start(bf16[192,1024]{1,0:T(8,128)(2,1)} %get-tuple-element.151), channel_id=1, source_target_pairs={{0,1},{2,0},{4,2},{6,4},{7,6},{5,7},{3,5},{1,3},{8,9},{10,8},{12,1... | collective-permute-start | bytes 1179656 | tf_op jit(solution)/shard_map/ppermute | solution.py:435
  379.9 16.6 %collective-permute-start.47 = (bf16[192,1024]{1,0:T(8,128)(2,1)}, bf16[192,1024]{1,0:T(8,128)(2,1)}, u32[]{:S(2)}, u32[]{:S(2)}) collective-permute-start(bf16[192,1024]{1,0:T(8,128)(2,1)} %get-tuple-element.152), channel_id=1, source_target_pairs={{0,2},{2,4},{4,6},{6,7},{7,5},{5,3},{3,1},{1,0},{8,10},{10,12},{12... | collective-permute-start | bytes 1179656 | tf_op jit(solution)/shard_map/ppermute | solution.py:435
  382.0 16.4 %collective-permute-start.50 = (bf16[1,384,1024]{2,1,0:T(8,128)(2,1)}, bf16[1,384,1024]{2,1,0:T(8,128)(2,1)}, u32[]{:S(2)}, u32[]{:S(2)}) collective-permute-start(bf16[1,384,1024]{2,1,0:T(8,128)(2,1)} %slice.321), channel_id=1, source_target_pairs={{0,8},{8,0},{16,24},{24,16},{1,9},{9,1},{17,25},{25,17},{2,10},{10... | collective-permute-start | bytes 2359304 | tf_op jit(solution)/shard_map/ppermute | solution.py:438
  383.2 17.6 %collective-permute-start.49 = (bf16[1,384,1024]{2,1,0:T(8,128)(2,1)}, bf16[1,384,1024]{2,1,0:T(8,128)(2,1)}, u32[]{:S(2)}, u32[]{:S(2)}) collective-permute-start(bf16[1,384,1024]{2,1,0:T(8,128)(2,1)} %slice.319), channel_id=1, source_target_pairs={{0,8},{8,0},{16,24},{24,16},{1,9},{9,1},{17,25},{25,17},{2,10},{10... | collective-permute-start | bytes 2359304 | tf_op jit(solution)/shard_map/ppermute | solution.py:438
  403.6 13.6 %collective-permute-start.51 = (bf16[192,1024]{1,0:T(8,128)(2,1)S(1)}, bf16[192,1024]{1,0:T(8,128)(2,1)S(1)}, u32[]{:S(2)}, u32[]{:S(2)}) collective-permute-start(bf16[192,1024]{1,0:T(8,128)(2,1)S(1)} %get-tuple-element.160), channel_id=1, source_target_pairs={{0,1},{2,0},{4,2},{6,4},{7,6},{5,7},{3,5},{1,3},{8,9},{10,8},{12,1... | collective-permute-start | bytes 1179656 | tf_op jit(solution)/shard_map/ppermute | solution.py:435
  405.9 13.0 %collective-permute-start.53 = (bf16[192,1024]{1,0:T(8,128)(2,1)S(1)}, bf16[192,1024]{1,0:T(8,128)(2,1)S(1)}, u32[]{:S(2)}, u32[]{:S(2)}) collective-permute-start(bf16[192,1024]{1,0:T(8,128)(2,1)S(1)} %get-tuple-element.163), channel_id=1, source_target_pairs={{0,2},{2,4},{4,6},{6,7},{7,5},{5,3},{3,1},{1,0},{8,10},{10,12},{12... | collective-permute-start | bytes 1179656 | tf_op jit(solution)/shard_map/ppermute | solution.py:435
  408.1 22.2 %collective-permute-start.55 = (bf16[1424,256]{1,0:T(8,128)(2,1)S(1)}, bf16[1424,256]{1,0:T(8,128)(2,1)S(1)}, u32[]{:S(2)}, u32[]{:S(2)}) collective-permute-start(bf16[1424,256]{1,0:T(8,128)(2,1)S(1)} %slice.529), channel_id=1, source_target_pairs={{0,16},{8,24},{16,0},{24,8},{1,17},{9,25},{17,1},{25,9},{2,18},{10... | collective-permute-start | bytes 2187272 | tf_op jit(solution)/shard_map/ppermute | solution.py:438
  424.0 28.6 %collective-permute-start.62 = (bf16[1,384,1024]{2,1,0:T(8,128)(2,1)}, bf16[1,384,1024]{2,1,0:T(8,128)(2,1)}, u32[]{:S(2)}, u32[]{:S(2)}) collective-permute-start(bf16[1,384,1024]{2,1,0:T(8,128)(2,1)} %convert_add_fusion.2), channel_id=1, source_target_pairs={{0,16},{8,24},{16,0},{24,8},{1,17},{9,25},{17,1},{25,9},{2,18},{10... | collective-permute-start | bytes 2359304 | tf_op jit(solution)/shard_map/ppermute | solution.py:438
  430.7 15.7 %collective-permute-start.56 = (bf16[192,1024]{1,0:T(8,128)(2,1)}, bf16[192,1024]{1,0:T(8,128)(2,1)}, u32[]{:S(2)}, u32[]{:S(2)}) collective-permute-start(bf16[192,1024]{1,0:T(8,128)(2,1)} %get-tuple-element.166), channel_id=1, source_target_pairs={{0,1},{2,0},{4,2},{6,4},{7,6},{5,7},{3,5},{1,3},{8,9},{10,8},{12,1... | collective-permute-start | bytes 1179656 | tf_op jit(solution)/shard_map/ppermute | solution.py:435
  431.9 13.5 %collective-permute-start.58 = (bf16[4,144,256]{2,1,0:T(8,128)(2,1)}, bf16[4,144,256]{2,1,0:T(8,128)(2,1)}, u32[]{:S(2)}, u32[]{:S(2)}) collective-permute-start(bf16[4,144,256]{2,1,0:T(8,128)(2,1)} %fusion.47), channel_id=1, source_target_pairs={{0,1},{1,0},{2,3},{3,2},{4,5},{5,4},{6,7},{7,6},{8,9},{9,8},{10,11... | collective-permute-start | bytes 884744 | tf_op jit(solution)/shard_map/ppermute | solution.py:441
  432.3 15.2 %collective-permute-start.57 = (bf16[192,1024]{1,0:T(8,128)(2,1)}, bf16[192,1024]{1,0:T(8,128)(2,1)}, u32[]{:S(2)}, u32[]{:S(2)}) collective-permute-start(bf16[192,1024]{1,0:T(8,128)(2,1)} %get-tuple-element.168), channel_id=1, source_target_pairs={{0,2},{2,4},{4,6},{6,7},{7,5},{5,3},{3,1},{1,0},{8,10},{10,12},{12... | collective-permute-start | bytes 1179656 | tf_op jit(solution)/shard_map/ppermute | solution.py:435
  448.9 11.4 %collective-permute-start.59 = (bf16[192,1024]{1,0:T(8,128)(2,1)S(1)}, bf16[192,1024]{1,0:T(8,128)(2,1)S(1)}, u32[]{:S(2)}, u32[]{:S(2)}) collective-permute-start(bf16[192,1024]{1,0:T(8,128)(2,1)S(1)} %get-tuple-element.170), channel_id=1, source_target_pairs={{0,1},{2,0},{4,2},{6,4},{7,6},{5,7},{3,5},{1,3},{8,9},{10,8},{12,1... | collective-permute-start | bytes 1179656 | tf_op jit(solution)/shard_map/ppermute | solution.py:435
  462.9 24.8 %collective-permute-start.63 = (bf16[192,1024]{1,0:T(8,128)(2,1)}, bf16[192,1024]{1,0:T(8,128)(2,1)}, u32[]{:S(2)}, u32[]{:S(2)}) collective-permute-start(bf16[192,1024]{1,0:T(8,128)(2,1)} %get-tuple-element.184), channel_id=1, source_target_pairs={{0,1},{2,0},{4,2},{6,4},{7,6},{5,7},{3,5},{1,3},{8,9},{10,8},{12,1... | collective-permute-start | bytes 1179656 | tf_op jit(solution)/shard_map/ppermute | solution.py:435
  466.6 21.0 %collective-permute-start.64 = (bf16[192,1024]{1,0:T(8,128)(2,1)}, bf16[192,1024]{1,0:T(8,128)(2,1)}, u32[]{:S(2)}, u32[]{:S(2)}) collective-permute-start(bf16[192,1024]{1,0:T(8,128)(2,1)} %get-tuple-element.186), channel_id=1, source_target_pairs={{0,2},{2,4},{4,6},{6,7},{7,5},{5,3},{3,1},{1,0},{8,10},{10,12},{12... | collective-permute-start | bytes 1179656 | tf_op jit(solution)/shard_map/ppermute | solution.py:435
  (97 other events, 986.0 us)
Sparse Core Ops, SparseCore 0:
  52.1 43.8 all-gather.6
  98.2 95.4 all-gather.10
  195.9 44.6 all-gather.8
  254.4 103.5 reduce-scatter.2
  375.0 69.3 reduce-scatter.4
